TPU v7x, 128 devices: a whole 4x4x4 slice. The times are simulated.
128 devices in a mesh: ctx: 32 (over x, z, y_hi), tp: 4 (over y_lo, core).
Axes of the slice: x: 4, y: 4 (y_hi: 2, y_lo: 2; y = y_hi * 2 + y_lo), z: 4, core: 2. Of those that a mesh axis runs over, the one named last changes fastest.
Arguments:
- queries: bfloat16 [24576, 2048], P('ctx', 'tp'), may hold values from -24 to 24
- keyvals: bfloat16 [24576, 2, 2048], P('ctx', None, 'tp'), may hold values from -6 to 6
- residual: bfloat16 [24576, 4096], P('ctx', 'tp'), may hold values from -6 to 6
- out_weight: bfloat16 [2048, 4096], P('tp'), may hold values from -0.125 to 0.125
- norm_gain: bfloat16 [4096], P('tp'), may hold values from 0.5 to 1.5
- norm_bias: bfloat16 [4096], P('tp'), may hold values from -3 to 3
- cross_weight: bfloat16 [4096, 2, 2048], P(None, None, 'tp'), may hold values from -0.09375 to 0.09375
- window_reach: int32 [16], P('tp'), may hold values from 1 to 3, as said below
- global_blocks: int32 [2], replicated, may hold values from 0 to 383, as said below
- random_blocks: int32 [384, 3], replicated, may hold values from 0 to 383, as said below
Outputs:
- encoded: bfloat16 [24576, 4096], P('ctx', 'tp')
- cross_kv: bfloat16 [24576, 2, 2048], P('ctx', None, 'tp')
Inputs may be any that keep to these rules, and one draw needn't show every extreme that they name: `window_reach`: some head has reach 3 and some head reach 1. `global_blocks`: 2 distinct block numbers; one of them is the document's last block. `random_blocks`: for the query blocks s*12 to (s+1)*12 - 1 of any index s of ctx, at most 3 of their 36 random entries name blocks of one index of ctx (block number // 12); for every s exactly 3 do for some index.
All inputs are finite; a program needn't handle non-finite values.
Results may differ from a plain program's by a relative error of at most 0.0056.
Values may be sent and summed in bfloat16 or wider, within the bound.
A program may use at most 192 MiB of HBM per device.

v0:
```python
import math

import jax
import jax.numpy as jnp
from jax import lax
from jax.sharding import PartitionSpec as P

D = 4096
BLOCK = 64
MAXR = 3
G = 2
R = 3


norm_eps = 1e-05


def extended(cells, sides, width):
    for axis, dim in sides:
        count = lax.axis_size(axis)
        ends = count - 1
        head = lax.slice_in_dim(cells, 0, width, axis=dim)
        tail = lax.slice_in_dim(cells, cells.shape[dim] - width, cells.shape[dim], axis=dim)
        cells = jnp.concatenate(
            [
                lax.ppermute(tail, axis, [(i, (i + 1) % count) for i in range(ends)]),
                cells,
                lax.ppermute(head, axis, [((i + 1) % count, i) for i in range(ends)]),
            ],
            axis=dim,
        )
    return cells


def combined_all(x, axis, combine):
    everything = jax.tree.map(lambda part: lax.all_gather(part, axis), x)
    first = jax.tree.map(lambda part: part[0], everything)

    def step(k, so_far):
        return combine(so_far, jax.tree.map(lambda part: part[k], everything))

    return lax.fori_loop(1, lax.axis_size(axis), step, first)


def passed_along(value, axis, steps):
    count = lax.axis_size(axis)
    pairs = [(source, (source + steps) % count) for source in range(count)]
    return lax.ppermute(value, axis, pairs)


def combine_partials(first, second):
    peak_first, total_first, acc_first = first
    peak_second, total_second, acc_second = second
    new_peak = jnp.maximum(peak_first, peak_second)
    factor_first = jnp.exp(peak_first - new_peak)
    factor_second = jnp.exp(peak_second - new_peak)
    merged_total = total_first * factor_first + total_second * factor_second
    merged_acc = acc_first * factor_first[..., None] + acc_second * factor_second[..., None]
    return (new_peak, merged_total, merged_acc)


def shards(
    queries,
    keyvals,
    residual,
    out_weight,
    norm_gain,
    norm_bias,
    cross_weight,
    window_reach,
    global_blocks,
    random_blocks,
):
    tok_rows, head_cols = queries.shape
    head_count = window_reach.shape[0]
    head_size = head_cols // head_count
    ctx_count = lax.axis_size("ctx")
    ctx_index = lax.axis_index("ctx")
    block_count = tok_rows // BLOCK
    all_blocks = block_count * ctx_count
    span = 2 * MAXR + 1
    score_scale = 1.0 / math.sqrt(head_size)
    query_blocks = queries.reshape(block_count, BLOCK, head_cols)
    pair_blocks = keyvals.reshape(block_count, BLOCK, 2, head_cols)
    padded = extended(keyvals, (("ctx", 0),), MAXR * BLOCK)
    padded_blocks = padded.reshape(block_count + 2 * MAXR, BLOCK, 2, head_cols)
    window_pairs = jnp.stack(
        [padded_blocks[shift_at : shift_at + block_count] for shift_at in range(span)], axis=1
    )
    own_ids = ctx_index * block_count + jnp.arange(block_count, dtype=jnp.int32)
    selector = global_blocks[:, None] == own_ids[None, :]
    select_low = selector.astype(jnp.bfloat16)
    local_queries = jnp.einsum(
        "gb,bkc->gkc", select_low, query_blocks, preferred_element_type=jnp.float32
    )
    local_pairs = jnp.einsum(
        "gb,bkmc->gkmc", select_low, pair_blocks, preferred_element_type=jnp.float32
    )
    global_q, global_kv = lax.psum((local_queries, local_pairs), "ctx")
    global_q = global_q.astype(jnp.bfloat16)
    global_kv = global_kv.astype(jnp.bfloat16)
    req_count = block_count * R
    capacity = 1 + (req_count + ctx_count - 2) // ctx_count
    requests = random_blocks.reshape(ctx_count, req_count)
    owners = requests // block_count
    local_ids = requests % block_count
    positions = jnp.arange(req_count, dtype=jnp.int32)
    earlier = positions[None, :] < positions[:, None]
    ranks = jnp.sum(
        ((owners[:, :, None] == owners[:, None, :]) & earlier[None, :, :]).astype(jnp.int32), axis=2
    )
    slot_ids = jnp.arange(capacity, dtype=jnp.int32)
    matches = (owners[:, None, :] == ctx_index) & (ranks[:, None, :] == slot_ids[None, :, None])
    source_ids = jnp.sum(jnp.where(matches, local_ids[:, None, :], 0), axis=2).reshape(-1)
    occupied = jnp.any(matches, axis=2).reshape(-1)
    outgoing = jnp.take(pair_blocks, source_ids, axis=0)
    outgoing = jnp.where(occupied[:, None, None, None], outgoing, jnp.zeros_like(outgoing))
    incoming = lax.all_to_all(outgoing, "ctx", split_axis=0, concat_axis=0, tiled=True)
    my_owners = lax.dynamic_index_in_dim(owners, ctx_index, 0, keepdims=False)
    my_ranks = lax.dynamic_index_in_dim(ranks, ctx_index, 0, keepdims=False)
    random_pairs = jnp.take(incoming, my_owners * capacity + my_ranks, axis=0).reshape(
        block_count, R, BLOCK, 2, head_cols
    )
    global_pairs = jnp.broadcast_to(global_kv[None], (block_count, G, BLOCK, 2, head_cols))
    listed = jnp.concatenate([window_pairs, global_pairs, random_pairs], axis=1)
    list_len = span + G + R
    listed_keys = listed[:, :, :, 0].reshape(block_count, list_len, BLOCK, head_count, head_size)
    listed_values = listed[:, :, :, 1].reshape(block_count, list_len, BLOCK, head_count, head_size)
    query_heads = query_blocks.reshape(block_count, BLOCK, head_count, head_size)
    logit_scores = (
        jnp.einsum(
            "bqhd,bjkhd->bhqjk", query_heads, listed_keys, preferred_element_type=jnp.float32
        )
        * score_scale
    )
    offsets = jnp.arange(span, dtype=jnp.int32) - MAXR
    window_ids = own_ids[:, None] + offsets[None, :]
    inside = (window_ids >= 0) & (window_ids < all_blocks)
    near = jnp.abs(offsets)[None, :] <= window_reach[:, None]
    window_ok = inside[:, None, :] & near[None, :, :]
    usable = jnp.concatenate(
        [window_ok, jnp.ones((block_count, head_count, G + R), dtype=bool)], axis=2
    )
    logit_scores = jnp.where(usable[:, :, None, :, None], logit_scores, -jnp.inf)
    peak = jnp.max(logit_scores, axis=(3, 4), keepdims=True)
    weights = jnp.exp(logit_scores - peak)
    softmax_totals = jnp.sum(weights, axis=(3, 4))
    rounded_output = weights.astype(jnp.bfloat16)
    sparse_output = jnp.einsum(
        "bhqjk,bjkhd->bqhd", rounded_output, listed_values, preferred_element_type=jnp.float32
    )
    sparse_output = sparse_output / jnp.transpose(softmax_totals, (0, 2, 1))[..., None]
    global_heads = global_q.reshape(G * BLOCK, head_count, head_size)
    key_heads = keyvals[:, 0].reshape(tok_rows, head_count, head_size)
    value_heads = keyvals[:, 1].reshape(tok_rows, head_count, head_size)
    far_scores = (
        jnp.einsum("qhd,khd->hqk", global_heads, key_heads, preferred_element_type=jnp.float32)
        * score_scale
    )
    far_peak = jnp.max(far_scores, axis=2)
    far_weights = jnp.exp(far_scores - far_peak[..., None])
    far_total = jnp.sum(far_weights, axis=2)
    far_acc = jnp.einsum(
        "hqk,khd->hqd",
        far_weights.astype(jnp.bfloat16),
        value_heads,
        preferred_element_type=jnp.float32,
    )
    merged_peak, merged_total, merged_acc = combined_all(
        (far_peak, far_total, far_acc), "ctx", combine_partials
    )
    global_out = jnp.transpose(merged_acc / merged_total[..., None], (1, 0, 2)).reshape(
        G, BLOCK, head_cols
    )
    owned = jnp.any(selector, axis=0)
    replacement = jnp.einsum(
        "gb,gkc->bkc", selector.astype(jnp.float32), global_out, precision=lax.Precision.HIGHEST
    )
    attended = jnp.where(
        owned[:, None, None], replacement, sparse_output.reshape(block_count, BLOCK, head_cols)
    )
    attended = attended.reshape(tok_rows, head_cols).astype(jnp.bfloat16)
    summed = lax.psum_scatter(
        lax.dot_general(
            out_weight, attended, (((0,), (1,)), ((), ())), preferred_element_type=jnp.float32
        ),
        "tp",
        scatter_dimension=0,
        tiled=True,
    )
    mixed_part = summed.T
    mixed = residual.astype(jnp.float32) + mixed_part
    row_sum = jnp.sum(mixed, axis=1)
    row_square = jnp.sum(mixed * mixed, axis=1)
    total_sum, total_square = lax.psum((row_sum, row_square), "tp")
    row_mean = total_sum / D
    variance = total_square / D - row_mean * row_mean
    normalized = (mixed - row_mean[:, None]) * lax.rsqrt(variance[:, None] + norm_eps)
    encoded = (normalized * norm_gain.astype(jnp.float32) + norm_bias.astype(jnp.float32)).astype(
        jnp.bfloat16
    )
    flat_weight = cross_weight.reshape(D, 2 * head_cols)
    half_way = ctx_count // 2
    arrived = passed_along(encoded, "ctx", half_way)
    cross_kv = jnp.dot(
        lax.all_gather(arrived, "tp", axis=1, tiled=True),
        flat_weight,
        preferred_element_type=jnp.float32,
    ).astype(jnp.bfloat16)
    return (encoded, cross_kv.reshape(tok_rows, 2, head_cols))


def solution(mesh):
    placed = (
        P("ctx", "tp"),
        P("ctx", None, "tp"),
        P("ctx", "tp"),
        P("tp", None),
        P("tp"),
        P("tp"),
        P(None, None, "tp"),
        P("tp"),
        P(),
        P(),
    )
    return jax.shard_map(
        shards,
        mesh=mesh,
        in_specs=placed,
        out_specs=(P("ctx", "tp"), P("ctx", None, "tp")),
        check_vma=False,
    )
```

profile of v0, /device:TPU:1, one launch (start us, length us, event | category | flops | bytes accessed | tf_op | source)
XLA Modules:
  0.0 1075.0 jit_solution(555551298517837543)
XLA Ops:
  11.4 28.4 %gather_fusion = bf16[96,64,2,512]{3,2,1,0:T(2,128)(2,1)} fusion(bf16[12,64,2,512]{3,2,1,0:T(2,128)(2,1)} %bitcast.109, s32[1024]{0:T(1024)S(1)} %pad_clamp_fusion.1), kind=kCustom, calls=%fused_computation | custom fusion | bytes 25166208 | tf_op jit(solution)/shard_map/jit(_take)/gather | solution.py:116
  39.8 16.2 %broadcast_select_fusion.1 = bf16[96,64,2,512]{3,2,1,0:T(2,128)(2,1)} fusion(pred[96]{0:T(512)(128)(4,1)S(1)} %broadcast_in_dim.75, bf16[96,64,2,512]{3,2,1,0:T(2,128)(2,1)} %gather_fusion, pred[96]{0:T(512)(128)(4,1)S(1)} %compare_and_fusion.1), kind=kLoop, calls=%fused_computation.11 | loop fusion | flops 12582912 | bytes 25166016 | tf_op jit(solution)/shard_map/jit(_where)/select_n | solution.py:117
  56.0 11.7 %all-to-all-start = ((bf16[96,64,2,512]{3,2,1,0:T(2,128)(2,1)}), bf16[96,64,2,512]{3,2,1,0:T(2,128)(2,1)}, u32[]{:S(2)}, u32[]{:S(2)}) async-start(bf16[96,64,2,512]{3,2,1,0:T(2,128)(2,1)} %broadcast_select_fusion.1), calls=%async_computation | async-start | bytes 25165824 | tf_op jit(solution)/shard_map/all_to_all | solution.py:118
  67.9 1.8 fusion.15
  70.2 3.1 fusion.50
  73.3 4.6 copy.212
  77.9 321.8 %all-reduce.4 = (bf16[2,64,2,512]{3,0,2,1:T(2,128)(2,1)}, bf16[2,64,512]{2,0,1:T(2,128)(2,1)S(1)}) all-reduce(f32[2,64,2,512]{3,0,2,1:T(2,128)} %fusion.15, f32[2,64,512]{2,0,1:T(2,128)S(1)} %fusion.26), channel_id=1, replica_groups=mesh['ctx'=32,'tp'=4] {'ctx'}, use_global_device_ids=true, to_apply=%region_6.7 | all-reduce | flops 196608 | bytes 1179648 | tf_op jit(solution)/shard_map/psum | solution.py:99
  399.8 2.9 copy.213
  402.7 1.6 fusion.52
  404.3 2.3 fusion.28
  406.7 1.4 fusion.51
  408.1 2.0 collective-permute-start
  410.1 1.3 collective-permute-start.1
  411.4 1.3 fusion.37
  412.7 1.3 copy.197
  414.1 85.0 %all-gather.3 = f32[32,4,128]{2,1,0:T(4,128)} all-gather(f32[1,4,128]{2,1,0:T(4,128)} %bitcast.127), channel_id=2, replica_groups=mesh['ctx'=32,'tp'=4] {'ctx'}, dimensions={0}, use_global_device_ids=true | all-gather | bytes 67584 | tf_op jit(solution)/shard_map/all_gather | solution.py:36
  500.2 75.0 %all-gather.4 = f32[32,4,128]{2,1,0:T(4,128)S(1)} all-gather(f32[1,4,128]{2,1,0:T(4,128)S(1)} %bitcast.129), channel_id=3, replica_groups=mesh['ctx'=32,'tp'=4] {'ctx'}, dimensions={0}, use_global_device_ids=true | all-gather | bytes 67584 | tf_op jit(solution)/shard_map/all_gather | solution.py:36
  575.7 1.4 fusion.46
  579.2 2.4 reshape_reshape.3
  583.5 1.3 constant_dynamic-update-slice_fusion.1
  584.8 1.7 constant_dynamic-update-slice_fusion.3
  586.9 3.3 fusion.49
  590.2 1.5 copy_dynamic-update-slice_fusion.6
  591.7 1.5 copy_dynamic-update-slice_fusion.5
  593.2 1.5 copy_dynamic-update-slice_fusion.4
  594.7 1.5 copy_dynamic-update-slice_fusion.3
  596.1 3.3 fusion.48
  599.4 1.5 copy_dynamic-update-slice_fusion.2
  600.9 1.5 copy_dynamic-update-slice_fusion.1
  602.3 1.5 copy_dynamic-update-slice_fusion
  603.8 2.1 broadcast_dynamic-update-slice_fusion
  605.9 16.9 %gather_fusion.1 = bf16[36,64,2,512]{3,2,1,0:T(2,128)(2,1)} fusion(bf16[96,64,2,512]{3,2,1,0:T(2,128)(2,1)} %all-to-all-done, s32[1024]{0:T(1024)S(1)} %pad_clamp_fusion), kind=kCustom, calls=%fused_computation.1 | custom fusion | bytes 9437328 | tf_op jit(solution)/shard_map/jit(_take)/gather | solution.py:121
  622.8 3.4 copy.189
  626.2 3.9 select_dynamic-update-slice_fusion
  630.1 13.0 %fusion.47 = (bf16[12,12,64,1,512]{4,2,1,0,3:T(8,128)(2,1)}, bf16[12,12,64,1,512]{4,2,1,0,3:T(8,128)(2,1)}) fusion(bf16[12,12,64,2,512]{4,2,1,0,3:T(8,128)(2,1)} %select_dynamic-update-slice_fusion), kind=kLoop, calls=%fused_computation.108 | loop fusion | bytes 37748736 | tf_op jit(solution)/shard_map/slice | solution.py:128
  643.2 14.0 %reshape_squeeze.15 = bf16[12,12,64,4,128]{4,3,2,1,0:T(4,128)(2,1)} reshape(bf16[12,12,64,1,512]{4,2,1,0,3:T(8,128)(2,1)} %get-tuple-element.210) | data formatting | bytes 18874368 | tf_op jit(solution)/shard_map/reshape;squeeze | solution.py:127
  657.1 13.9 %reshape_squeeze.14 = bf16[12,12,64,4,128]{4,3,2,1,0:T(4,128)(2,1)} reshape(bf16[12,12,64,1,512]{4,2,1,0,3:T(8,128)(2,1)} %get-tuple-element.209) | data formatting | bytes 18874368 | tf_op jit(solution)/shard_map/reshape;squeeze | solution.py:128
  671.1 6.9 bitcast_reduce_fusion
  677.9 5.1 fusion.4
  683.0 1.4 copy-done.1
  684.4 12.8 %fusion.18 = bf16[12,4,8,8,128]{4,3,2,1,0:T(8,128)(2,1)S(1)} fusion(f32[12,4,12,64,64]{4,3,2,1,0:T(8,128)} %copy-done.1, f32[12,4,64]{2,1,0:T(4,128)S(1)} %get-tuple-element.227, pred[12,4,12]{2,1,0:T(4,128)(4,1)S(1)} %concatenate.20, bf16[12,12,64,4,128]{4,3,2,1,0:T(4,128)(2,1)} %reshape_squeeze.14, f32[12,64,4]{1,2,0:T(4,128)S(1)} %bitcast.128), kind=kOutput, calls=%fused_computation.37 | convolution fusion | flops 614203392 | bytes 19685952 | tf_op jit(solution)/shard_map/bhqjk,bjkhd->bqhd/dot_general | solution.py:149
  698.2 59.2 %while.19 = (s32[]{:T(128)}, f32[4,128]{1,0:T(4,128)S(1)}, f32[4,128]{1,0:T(4,128)S(1)}, f32[4,128,128]{2,1,0:T(8,128)S(1)}, f32[32,4,128]{2,1,0:T(4,128)}, /*in...) while((s32[]{:T(128)}, f32[4,128]{1,0:T(4,128)S(1)}, ...), condition=%wide.region_5.6_spmd, body=%wide.region_4.5_spmd.sunk | while | flops 199685 | bytes 807063 | solution.py:42
  698.9 1.2 fusion.62
  700.8 1.2 fusion.62
  702.8 1.2 fusion.62
  704.6 1.2 fusion.62
  706.6 1.2 fusion.62
  708.4 1.2 fusion.62
  710.4 1.2 fusion.62
  723.7 1.2 fusion.62
  727.5 1.2 fusion.62
  744.8 1.2 fusion.62
  750.5 1.2 fusion.62
  760.0 8.8 convolution_bitcast_fusion
  769.5 169.2 %reduce-scatter.2.cloned.1.call-done = f32[1024,768]{0,1:T(8,128)} async-done(((f32[4096,768]{0,1:T(8,128)}), f32[1024,768]{0,1:T(8,128)}) %reduce-scatter.2.cloned.1.call-update) | async-done | bytes 3145744 | tf_op jit(solution)/shard_map/reduce_scatter | solution.py:183
  938.7 3.1 fusion.25
  941.8 5.5 all-reduce.2
  947.3 2.1 add_convert_fusion
  950.6 2.7 collective-permute-start.2
  953.3 33.9 %collective-permute-done.2 = bf16[768,1024]{1,0:T(8,128)(2,1)S(1)} collective-permute-done((bf16[768,1024]{1,0:T(8,128)(2,1)S(1)}, bf16[768,1024]{1,0:T(8,128)(2,1)S(1)}, u32[]{:S(2)}, u32[]{:S(2)}) %collective-permute-start.2) | collective-permute-done | bytes 1572896 | tf_op jit(solution)/shard_map/ppermute | solution.py:48
  988.4 9.3 copy.215
  997.7 57.2 %all-gather.8.cloned.1.call-done = bf16[768,4096]{1,0:T(8,128)(2,1)} async-done(((bf16[768,1024]{1,0:T(8,128)(2,1)}), bf16[768,4096]{1,0:T(8,128)(2,1)}) %all-gather.8.cloned.1.call-update) | async-done | bytes 6291472 | tf_op jit(solution)/shard_map/all_gather | solution.py:206
  1054.9 10.9 %convolution_convert_fusion = bf16[768,1024]{1,0:T(8,128)(2,1)S(1)} fusion(bf16[768,4096]{1,0:T(8,128)(2,1)} %all-gather.8.cloned.1.call-done, bf16[4096,1024]{1,0:T(8,128)(2,1)} %bitcast.114), kind=kOutput, calls=%fused_computation.33 | convolution fusion | flops 6443237376 | bytes 16252928 | tf_op jit(solution)/shard_map/dot_general | solution.py:205
  1065.8 2.4 reshape.294
  (141 shorter events, 62.5 us)
Async XLA Ops:
  10.5 29.3 %copy-start.6 = (s32[32,36]{1,0:T(8,128)}, s32[32,36]{1,0:T(8,128)S(1)}, u32[]{:S(2)}) copy-start(s32[32,36]{1,0:T(8,128)S(1)} %copy.184) | copy-start | bytes 13828
  56.0 11.8 %copy-start = (bf16[768,2,512]{2,1,0:T(2,128)(2,1)S(1)}, bf16[768,2,512]{2,1,0:T(2,128)(2,1)}, u32[]{:S(2)}) copy-start(bf16[768,2,512]{2,1,0:T(2,128)(2,1)} %param.13) | copy-start | bytes 4718596
  56.0 11.8 %copy-start.10 = (s32[2]{0:T(128)S(1)}, s32[2]{0:T(128)}, u32[]{:S(2)}) copy-start(s32[2]{0:T(128)} %param.20) | copy-start | bytes 28
  56.0 13.7 %copy-start.3 = (bf16[768,512]{1,0:T(8,128)(2,1)S(1)}, bf16[768,512]{1,0:T(8,128)(2,1)}, u32[]{:S(2)}) copy-start(bf16[768,512]{1,0:T(8,128)(2,1)} %param.12) | copy-start | bytes 2359300
  56.0 549.9 %all-to-all-start = ((bf16[96,64,2,512]{3,2,1,0:T(2,128)(2,1)}), bf16[96,64,2,512]{3,2,1,0:T(2,128)(2,1)}, u32[]{:S(2)}, u32[]{:S(2)}) async-start(bf16[96,64,2,512]{3,2,1,0:T(2,128)(2,1)} %broadcast_select_fusion.1), calls=%async_computation | async-start | bytes 25165824 | tf_op jit(solution)/shard_map/all_to_all | solution.py:118
  67.8 629.5 %all-gather.10.cloned.1.call-start = ((), (), s32[]{:S(2)}) async-start(), calls=%async_computation.4 | async-start | bytes 8650752 | tf_op jit(solution)/shard_map/all_gather | solution.py:36
  67.8 5.4 copy-start.8
  404.3 5.9 copy-start.7
  406.6 532.1 %reduce-scatter.2.cloned.1.call-start = ((), (), s32[]{:S(2)}) async-start(), calls=%async_computation.2 | async-start | bytes 15728640 | tf_op jit(solution)/shard_map/reduce_scatter | solution.py:183
  408.1 175.4 %collective-permute-start = (bf16[192,2,512]{2,1,0:T(2,128)(2,1)}, bf16[192,2,512]{2,1,0:T(2,128)(2,1)}, u32[]{:S(2)}, u32[]{:S(2)}) collective-permute-start(bf16[192,2,512]{2,1,0:T(2,128)(2,1)} %get-tuple-element.220), channel_id=1, source_target_pairs={{0,4},{4,8},{8,12},{12,16},{16,20},{20,24},{24,28},{28,32},{32,36}... | collective-permute-start | bytes 1179656 | tf_op jit(solution)/shard_map/ppermute | solution.py:26
  410.1 176.4 %collective-permute-start.1 = (bf16[192,2,512]{2,1,0:T(2,128)(2,1)}, bf16[192,2,512]{2,1,0:T(2,128)(2,1)S(1)}, u32[]{:S(2)}, u32[]{:S(2)}) collective-permute-start(bf16[192,2,512]{2,1,0:T(2,128)(2,1)} %get-tuple-element.219), channel_id=1, source_target_pairs={{4,0},{8,4},{12,8},{16,12},{20,16},{24,20},{28,24},{32,28},{36,32}... | collective-permute-start | bytes 1179656 | tf_op jit(solution)/shard_map/ppermute | solution.py:28
  677.9 6.5 copy-start.1
  697.2 60.7 %copy-start.9 = (s32[12]{0:T(128)S(1)}, s32[12]{0:T(128)}, u32[]{:S(2)}) copy-start(s32[12]{0:T(128)} %copy-done.8) | copy-start | bytes 148
  697.2 60.7 %copy-start.11 = (s32[2]{0:T(128)S(1)}, s32[2]{0:T(128)}, u32[]{:S(2)}) copy-start(s32[2]{0:T(128)} %param.20) | copy-start | bytes 28
  768.8 0.7 copy-start.12
  768.8 0.7 copy-start.13
  768.8 286.1 %all-gather.8.cloned.1.call-start = ((), (), s32[]{:S(2)}) async-start(), calls=%async_computation.3 | async-start | bytes 7864320 | tf_op jit(solution)/shard_map/all_gather | solution.py:206
  938.7 8.6 copy-start.2
  949.4 1.1 copy-start.5
  950.6 36.6 %collective-permute-start.2 = (bf16[768,1024]{1,0:T(8,128)(2,1)S(1)}, bf16[768,1024]{1,0:T(8,128)(2,1)S(1)}, u32[]{:S(2)}, u32[]{:S(2)}) collective-permute-start(bf16[768,1024]{1,0:T(8,128)(2,1)S(1)} %add_convert_fusion), channel_id=1, source_target_pairs={{0,64},{4,68},{8,72},{12,76},{16,80},{20,84},{24,88},{28,92},{32,9... | collective-permute-start | bytes 4718600 | tf_op jit(solution)/shard_map/ppermute | solution.py:48
  987.2 1.1 copy-start.4
Sparse Core Ops, SparseCore 0:
  406.7 135.6 all-gather.9
  769.0 169.6 reduce-scatter.1
  988.5 66.3 all-gather.7
where the time goes:
time: 1090 us; the launch traced here: 1070 us
  blocking collectives  487 us (45%)
  waiting for transfers between devices  260 us (24%)
  local copies, waits for them, and re-layouts  149 us (14%)
  other arithmetic  98.5 us (9%)
  matrix products  46.8 us (4%)
  starting transfers between devices  17.9 us (2%)
  between operations  14.4 us (1%)
    psum x1, blocking collectives, shards(): global_q, global_kv = lax.psum((local_queries, local_pairs), 'ctx')  322 us
    reduce_scatter x1, waiting for transfers between devices, shards(): lax.psum_scatter(lax.dot_general(out_weight, attended, (((0,), (1,)), (()...  169 us
    all_gather x2, blocking collectives, combined_all(): everything = jax.tree.map(lambda part: lax.all_gather(part, axis), x)  160 us
    all_gather x1, waiting for transfers between devices, shards(): lax.all_gather(arrived, 'tp', axis=1, tiled=True)  57.2 us
    add x31, other arithmetic, combine_partials(): acc_first * factor_first[..., None] + acc_second * factor_second[..., None]  37.3 us
    unnamed x41, local copies, waits for them, and re-layouts  36.6 us
    ppermute x1, waiting for transfers between devices, passed_along(): return lax.ppermute(value, axis, pairs)  33.9 us
    gather x1, local copies, waits for them, and re-layouts, shards(): outgoing = jnp.take(pair_blocks, source_ids, axis=0)  28.4 us
  transfers between devices with their start and end apart: 7, of which 3 were waited for; matrix products, arithmetic and copies ran while one was open for 14% of the time, Pallas kernels for 0%

commit v1 on v0

v1 whole, which is shorter than its diff:
```python
import functools
import math

import jax
import jax.numpy as jnp
from jax import lax
from jax.experimental import pallas as pl
from jax.experimental.pallas import tpu as pltpu
from jax.sharding import PartitionSpec as P

D = 4096
BLOCK = 64
MAXR = 3
G = 2
R = 3
SPAN = 2 * MAXR + 1
MESH = pl.DeviceIdType.MESH
VMEM = pltpu.VMEM
SMEM = pltpu.SMEM

norm_eps = 1e-05


def greet(axis, count):
    me = lax.axis_index(axis)
    barrier = pltpu.get_barrier_semaphore()

    def signal(k, carry):
        pl.semaphore_signal(
            barrier, inc=1, device_id={axis: lax.rem(me + k, count)}, device_id_type=MESH
        )
        return carry

    lax.fori_loop(1, count, signal, 0)
    pl.semaphore_wait(barrier, count - 1)


def edges_kernel(
    count,
    place_ref,
    kv_ref,
    q_ref,
    ext_ref,
    gkv_ref,
    gq_ref,
    cand,
    got,
    full,
    halo_send,
    halo_recv,
    send1,
    recv1,
    send2,
    recv2,
):
    me = lax.axis_index("ctx")
    blocks = kv_ref.shape[0]
    wide = kv_ref.shape[2]
    half = q_ref.shape[2]
    part = (wide + half) // 4
    greet("ctx", count)
    after = lax.rem(me + 1, count)
    before = lax.rem(me + count - 1, count)
    to_after = pltpu.make_async_remote_copy(
        src_ref=kv_ref.at[pl.ds(blocks - MAXR, MAXR)],
        dst_ref=ext_ref.at[pl.ds(0, MAXR)],
        send_sem=halo_send.at[0],
        recv_sem=halo_recv.at[0],
        device_id={"ctx": after},
        device_id_type=MESH,
    )
    to_before = pltpu.make_async_remote_copy(
        src_ref=kv_ref.at[pl.ds(0, MAXR)],
        dst_ref=ext_ref.at[pl.ds(blocks + MAXR, MAXR)],
        send_sem=halo_send.at[1],
        recv_sem=halo_recv.at[1],
        device_id={"ctx": before},
        device_id_type=MESH,
    )
    for g in range(G):
        local = place_ref[G + g]
        row = jnp.concatenate([kv_ref[local], q_ref[local]], axis=1)
        for r in range(4):
            for c in range(4):
                cand[(g * 4 + r) * 4 + c] = row[r * 16 : r * 16 + 16, c * part : (c + 1) * part]

    def first(k):
        to = lax.rem(me + k, count)
        return pltpu.make_async_remote_copy(
            src_ref=cand.at[to],
            dst_ref=got.at[me],
            send_sem=send1.at[k],
            recv_sem=recv1.at[k],
            device_id={"ctx": to},
            device_id_type=MESH,
        )

    def second(k):
        to = lax.rem(me + k, count)
        return pltpu.make_async_remote_copy(
            src_ref=full.at[me],
            dst_ref=full.at[me],
            send_sem=send2.at[k],
            recv_sem=recv2.at[k],
            device_id={"ctx": to},
            device_id_type=MESH,
        )

    def each(action):
        def body(k, carry):
            action(k)
            return carry

        lax.fori_loop(1, count, body, 0)

    each(lambda k: first(k).start())
    to_after.start()
    to_before.start()
    got[me] = cand[me]
    ext_ref[pl.ds(MAXR, blocks)] = kv_ref[...]
    each(lambda k: first(k).wait())
    full[me] = got[place_ref[me // (count // G)]]
    each(lambda k: second(k).start())
    each(lambda k: second(k).wait())
    for g in range(G):
        for r in range(4):
            row = jnp.concatenate([full[(g * 4 + r) * 4 + c] for c in range(4)], axis=1)
            gkv_ref[g, r * 16 : r * 16 + 16, :] = row[:, :wide]
            gq_ref[g, r * 16 : r * 16 + 16, :] = row[:, wide:]
    to_after.wait()
    to_before.wait()


def edges(place, kv, q, count):
    blocks, rows, wide = kv.shape
    half = q.shape[2]
    part = (wide + half) // 4
    return pl.pallas_call(
        functools.partial(edges_kernel, count),
        name="edges",
        out_shape=(
            jax.ShapeDtypeStruct((blocks + 2 * MAXR, rows, wide), kv.dtype),
            jax.ShapeDtypeStruct((G, rows, wide), kv.dtype),
            jax.ShapeDtypeStruct((G, rows, half), kv.dtype),
        ),
        in_specs=[
            pl.BlockSpec(memory_space=SMEM),
            pl.BlockSpec(memory_space=VMEM),
            pl.BlockSpec(memory_space=VMEM),
        ],
        out_specs=(pl.BlockSpec(memory_space=VMEM),) * 3,
        scratch_shapes=[
            VMEM((count, 16, part), kv.dtype),
            VMEM((count, 16, part), kv.dtype),
            VMEM((count, 16, part), kv.dtype),
            pltpu.SemaphoreType.DMA((2,)),
            pltpu.SemaphoreType.DMA((2,)),
            pltpu.SemaphoreType.DMA((count,)),
            pltpu.SemaphoreType.DMA((count,)),
            pltpu.SemaphoreType.DMA((count,)),
            pltpu.SemaphoreType.DMA((count,)),
        ],
        compiler_params=pltpu.CompilerParams(
            collective_id=0, has_side_effects=True, vmem_limit_bytes=48 * 2**20
        ),
    )(place, kv, q)


def far_kernel(scale, head_count, gq_ref, kv_ref, out_ref):
    blocks, rows, wide = kv_ref.shape
    size = wide // (2 * head_count)
    for h in range(head_count):
        lanes = slice(h * size, (h + 1) * size)
        q = gq_ref[:, :, lanes].reshape(G * rows, size)
        k = kv_ref[:, :, lanes].reshape(blocks * rows, size)
        v = kv_ref[:, :, wide // 2 + h * size : wide // 2 + (h + 1) * size].reshape(
            blocks * rows, size
        )
        s = (
            lax.dot_general(q, k, (((1,), (1,)), ((), ())), preferred_element_type=jnp.float32)
            * scale
        )
        peak = jnp.max(s, axis=1, keepdims=True)
        p = jnp.exp(s - peak)
        total = jnp.sum(p, axis=1, keepdims=True)
        acc = jnp.dot(p.astype(jnp.bfloat16), v, preferred_element_type=jnp.float32)
        peak = jnp.broadcast_to(peak, acc.shape)
        total = jnp.broadcast_to(total, acc.shape)
        for r in range(8):
            cut = slice(r * 16, r * 16 + 16)
            out_ref[h * 8 + r, 0:16, :] = acc[cut]
            out_ref[h * 8 + r, 16:32, :] = peak[cut]
            out_ref[h * 8 + r, 32:48, :] = total[cut]


def far_partials(gq, kv, scale, head_count, count):
    size = gq.shape[2] // head_count
    return pl.pallas_call(
        functools.partial(far_kernel, scale, head_count),
        name="far_partials",
        out_shape=jax.ShapeDtypeStruct((count, 48, size), jnp.float32),
        in_specs=[pl.BlockSpec(memory_space=VMEM)] * 2,
        out_specs=pl.BlockSpec(memory_space=VMEM),
        compiler_params=pltpu.CompilerParams(vmem_limit_bytes=48 * 2**20),
    )(gq, kv)


def exchange_kernel(
    count,
    slots,
    source_ref,
    kv_ref,
    part_ref,
    random_ref,
    far_ref,
    stage,
    got,
    bulk_send,
    bulk_recv,
    send1,
    recv1,
    send2,
    recv2,
    own_sem,
):
    me = lax.axis_index("ctx")
    greet("ctx", count)

    def first(k):
        to = lax.rem(me + k, count)
        return pltpu.make_async_remote_copy(
            src_ref=part_ref.at[to],
            dst_ref=got.at[me],
            send_sem=send1.at[k],
            recv_sem=recv1.at[k],
            device_id={"ctx": to},
            device_id_type=MESH,
        )

    def second(k):
        to = lax.rem(me + k, count)
        return pltpu.make_async_remote_copy(
            src_ref=far_ref.at[me],
            dst_ref=far_ref.at[me],
            send_sem=send2.at[k],
            recv_sem=recv2.at[k],
            device_id={"ctx": to},
            device_id_type=MESH,
        )

    def bulk(k):
        to = lax.rem(me + k, count)
        return pltpu.make_async_remote_copy(
            src_ref=stage.at[pl.ds(to * slots, slots)],
            dst_ref=random_ref.at[pl.ds(me * slots, slots)],
            send_sem=bulk_send.at[k],
            recv_sem=bulk_recv.at[k],
            device_id={"ctx": to},
            device_id_type=MESH,
        )

    def each(action):
        def body(k, carry):
            action(k)
            return carry

        lax.fori_loop(1, count, body, 0)

    each(lambda k: first(k).start())
    got[me] = part_ref[me]

    def place(i, carry):
        stage[i] = kv_ref[source_ref[i]]
        return carry

    lax.fori_loop(0, count * slots, place, 0)
    each(lambda k: bulk(k).start())
    own = pltpu.make_async_copy(
        stage.at[pl.ds(me * slots, slots)], random_ref.at[pl.ds(me * slots, slots)], own_sem
    )
    own.start()
    each(lambda k: first(k).wait())

    def top(i, so_far):
        return jnp.maximum(so_far, got[i, 16:32, :])

    peak = lax.fori_loop(1, count, top, got[0, 16:32, :])

    def add(i, so_far):
        acc, total = so_far
        factor = jnp.exp(got[i, 16:32, :] - peak)
        return acc + got[i, 0:16, :] * factor, total + got[i, 32:48, :] * factor

    zero = jnp.zeros_like(peak)
    acc, total = lax.fori_loop(0, count, add, (zero, zero))
    far_ref[me] = (acc / total).astype(far_ref.dtype)
    each(lambda k: second(k).start())
    own.wait()
    each(lambda k: bulk(k).wait())
    each(lambda k: second(k).wait())


def exchange(source, kv, partials, count, slots):
    blocks, rows, wide = kv.shape
    size = partials.shape[2]
    dma = pltpu.SemaphoreType.DMA((count,))
    return pl.pallas_call(
        functools.partial(exchange_kernel, count, slots),
        name="exchange",
        out_shape=(
            jax.ShapeDtypeStruct((count * slots, rows, wide), kv.dtype),
            jax.ShapeDtypeStruct((count, 16, size), kv.dtype),
        ),
        in_specs=[
            pl.BlockSpec(memory_space=SMEM),
            pl.BlockSpec(memory_space=VMEM),
            pl.BlockSpec(memory_space=VMEM),
        ],
        out_specs=(pl.BlockSpec(memory_space=pl.ANY), pl.BlockSpec(memory_space=VMEM)),
        scratch_shapes=[
            VMEM((count * slots, rows, wide), kv.dtype),
            VMEM((count, 48, size), jnp.float32),
            dma,
            dma,
            dma,
            dma,
            dma,
            dma,
            pltpu.SemaphoreType.DMA,
        ],
        compiler_params=pltpu.CompilerParams(
            collective_id=1, has_side_effects=True, vmem_limit_bytes=56 * 2**20
        ),
    )(source, kv, partials)


def attention_kernel(
    scale,
    head_count,
    all_blocks,
    index_ref,
    info_ref,
    q_ref,
    ext_ref,
    gkv_ref,
    far_ref,
    rand0,
    rand1,
    rand2,
    out_ref,
):
    b = pl.program_id(0)
    rows = q_ref.shape[1]
    wide = gkv_ref.shape[2]
    half = wide // 2
    size = half // head_count
    me = lax.axis_index("ctx")
    block = me * pl.num_programs(0) + b
    replaced = info_ref[head_count + b]
    near = SPAN * rows
    spot = lax.broadcasted_iota(jnp.int32, (rows, near), 1) // rows - MAXR
    inside = (spot + block >= 0) & (spot + block < all_blocks)
    for h in range(head_count):
        kl = slice(h * size, (h + 1) * size)
        vl = slice(half + h * size, half + (h + 1) * size)
        reach = info_ref[h]
        q = q_ref[0, :, kl]

        def listed(lanes):
            return jnp.concatenate(
                [
                    gkv_ref[0, :, lanes],
                    gkv_ref[1, :, lanes],
                    rand0[0, :, lanes],
                    rand1[0, :, lanes],
                    rand2[0, :, lanes],
                ],
                axis=0,
            )

        def score(keys):
            return (
                lax.dot_general(
                    q, keys, (((1,), (1,)), ((), ())), preferred_element_type=jnp.float32
                )
                * scale
            )

        window_k = ext_ref[pl.ds(b, SPAN), :, kl].reshape(near, size)
        window_v = ext_ref[pl.ds(b, SPAN), :, vl].reshape(near, size)
        s1 = jnp.where(inside & (jnp.abs(spot) <= reach), score(window_k), -jnp.inf)
        s2 = score(listed(kl))
        peak = jnp.maximum(
            jnp.max(s1, axis=1, keepdims=True), jnp.max(s2, axis=1, keepdims=True)
        )
        p1 = jnp.exp(s1 - peak)
        p2 = jnp.exp(s2 - peak)
        total = jnp.sum(p1, axis=1, keepdims=True) + jnp.sum(p2, axis=1, keepdims=True)
        acc = jnp.dot(p1.astype(jnp.bfloat16), window_v, preferred_element_type=jnp.float32)
        acc = acc + jnp.dot(
            p2.astype(jnp.bfloat16), listed(vl), preferred_element_type=jnp.float32
        )
        out_ref[0, :, kl] = (acc / total).astype(out_ref.dtype)

    for g in range(G):

        @pl.when(replaced == g)
        def _():
            for h in range(head_count):
                for r in range(4):
                    out_ref[0, r * 16 : r * 16 + 16, h * size : (h + 1) * size] = far_ref[
                        h * 8 + g * 4 + r
                    ]


def attention(index, info, q, ext, gkv, far, random, scale, head_count, all_blocks):
    blocks, rows, half = q.shape
    wide = 2 * half

    def whole(x):
        return pl.BlockSpec(x.shape, lambda b, *_: (0,) * x.ndim)

    def pick(r):
        return pl.BlockSpec((1, rows, wide), lambda b, index, info: (index[b * R + r], 0, 0))

    one = pl.BlockSpec((1, rows, half), lambda b, *_: (b, 0, 0))
    return pl.pallas_call(
        functools.partial(attention_kernel, scale, head_count, all_blocks),
        name="attention",
        grid_spec=pltpu.PrefetchScalarGridSpec(
            num_scalar_prefetch=2,
            grid=(blocks,),
            in_specs=[one, whole(ext), whole(gkv), whole(far), pick(0), pick(1), pick(2)],
            out_specs=one,
        ),
        out_shape=jax.ShapeDtypeStruct(q.shape, q.dtype),
        compiler_params=pltpu.CompilerParams(vmem_limit_bytes=48 * 2**20),
    )(index, info, q, ext, gkv, far, random, random, random)


def shards(
    queries,
    keyvals,
    residual,
    out_weight,
    norm_gain,
    norm_bias,
    cross_weight,
    window_reach,
    global_blocks,
    random_blocks,
):
    tok_rows, head_cols = queries.shape
    head_count = window_reach.shape[0]
    head_size = head_cols // head_count
    ctx_count = lax.axis_size("ctx")
    me = lax.axis_index("ctx")
    block_count = tok_rows // BLOCK
    all_blocks = block_count * ctx_count
    scale = 1.0 / math.sqrt(head_size)
    q = queries.reshape(block_count, BLOCK, head_cols)
    kv = keyvals.reshape(block_count, BLOCK, 2 * head_cols)

    req_count = block_count * R
    slots = 1 + (req_count + ctx_count - 2) // ctx_count
    requests = random_blocks.reshape(ctx_count, req_count)
    owners = requests // block_count
    local_ids = requests % block_count
    positions = jnp.arange(req_count, dtype=jnp.int32)
    earlier = positions[None, :] < positions[:, None]
    ranks = jnp.sum(
        ((owners[:, :, None] == owners[:, None, :]) & earlier[None, :, :]).astype(jnp.int32), axis=2
    )
    slot_ids = jnp.arange(slots, dtype=jnp.int32)
    matches = (owners[:, None, :] == me) & (ranks[:, None, :] == slot_ids[None, :, None])
    source_ids = jnp.sum(jnp.where(matches, local_ids[:, None, :], 0), axis=2).reshape(-1)
    my_index = lax.dynamic_index_in_dim(owners * slots + ranks, me, 0, keepdims=False)
    place = jnp.concatenate([global_blocks // block_count, global_blocks % block_count])
    own_ids = me * block_count + jnp.arange(block_count, dtype=jnp.int32)
    replaced = jnp.where(
        own_ids == global_blocks[0], 0, jnp.where(own_ids == global_blocks[1], 1, -1)
    )
    info = jnp.concatenate([window_reach, replaced])

    ext, gkv, gq = edges(place, kv, q, ctx_count)
    partials = far_partials(gq, kv, scale, head_count, ctx_count)
    random, far = exchange(source_ids, kv, partials, ctx_count, slots)
    attended = attention(my_index, info, q, ext, gkv, far, random, scale, head_count, all_blocks)
    attended = attended.reshape(tok_rows, head_cols)
    summed = lax.psum_scatter(
        lax.dot_general(
            out_weight, attended, (((0,), (1,)), ((), ())), preferred_element_type=jnp.float32
        ),
        "tp",
        scatter_dimension=0,
        tiled=True,
    )
    mixed_part = summed.T
    mixed = residual.astype(jnp.float32) + mixed_part
    row_sum = jnp.sum(mixed, axis=1)
    row_square = jnp.sum(mixed * mixed, axis=1)
    total_sum, total_square = lax.psum((row_sum, row_square), "tp")
    row_mean = total_sum / D
    variance = total_square / D - row_mean * row_mean
    normalized = (mixed - row_mean[:, None]) * lax.rsqrt(variance[:, None] + norm_eps)
    encoded = (normalized * norm_gain.astype(jnp.float32) + norm_bias.astype(jnp.float32)).astype(
        jnp.bfloat16
    )
    flat_weight = cross_weight.reshape(D, 2 * head_cols)
    half_way = ctx_count // 2
    arrived = passed_along(encoded, "ctx", half_way)
    cross_kv = jnp.dot(
        lax.all_gather(arrived, "tp", axis=1, tiled=True),
        flat_weight,
        preferred_element_type=jnp.float32,
    ).astype(jnp.bfloat16)
    return (encoded, cross_kv.reshape(tok_rows, 2, head_cols))


def passed_along(value, axis, steps):
    count = lax.axis_size(axis)
    pairs = [(source, (source + steps) % count) for source in range(count)]
    return lax.ppermute(value, axis, pairs)


def solution(mesh):
    placed = (
        P("ctx", "tp"),
        P("ctx", None, "tp"),
        P("ctx", "tp"),
        P("tp", None),
        P("tp"),
        P("tp"),
        P(None, None, "tp"),
        P("tp"),
        P(),
        P(),
    )
    return jax.shard_map(
        shards,
        mesh=mesh,
        in_specs=placed,
        out_specs=(P("ctx", "tp"), P("ctx", None, "tp")),
        check_vma=False,
    )
```

time: 1090 us -> 672 us (0.62); the launches traced: 1070 us -> 672 us
  blocking collectives: 487 us -> 5.5 us
  Pallas kernels: 0 us -> 357 us
  local copies, waits for them, and re-layouts: 149 us -> 23.7 us
  other arithmetic: 98.5 us -> 9.75 us
  matrix products: 46.8 us -> 17.3 us
  waiting for transfers between devices: 260 us -> 242 us
  starting transfers between devices: 17.9 us -> 2.77 us
    pallas_call x0 -> x4, Pallas kernels: none -> 357 us  [the longest x1 298 us: exchange(): pl.pallas_call(functools.partial(exchange_kernel, count, slots), name='ex...]
    psum x1 -> x0, blocking collectives: 322 us -> none  [shards(): global_q, global_kv = lax.psum((local_queries, local_pairs), 'ctx')]
    all_gather x2 -> x0, blocking collectives: 160 us -> none  [combined_all(): everything = jax.tree.map(lambda part: lax.all_gather(part, axis), x)]
    add x64 -> x0, other arithmetic: 59.8 us -> none  [the longest x31 37.3 us: combine_partials(): acc_first * factor_first[..., None] + acc_second * factor_second[..., None]]
    gather x3 -> x0, local copies, waits for them, and re-layouts: 48.7 us -> none  [the longest x1 28.4 us: shards(): outgoing = jnp.take(pair_blocks, source_ids, axis=0)]
    another operation x3 -> x0, local copies, waits for them, and re-layouts: 30.3 us -> none  [the longest x1 14 us: shards(): listed[:, :, :, 0]]
    dot_general x7 -> x0, matrix products: 27.1 us -> none  [the longest x1 12.8 us: shards(): jnp.einsum('bhqjk,bjkhd->bqhd', rounded_output, listed_values, preferred_...]
    slice x8 -> x1, local copies, waits for them, and re-layouts: 25.7 us -> 1.37 us  [shards(): global_blocks[0]]
  transfers between devices with their start and end apart: 7 -> 3, of which waited for: 3 -> 3; matrix products, arithmetic and copies ran while one was open for 14% -> 1% of each run, Pallas kernels for 0% -> 0%
where the time goes in v1:
time: 672 us
  Pallas kernels  357 us (53%)
  waiting for transfers between devices  242 us (36%)
  local copies, waits for them, and re-layouts  23.7 us (4%)
  matrix products  17.3 us (3%)
  between operations  14.3 us (2%)
  other arithmetic  9.75 us (1%)
    pallas_call x1, Pallas kernels, exchange(): pl.pallas_call(functools.partial(exchange_kernel, count, slots), name='ex...  298 us
    reduce_scatter x1, waiting for transfers between devices, shards(): lax.psum_scatter(lax.dot_general(out_weight, attended, (((0,), (1,)), (()...  150 us
    all_gather x1, waiting for transfers between devices, shards(): lax.all_gather(arrived, 'tp', axis=1, tiled=True)  57.2 us
    pallas_call x1, Pallas kernels, edges(): pl.pallas_call(functools.partial(edges_kernel, count), name='edges', out_...  38.4 us
    ppermute x1, waiting for transfers between devices, passed_along(): return lax.ppermute(value, axis, pairs)  34 us
    pallas_call x1, Pallas kernels, attention(): pl.pallas_call(functools.partial(attention_kernel, scale, head_count, all...  19.5 us
    unnamed x27, local copies, waits for them, and re-layouts  15.4 us
  transfers between devices with their start and end apart: 3, of which 3 were waited for; matrix products, arithmetic and copies ran while one was open for 1% of the time, Pallas kernels for 0%

profile of v1, /device:TPU:1, one launch (start us, length us, event | category | flops | bytes accessed | tf_op | source)
XLA Modules:
  0.0 672.0 jit_solution(2776466798942620087)
XLA Ops:
  7.2 0.0 copy-start.2
  7.2 0.0 reduce-scatter.2.cloned.1.call-start
  7.2 0.8 broadcast_remainder_fusion
  8.0 0.7 sign_compare_fusion
  8.7 0.7 and_select_fusion.1
  9.4 1.4 fusion.3
  10.7 0.1 copy.46
  10.9 0.1 rem.45
  11.0 0.1 copy.47
  11.2 0.1 div.33
  11.3 0.2 copy.45
  11.5 0.1 ne.74
  11.6 0.1 copy.48
  11.7 0.9 convert_reduce_fusion
  12.6 0.1 copy.49
  12.7 0.1 select_reduce_fusion
  12.8 0.1 copy.51
  12.9 0.6 reshape.103.source_ref
  13.6 2.8 reshape.102.kv_ref
  16.4 0.0 copy-start
  16.4 0.1 pad_add_fusion.1.place_ref
  16.5 0.0 copy-done.2
  16.5 0.0 copy-start.12
  16.5 38.4 %edges.1 = (bf16[18,64,1024]{2,1,0:T(8,128)(2,1)S(1)}, bf16[2,64,1024]{2,1,0:T(8,128)(2,1)S(1)}, bf16[2,64,512]{2,1,0:T(8,128)(2,1)S(1)}) custom-call(s32[4]{0:T(128)S(1)} %pad_add_fusion.1.place_ref, bf16[12,64,1024]{2,1,0:T(8,128)(2,1)S(1)} %reshape.102.kv_ref, bf16[12,64,512]{2,1,0:T(8,128)(2,1)S(1)} %bitcast.22), custom_call_target="tpu_custom_call" | custom-call | tf_op jit(solution)/shard_map/edges/pallas_call | solution.py:138
  54.8 0.0 copy-start.3
  54.9 1.4 copy-done.3
  56.2 1.5 far_partials.1.part_ref
  57.7 0.0 copy-start.1
  57.7 0.9 copy-done.1
  58.6 0.0 copy-done
  58.6 0.0 copy-start.4
  58.6 297.8 %exchange.1 = (bf16[96,64,1024]{2,1,0:T(8,128)(2,1)}, bf16[32,16,128]{2,1,0:T(8,128)(2,1)}) custom-call(s32[96]{0:T(128)} %reshape.103.source_ref, bf16[12,64,1024]{2,1,0:T(8,128)(2,1)} %copy-done, f32[32,48,128]{2,1,0:T(8,128)} %copy-done.1), custom_call_target="tpu_custom_call" | custom-call | tf_op jit(solution)/shard_map/exchange/pallas_call | solution.py:307
  356.4 1.3 compare_select_fusion.1
  357.7 0.0 copy-done.12
  357.7 0.1 pad_add_fusion.info_ref
  357.8 0.0 copy-done.4
  357.8 0.0 copy-start.5
  357.8 0.9 copy-done.5
  358.7 0.0 copy-start.11
  358.7 19.5 %attention.1 = bf16[12,64,512]{2,1,0:T(8,128)(2,1)S(1)} custom-call(s32[36]{0:T(128)S(1)} %fusion.2.index_ref, s32[16]{0:T(128)S(1)} %pad_add_fusion.info_ref, bf16[12,64,512]{2,1,0:T(8,128)(2,1)S(1)} %bitcast.23, bf16[18,64,1024]{2,1,0:T(8,128)(2,1)S(1)} %copy-done.4, bf16[2,64,1024]{2,1,0:T(8,128)(2,1)S(1)} %get-tuple-element.8.gkv_ref, ...), custom_call_target="tpu_custom_call" | custom-call | tf_op jit(solution)/shard_map/attention/pallas_call | solution.py:427
  378.2 0.0 copy-done.11
  378.2 6.4 convolution_bitcast_fusion
  384.6 0.0 copy-start.10
  384.6 0.0 copy-start.6
  384.6 0.0 reduce-scatter.2.cloned.1.call-update
  384.7 0.0 all-gather.2.cloned.1.call-start
  384.7 0.6 copy-done.9
  385.3 0.0 copy-done.10
  385.3 150.5 %reduce-scatter.2.cloned.1.call-done = f32[1024,768]{0,1:T(8,128)} async-done(((f32[4096,768]{0,1:T(8,128)}), f32[1024,768]{0,1:T(8,128)}) %reduce-scatter.2.cloned.1.call-update) | async-done | bytes 3145744 | tf_op jit(solution)/shard_map/reduce_scatter | solution.py:490
  535.8 0.0 copy-done.6
  535.8 2.5 fusion
  538.3 5.5 all-reduce
  543.9 2.6 add_convert_fusion
  546.5 0.0 copy-start.8
  546.5 1.1 copy-done.8
  547.6 2.7 collective-permute-start
  550.3 34.0 %collective-permute-done = bf16[768,1024]{1,0:T(8,128)(2,1)S(1)} collective-permute-done((bf16[768,1024]{1,0:T(8,128)(2,1)S(1)}, bf16[768,1024]{1,0:T(8,128)(2,1)S(1)}, u32[]{:S(2)}, u32[]{:S(2)}) %collective-permute-start) | collective-permute-done | bytes 1572896 | tf_op jit(solution)/shard_map/ppermute | solution.py:523
  584.3 0.0 copy-start.7
  584.3 1.1 copy-done.7
  585.4 0.0 all-gather.2.cloned.1.call-update
  585.4 9.3 %copy.52 = bf16[512,8,2,512]{3,1,2,0:T(8,128)(2,1)} copy(bf16[512,8,2,512]{3,2,1,0:T(2,128)(2,1)} %bitcast.25) | data formatting | bytes 16777216
  594.7 57.2 %all-gather.2.cloned.1.call-done = bf16[768,4096]{1,0:T(8,128)(2,1)} async-done(((bf16[768,1024]{1,0:T(8,128)(2,1)}), bf16[768,4096]{1,0:T(8,128)(2,1)}) %all-gather.2.cloned.1.call-update) | async-done | bytes 6291472 | tf_op jit(solution)/shard_map/all_gather | solution.py:513
  651.9 10.9 %convolution_convert_fusion = bf16[768,1024]{1,0:T(8,128)(2,1)S(1)} fusion(bf16[768,4096]{1,0:T(8,128)(2,1)} %all-gather.2.cloned.1.call-done, bf16[4096,1024]{1,0:T(8,128)(2,1)} %bitcast.26), kind=kOutput, calls=%fused_computation.4 | convolution fusion | flops 6443237376 | bytes 16252928 | tf_op jit(solution)/shard_map/dot_general | solution.py:512
  662.8 2.4 reshape.106
  (8 shorter events, 0.0 us)
Async XLA Ops:
  7.2 9.3 %copy-start.2 = (bf16[768,512]{1,0:T(8,128)(2,1)S(1)}, bf16[768,512]{1,0:T(8,128)(2,1)}, u32[]{:S(2)}) copy-start(bf16[768,512]{1,0:T(8,128)(2,1)} %param.10) | copy-start | bytes 2359300
  7.2 528.7 %reduce-scatter.2.cloned.1.call-start = ((), (), s32[]{:S(2)}) async-start(), calls=%async_computation.1 | async-start | bytes 15728640 | tf_op jit(solution)/shard_map/reduce_scatter | solution.py:490
  16.4 42.2 %copy-start = (bf16[12,64,1024]{2,1,0:T(8,128)(2,1)}, bf16[12,64,1024]{2,1,0:T(8,128)(2,1)S(1)}, u32[]{:S(2)}) copy-start(bf16[12,64,1024]{2,1,0:T(8,128)(2,1)S(1)} %reshape.102.kv_ref) | copy-start | bytes 4718596
  16.5 341.2 %copy-start.12 = (s32[4]{0:T(128)S(1)}, s32[4]{0:T(128)}, u32[]{:S(2)}) copy-start(s32[4]{0:T(128)} %param.17) | copy-start | bytes 52
  54.8 1.4 copy-start.3
  57.7 0.9 copy-start.1
  58.6 299.2 %copy-start.4 = (bf16[18,64,1024]{2,1,0:T(8,128)(2,1)S(1)}, bf16[18,64,1024]{2,1,0:T(8,128)(2,1)}, u32[]{:S(2)}) copy-start(bf16[18,64,1024]{2,1,0:T(8,128)(2,1)} %copy-done.3) | copy-start | bytes 7077892
  357.8 0.9 copy-start.5
  358.7 19.6 %copy-start.11 = (bf16[512,4096]{1,0:T(8,128)(2,1)S(1)}, bf16[512,4096]{1,0:T(8,128)(2,1)}, u32[]{:S(2)}) copy-start(bf16[512,4096]{1,0:T(8,128)(2,1)} %param.13) | copy-start | bytes 12582916
  384.6 0.7 copy-start.9
  384.6 0.7 copy-start.10
  384.6 151.2 %copy-start.6 = (bf16[768,1024]{1,0:T(8,128)(2,1)S(1)}, bf16[768,1024]{1,0:T(8,128)(2,1)}, u32[]{:S(2)}) copy-start(bf16[768,1024]{1,0:T(8,128)(2,1)} %param.12) | copy-start | bytes 4718596
  384.7 267.3 %all-gather.2.cloned.1.call-start = ((), (), s32[]{:S(2)}) async-start(), calls=%async_computation.2 | async-start | bytes 7864320 | tf_op jit(solution)/shard_map/all_gather | solution.py:513
  546.5 1.1 copy-start.8
  547.6 36.6 %collective-permute-start = (bf16[768,1024]{1,0:T(8,128)(2,1)S(1)}, bf16[768,1024]{1,0:T(8,128)(2,1)S(1)}, u32[]{:S(2)}, u32[]{:S(2)}) collective-permute-start(bf16[768,1024]{1,0:T(8,128)(2,1)S(1)} %add_convert_fusion), channel_id=1, source_target_pairs={{0,64},{4,68},{8,72},{12,76},{16,80},{20,84},{24,88},{28,92},{32,9... | collective-permute-start | bytes 4718600 | tf_op jit(solution)/shard_map/ppermute | solution.py:523
  584.3 1.1 copy-start.7
Sparse Core Ops, SparseCore 0:
  384.8 150.9 reduce-scatter.1
  585.5 66.3 all-gather.1

commit v2 on v1

--- a/solution.py
+++ b/solution.py
@@ -438,6 +438,251 @@
     )(index, info, q, ext, gkv, far, random, random, random)
 
 
+def project_kernel(
+    ctx_count,
+    tp_count,
+    chunks,
+    width,
+    att_ref,
+    residual_ref,
+    gain_ref,
+    bias_ref,
+    w0,
+    w1,
+    w2,
+    w3,
+    cross_ref,
+    encoded_ref,
+    out_ref,
+    w_all,
+    cross,
+    a1,
+    a2,
+    a3,
+    mixed,
+    stats,
+    g0,
+    g1,
+    g2,
+    g3,
+    w_sem,
+    cross_sem,
+    send_sem,
+    recv_sem,
+):
+    ctx = lax.axis_index("ctx")
+    tp = lax.axis_index("tp")
+    mate = tp + 1 - 2 * lax.rem(tp, 2)
+    over = lax.rem(tp + 2, tp_count)
+    cater = tp_count - 1 - tp
+    beyond = lax.rem(ctx + ctx_count // 2, ctx_count)
+    rows = att_ref.shape[0] // chunks
+    cols = residual_ref.shape[1]
+
+    for k, w in enumerate((w0, w1, w2, w3)):
+        pltpu.make_async_copy(w, w_all.at[k], w_sem.at[k]).start()
+    for k, block in enumerate((tp, mate, over, cater)):
+        pltpu.make_async_copy(
+            cross_ref.at[pl.ds(block * cols, cols)], cross.at[k], cross_sem.at[k]
+        ).start()
+
+    barrier = pltpu.get_barrier_semaphore()
+    for other in (mate, over, cater):
+        pl.semaphore_signal(barrier, inc=1, device_id={"tp": other}, device_id_type=MESH)
+    pl.semaphore_signal(barrier, inc=1, device_id={"ctx": beyond}, device_id_type=MESH)
+    pl.semaphore_wait(barrier, 4)
+
+    def cut(c):
+        return pl.ds(pl.multiple_of(c * rows, rows), rows)
+
+    def hop(kind, c, src, dst, where):
+        return pltpu.make_async_remote_copy(
+            src_ref=src,
+            dst_ref=dst,
+            send_sem=send_sem.at[kind, c],
+            recv_sem=recv_sem.at[kind, c],
+            device_id=where,
+            device_id_type=MESH,
+        )
+
+    def att_mate(c):
+        return hop(0, c, att_ref.at[cut(c)], a1.at[cut(c)], {"tp": mate})
+
+    def att_over(c):
+        return hop(1, c, att_ref.at[cut(c)], a2.at[cut(c)], {"tp": over})
+
+    def att_on(c):
+        return hop(2, c, a2.at[cut(c)], a3.at[cut(c)], {"tp": mate})
+
+    def stat(c, k):
+        other = (mate, over, cater)[k - 1]
+        return hop(2 + k, c, stats.at[c, 0], stats.at[c, k], {"tp": other})
+
+    def roll(c):
+        return hop(6, c, encoded_ref.at[cut(c)], g0.at[cut(c)], {"ctx": beyond})
+
+    def enc_mate(c):
+        return hop(7, c, g0.at[cut(c)], g1.at[cut(c)], {"tp": mate})
+
+    def enc_over(c):
+        return hop(8, c, g0.at[cut(c)], g2.at[cut(c)], {"tp": over})
+
+    def enc_on(c):
+        return hop(9, c, g2.at[cut(c)], g3.at[cut(c)], {"tp": mate})
+
+    def begin(c, carry):
+        att_over(c).start()
+        att_mate(c).start()
+        return carry
+
+    lax.fori_loop(0, chunks, begin, 0)
+    for k, w in enumerate((w0, w1, w2, w3)):
+        pltpu.make_async_copy(w, w_all.at[k], w_sem.at[k]).wait()
+
+    def step(t, carry):
+        def at(delay, body):
+            c = t - delay
+
+            @pl.when((c >= 0) & (c < chunks))
+            def _():
+                body(c)
+
+        def relay_att(c):
+            att_over(c).wait_recv()
+            att_on(c).start()
+
+        def relay_enc(c):
+            roll(c).wait_recv()
+            enc_over(c).start()
+            enc_mate(c).start()
+
+        def relay_on(c):
+            enc_over(c).wait_recv()
+            enc_on(c).start()
+
+        def normalize(c):
+            for k in (1, 2, 3):
+                stat(c, k).wait_recv()
+            both = stats[c, 0] + stats[c, 1] + stats[c, 2] + stats[c, 3]
+            total = jnp.transpose(jnp.broadcast_to(both[0:1], (rows, rows)))[:, 0:1]
+            square = jnp.transpose(jnp.broadcast_to(both[8:9], (rows, rows)))[:, 0:1]
+            mean = total / width
+            variance = square / width - mean * mean
+            scaled = (mixed[cut(c), :] - mean) * lax.rsqrt(variance + norm_eps)
+            encoded_ref[cut(c), :] = (
+                scaled * gain_ref[...].astype(jnp.float32) + bias_ref[...].astype(jnp.float32)
+            ).astype(encoded_ref.dtype)
+
+        def mix(c):
+            att_mate(c).wait_recv()
+            att_on(c).wait_recv()
+            part = residual_ref[cut(c), :].astype(jnp.float32)
+            for k, a in enumerate((att_ref, a1, a2, a3)):
+                part = part + jnp.dot(
+                    a[cut(c), :], w_all[k], preferred_element_type=jnp.float32
+                )
+            mixed[cut(c), :] = part
+            lane = lax.broadcasted_iota(jnp.int32, (rows, rows), 1)
+            total = jnp.sum(part, axis=1, keepdims=True)
+            square = jnp.sum(part * part, axis=1, keepdims=True)
+            turned = jnp.transpose(jnp.where(lane < rows // 2, total, square))
+            stats[c, 0, 0:8, :] = turned[0:8]
+            stats[c, 0, 8:16, :] = turned[rows // 2 : rows // 2 + 8]
+
+        def cast(c):
+            enc_mate(c).wait_recv()
+            enc_on(c).wait_recv()
+            acc = jnp.zeros((rows, out_ref.shape[1]), jnp.float32)
+            for k, g in enumerate((g0, g1, g2, g3)):
+                acc = acc + jnp.dot(g[cut(c), :], cross[k], preferred_element_type=jnp.float32)
+            out_ref[cut(c), :] = acc.astype(out_ref.dtype)
+
+        at(0, relay_att)
+        at(ROLL, relay_enc)
+        at(ROLL + 2, relay_on)
+        at(2, normalize)
+        at(1, mix)
+
+        def send_rows(c):
+            roll(c).start()
+
+        def send_stats(c):
+            for k in (1, 2, 3):
+                stat(c, k).start()
+
+        at(2, send_rows)
+        at(1, send_stats)
+
+        @pl.when(t == ROLL + 3)
+        def _():
+            for k in range(4):
+                pltpu.make_async_copy(
+                    cross_ref.at[pl.ds(0, cols)], cross.at[k], cross_sem.at[k]
+                ).wait()
+
+        at(ROLL + 3, cast)
+        return carry
+
+    lax.fori_loop(0, chunks + ROLL + 3, step, 0)
+
+    def finish(c, carry):
+        att_mate(c).wait_send()
+        att_over(c).wait_send()
+        att_on(c).wait_send()
+        for k in (1, 2, 3):
+            stat(c, k).wait_send()
+        roll(c).wait_send()
+        enc_mate(c).wait_send()
+        enc_over(c).wait_send()
+        enc_on(c).wait_send()
+        return carry
+
+    lax.fori_loop(0, chunks, finish, 0)
+
+
+ROLL = 5
+CHUNKS = 6
+
+
+def project(att, residual, gain, bias, weights, cross_weight, ctx_count, tp_count):
+    rows, depth = att.shape
+    cols = residual.shape[1]
+    wide = cross_weight.shape[1]
+    vmem = pl.BlockSpec(memory_space=VMEM)
+    hbm = pl.BlockSpec(memory_space=pl.ANY)
+    kept = jnp.bfloat16
+    return pl.pallas_call(
+        functools.partial(project_kernel, ctx_count, tp_count, CHUNKS, cols * tp_count),
+        name="project",
+        out_shape=(
+            jax.ShapeDtypeStruct((rows, cols), kept),
+            jax.ShapeDtypeStruct((rows, wide), kept),
+        ),
+        in_specs=[vmem] * 4 + [hbm] * 5,
+        out_specs=(vmem, vmem),
+        scratch_shapes=[
+            VMEM((4, depth, cols), kept),
+            VMEM((4, cols, wide), kept),
+            VMEM((rows, depth), kept),
+            VMEM((rows, depth), kept),
+            VMEM((rows, depth), kept),
+            VMEM((rows, cols), jnp.float32),
+            VMEM((CHUNKS, 4, 16, rows // CHUNKS), jnp.float32),
+            VMEM((rows, cols), kept),
+            VMEM((rows, cols), kept),
+            VMEM((rows, cols), kept),
+            VMEM((rows, cols), kept),
+            pltpu.SemaphoreType.DMA((4,)),
+            pltpu.SemaphoreType.DMA((4,)),
+            pltpu.SemaphoreType.DMA((10, CHUNKS)),
+            pltpu.SemaphoreType.DMA((10, CHUNKS)),
+        ],
+        compiler_params=pltpu.CompilerParams(
+            collective_id=2, has_side_effects=True, vmem_limit_bytes=60 * 2**20
+        ),
+    )(att, residual, gain, bias, *weights, cross_weight)
+
+
 def shards(
     queries,
     keyvals,
@@ -487,40 +732,27 @@
     random, far = exchange(source_ids, kv, partials, ctx_count, slots)
     attended = attention(my_index, info, q, ext, gkv, far, random, scale, head_count, all_blocks)
     attended = attended.reshape(tok_rows, head_cols)
-    summed = lax.psum_scatter(
-        lax.dot_general(
-            out_weight, attended, (((0,), (1,)), ((), ())), preferred_element_type=jnp.float32
-        ),
-        "tp",
-        scatter_dimension=0,
-        tiled=True,
+    tp = lax.axis_index("tp")
+    tp_count = lax.axis_size("tp")
+    cols = residual.shape[1]
+    mates = (tp, tp + 1 - 2 * lax.rem(tp, 2), lax.rem(tp + 2, tp_count), tp_count - 1 - tp)
+    weights = []
+    for k in range(tp_count):
+        block = lax.dynamic_slice_in_dim(out_weight, mates[k] * cols, cols, axis=1)
+        if k > 0:
+            block = lax.ppermute(block, "tp", [(i, i ^ k) for i in range(tp_count)])
+        weights.append(block)
+    encoded, cross_kv = project(
+        attended,
+        residual,
+        norm_gain.reshape(1, cols),
+        norm_bias.reshape(1, cols),
+        weights,
+        cross_weight.reshape(D, 2 * head_cols),
+        ctx_count,
+        tp_count,
     )
-    mixed_part = summed.T
-    mixed = residual.astype(jnp.float32) + mixed_part
-    row_sum = jnp.sum(mixed, axis=1)
-    row_square = jnp.sum(mixed * mixed, axis=1)
-    total_sum, total_square = lax.psum((row_sum, row_square), "tp")
-    row_mean = total_sum / D
-    variance = total_square / D - row_mean * row_mean
-    normalized = (mixed - row_mean[:, None]) * lax.rsqrt(variance[:, None] + norm_eps)
-    encoded = (normalized * norm_gain.astype(jnp.float32) + norm_bias.astype(jnp.float32)).astype(
-        jnp.bfloat16
-    )
-    flat_weight = cross_weight.reshape(D, 2 * head_cols)
-    half_way = ctx_count // 2
-    arrived = passed_along(encoded, "ctx", half_way)
-    cross_kv = jnp.dot(
-        lax.all_gather(arrived, "tp", axis=1, tiled=True),
-        flat_weight,
-        preferred_element_type=jnp.float32,
-    ).astype(jnp.bfloat16)
     return (encoded, cross_kv.reshape(tok_rows, 2, head_cols))
-
-
-def passed_along(value, axis, steps):
-    count = lax.axis_size(axis)
-    pairs = [(source, (source + steps) % count) for source in range(count)]
-    return lax.ppermute(value, axis, pairs)
 
 
 def solution(mesh):

time: 672 us -> 533 us (0.79)
  waiting for transfers between devices: 242 us -> 0.01 us
  Pallas kernels: 357 us -> 497 us
  matrix products: 17.3 us -> 0 us
  between operations: 14.3 us -> 0.88 us
  other arithmetic: 9.75 us -> 2.5 us
    reduce_scatter x1 -> x0, waiting for transfers between devices: 150 us -> none  [shards(): lax.psum_scatter(lax.dot_general(out_weight, attended, (((0,), (1,)), (()...]
    pallas_call x0 -> x1, Pallas kernels: none -> 102 us  [project(): pl.pallas_call(functools.partial(project_kernel, ctx_count, tp_count, CHU...]
    all_gather x1 -> x0, waiting for transfers between devices: 57.2 us -> none  [shards(): lax.all_gather(arrived, 'tp', axis=1, tiled=True)]
    ppermute x1 -> x3, waiting for transfers between devices: 34 us -> 0.01 us  [shards(): block = lax.ppermute(block, 'tp', [(i, i ^ k) for i in range(tp_count)])]
    pallas_call x1, Pallas kernels: 38.4 us -> 71.3 us  [edges(): pl.pallas_call(functools.partial(edges_kernel, count), name='edges', out_...]
    dot_general x2 -> x0, matrix products: 17.3 us -> none  [the longest x1 10.9 us: shards(): jnp.dot(lax.all_gather(arrived, 'tp', axis=1, tiled=True), flat_weight, p...]
    unnamed x27 -> x28, local copies, waits for them, and re-layouts: 15.4 us -> 14.6 us
  transfers between devices with their start and end apart: 3 -> 3, of which waited for: 3 -> 0; matrix products, arithmetic and copies ran while one was open for 1% -> 3% of each run, Pallas kernels for 0% -> 74%
where the time goes in v2:
time: 533 us; the launch traced here: 532 us
  Pallas kernels  497 us (93%)
  local copies, waits for them, and re-layouts  29.5 us (6%)
    pallas_call x1, Pallas kernels, exchange(): pl.pallas_call(functools.partial(exchange_kernel, count, slots), name='ex...  303 us
    pallas_call x1, Pallas kernels, project(): pl.pallas_call(functools.partial(project_kernel, ctx_count, tp_count, CHU...  102 us
    pallas_call x1, Pallas kernels, edges(): pl.pallas_call(functools.partial(edges_kernel, count), name='edges', out_...  71.3 us
    pallas_call x1, Pallas kernels, attention(): pl.pallas_call(functools.partial(attention_kernel, scale, head_count, all...  19.3 us
    unnamed x28, local copies, waits for them, and re-layouts  14.6 us
  transfers between devices with their start and end apart: 3, of which 0 were waited for; matrix products, arithmetic and copies ran while one was open for 3% of the time, Pallas kernels for 74%

profile of v2, /device:TPU:1, one launch (start us, length us, event | category | flops | bytes accessed | tf_op | source)
XLA Modules:
  0.0 532.5 jit_solution(4292046713214553063)
XLA Ops:
  0.6 0.0 copy-start.8
  0.7 4.3 constant_dynamic-slice_fusion
  5.0 1.4 collective-permute-start
  6.4 1.4 collective-permute-start.1
  7.8 0.3 collective-permute-start.2
  8.0 0.0 copy-done.8
  8.1 0.1 copy.47
  8.2 0.1 div.27
  8.3 0.2 copy.45
  8.5 0.1 ne.74
  8.7 0.1 copy.46
  8.8 0.1 rem.71
  8.9 0.1 copy.48
  9.0 0.9 convert_reduce_fusion
  9.9 0.1 copy.49
  10.0 0.0 copy-start.11
  10.0 0.0 copy-start.3
  10.0 2.9 reshape.102.kv_ref
  12.9 0.0 copy-start
  12.9 0.1 select_reduce_fusion
  13.1 0.1 copy.51
  13.2 0.8 reshape.103.source_ref
  14.0 0.0 copy-done.11
  14.0 0.1 pad_add_fusion.1.place_ref
  14.1 0.0 copy-done.3
  14.1 71.3 %edges.1 = (bf16[18,64,1024]{2,1,0:T(8,128)(2,1)S(1)}, bf16[2,64,1024]{2,1,0:T(8,128)(2,1)S(1)}, bf16[2,64,512]{2,1,0:T(8,128)(2,1)S(1)}) custom-call(s32[4]{0:T(128)S(1)} %pad_add_fusion.1.place_ref, bf16[12,64,1024]{2,1,0:T(8,128)(2,1)S(1)} %reshape.102.kv_ref, bf16[12,64,512]{2,1,0:T(8,128)(2,1)S(1)} %bitcast.9), custom_call_target="tpu_custom_call" | custom-call | tf_op jit(solution)/shard_map/edges/pallas_call | solution.py:138
  85.4 0.0 copy-start.4
  85.4 1.4 copy-done.4
  86.8 0.0 copy-start.9
  86.8 0.0 copy-start.10
  86.8 1.4 far_partials.1.part_ref
  88.3 0.0 copy-done
  88.3 0.0 copy-start.2
  88.3 0.9 copy-done.2
  89.2 0.0 copy-done.9
  89.2 0.6 reshape.105.gain_ref
  89.8 0.0 copy-done.10
  89.8 0.6 reshape.106.bias_ref
  90.4 9.3 %copy.52 = bf16[512,8,2,512]{3,1,2,0:T(8,128)(2,1)} copy(bf16[512,8,2,512]{3,2,1,0:T(2,128)(2,1)} %bitcast.12) | data formatting | bytes 16777216
  99.7 0.0 copy-start.12
  99.7 0.0 copy-start.5
  99.7 302.8 %exchange.1 = (bf16[96,64,1024]{2,1,0:T(8,128)(2,1)}, bf16[32,16,128]{2,1,0:T(8,128)(2,1)}) custom-call(s32[96]{0:T(128)} %reshape.103.source_ref, bf16[12,64,1024]{2,1,0:T(8,128)(2,1)} %copy-done, f32[32,48,128]{2,1,0:T(8,128)} %copy-done.2), custom_call_target="tpu_custom_call" | custom-call | tf_op jit(solution)/shard_map/exchange/pallas_call | solution.py:307
  402.6 0.6 fusion.4
  403.2 1.3 compare_select_fusion.1
  404.4 0.0 copy-done.12
  404.4 0.1 pad_add_fusion.info_ref
  404.5 0.0 copy-done.5
  404.5 0.0 copy-start.6
  404.5 0.9 copy-done.6
  405.4 19.3 %attention.1 = bf16[12,64,512]{2,1,0:T(8,128)(2,1)S(1)} custom-call(s32[36]{0:T(128)S(1)} %fusion.2.index_ref, s32[16]{0:T(128)S(1)} %pad_add_fusion.info_ref, bf16[12,64,512]{2,1,0:T(8,128)(2,1)S(1)} %bitcast.10, bf16[18,64,1024]{2,1,0:T(8,128)(2,1)S(1)} %copy-done.5, bf16[2,64,1024]{2,1,0:T(8,128)(2,1)S(1)} %get-tuple-element.10.gkv_ref, ...), custom_call_target="tpu_custom_call" | custom-call | tf_op jit(solution)/shard_map/attention/pallas_call | solution.py:427
  424.7 0.0 copy-start.1
  424.7 0.9 copy-done.1
  425.6 0.0 collective-permute-done.w1
  425.6 0.0 collective-permute-done.1.w2
  425.6 0.0 collective-permute-done.2.w3
  425.6 101.7 %project.1 = (bf16[768,1024]{1,0:T(8,128)(2,1)}, bf16[768,1024]{1,0:T(8,128)(2,1)}) custom-call(bf16[768,512]{1,0:T(8,128)(2,1)} %bitcast.8, bf16[768,1024]{1,0:T(8,128)(2,1)} %residual_ref.1, bf16[1,1024]{1,0:T(2,128)(2,1)} %reshape.105.gain_ref, bf16[1,1024]{1,0:T(2,128)(2,1)} %reshape.106.bias_ref, bf16[512,1024]{1,0:T(8,128)(2,1)} %get-tuple-element.20.w0, ...), custom_call_target="tpu_custom_call" | custom-call | tf_op jit(solution)/shard_map/project/pallas_call | solution.py:654
  527.3 0.0 copy-start.7
  527.3 4.0 reshape.108
  531.3 0.0 copy-done.7
  531.3 1.1 copy.54
  (7 shorter events, 0.1 us)
Async XLA Ops:
  0.6 7.4 %copy-start.8 = (s32[384,3]{0,1:T(4,128)S(1)}, s32[384,3]{0,1:T(4,128)}, u32[]{:S(2)}) copy-start(s32[384,3]{0,1:T(4,128)} %param.19) | copy-start | bytes 13828
  5.0 420.6 %collective-permute-start = (bf16[512,1024]{1,0:T(8,128)(2,1)}, bf16[512,1024]{1,0:T(8,128)(2,1)}, u32[]{:S(2)}, u32[]{:S(2)}) collective-permute-start(bf16[512,1024]{1,0:T(8,128)(2,1)} %get-tuple-element.19), channel_id=1, source_target_pairs={{0,1},{1,0},{2,3},{3,2},{4,5},{5,4},{6,7},{7,6},{8,9},{9,8},{10,11... | collective-permute-start | bytes 3145736 | tf_op jit(solution)/shard_map/ppermute | solution.py:743
  6.4 419.2 %collective-permute-start.1 = (bf16[512,1024]{1,0:T(8,128)(2,1)}, bf16[512,1024]{1,0:T(8,128)(2,1)}, u32[]{:S(2)}, u32[]{:S(2)}) collective-permute-start(bf16[512,1024]{1,0:T(8,128)(2,1)} %get-tuple-element.21), channel_id=1, source_target_pairs={{0,2},{1,3},{2,0},{3,1},{4,6},{5,7},{6,4},{7,5},{8,10},{9,11},{10,... | collective-permute-start | bytes 3145736 | tf_op jit(solution)/shard_map/ppermute | solution.py:743
  7.8 417.9 %collective-permute-start.2 = (bf16[512,1024]{1,0:T(8,128)(2,1)}, bf16[512,1024]{1,0:T(8,128)(2,1)}, u32[]{:S(2)}, u32[]{:S(2)}) collective-permute-start(bf16[512,1024]{1,0:T(8,128)(2,1)} %get-tuple-element.18), channel_id=1, source_target_pairs={{0,3},{1,2},{2,1},{3,0},{4,7},{5,6},{6,5},{7,4},{8,11},{9,10},{10,... | collective-permute-start | bytes 3145736 | tf_op jit(solution)/shard_map/ppermute | solution.py:743
  10.0 4.0 copy-start.11
  10.0 4.1 copy-start.3
  12.9 75.4 %copy-start = (bf16[12,64,1024]{2,1,0:T(8,128)(2,1)}, bf16[12,64,1024]{2,1,0:T(8,128)(2,1)S(1)}, u32[]{:S(2)}) copy-start(bf16[12,64,1024]{2,1,0:T(8,128)(2,1)S(1)} %reshape.102.kv_ref) | copy-start | bytes 4718596
  85.4 1.5 copy-start.4
  86.8 2.4 copy-start.9
  86.8 3.0 copy-start.10
  88.3 0.9 copy-start.2
  99.7 304.7 %copy-start.12 = (s32[4]{0:T(128)S(1)}, s32[4]{0:T(128)}, u32[]{:S(2)}) copy-start(s32[4]{0:T(128)} %param.17) | copy-start | bytes 52
  99.7 304.8 %copy-start.5 = (bf16[18,64,1024]{2,1,0:T(8,128)(2,1)S(1)}, bf16[18,64,1024]{2,1,0:T(8,128)(2,1)}, u32[]{:S(2)}) copy-start(bf16[18,64,1024]{2,1,0:T(8,128)(2,1)} %copy-done.4) | copy-start | bytes 7077892
  404.5 0.9 copy-start.6
  424.7 0.9 copy-start.1
  527.3 4.0 copy-start.7

commit v3 on v2

--- a/solution.py
+++ b/solution.py
@@ -479,7 +479,8 @@
     rows = att_ref.shape[0] // chunks
     cols = residual_ref.shape[1]
 
-    for k, w in enumerate((w0, w1, w2, w3)):
+    own_cols = w0.at[:, pl.ds(pl.multiple_of(tp * residual_ref.shape[1], residual_ref.shape[1]), residual_ref.shape[1])]
+    for k, w in enumerate((own_cols, w1, w2, w3)):
         pltpu.make_async_copy(w, w_all.at[k], w_sem.at[k]).start()
     for k, block in enumerate((tp, mate, over, cater)):
         pltpu.make_async_copy(
@@ -536,7 +537,7 @@
         return carry
 
     lax.fori_loop(0, chunks, begin, 0)
-    for k, w in enumerate((w0, w1, w2, w3)):
+    for k, w in enumerate((own_cols, w1, w2, w3)):
         pltpu.make_async_copy(w, w_all.at[k], w_sem.at[k]).wait()
 
     def step(t, carry):
@@ -644,7 +645,7 @@
 CHUNKS = 6
 
 
-def project(att, residual, gain, bias, weights, cross_weight, ctx_count, tp_count):
+def project(att, residual, gain, bias, out_weight, weights, cross_weight, ctx_count, tp_count):
     rows, depth = att.shape
     cols = residual.shape[1]
     wide = cross_weight.shape[1]
@@ -680,7 +681,494 @@
         compiler_params=pltpu.CompilerParams(
             collective_id=2, has_side_effects=True, vmem_limit_bytes=60 * 2**20
         ),
-    )(att, residual, gain, bias, *weights, cross_weight)
+    )(att, residual, gain, bias, out_weight, *weights, cross_weight)
+
+
+FIRST = 16
+SECOND = 12
+LINE = 4
+HEAD_COLS = 128
+
+
+def front_kernel(
+    count,
+    scale,
+    list_ref,
+    kv_ref,
+    q_ref,
+    weight_ref,
+    out_ref,
+    w1_ref,
+    w2_ref,
+    w3_ref,
+    ext,
+    cand,
+    got,
+    full,
+    gkv,
+    gq,
+    part,
+    far_got,
+    far,
+    pool0,
+    pool1,
+    pool2,
+    pool3,
+    hold0,
+    hold1,
+    hold2,
+    hold3,
+    last0,
+    last1,
+    last2,
+    last3,
+    stage1,
+    stage2,
+    pair_send,
+    pair_recv,
+    halo_send,
+    halo_recv,
+    weight_send,
+    weight_recv,
+    small_send,
+    small_recv,
+    bulk_send,
+    bulk_recv,
+):
+    me = lax.axis_index("ctx")
+    tp = lax.axis_index("tp")
+    heads, blocks, rows, pair = kv_ref.shape
+    size = pair // 2
+    spot = (me // 8, lax.rem(me // 2, LINE))
+    level = lax.rem(me, 2)
+    twin = me + 1 - 2 * level
+    mates = (tp + 1 - 2 * lax.rem(tp, 2), lax.rem(tp + 2, 4), 3 - tp)
+    pools = (pool0, pool1, pool2, pool3)
+    holds = (hold0, hold1, hold2, hold3)
+    lasts = (last0, last1, last2, last3)
+    wcols = w1_ref.shape[1]
+    near = SPAN * rows
+
+    barrier = pltpu.get_barrier_semaphore()
+
+    def greeting(k, carry):
+        pl.semaphore_signal(
+            barrier, inc=1, device_id={"ctx": lax.rem(me + k, count)}, device_id_type=MESH
+        )
+        return carry
+
+    lax.fori_loop(1, count, greeting, 0)
+    for other in mates:
+        pl.semaphore_signal(barrier, inc=1, device_id={"tp": other}, device_id_type=MESH)
+
+    def base(c):
+        return 20 + (c % 2) * (LINE * FIRST + LINE * SECOND + blocks * R)
+
+    def along(c, stage, d):
+        x, z = spot
+        if (c + stage) % 2 == 0:
+            x = lax.rem(x + d, LINE)
+            return x, x * 8 + z * 2 + level
+        z = lax.rem(z + d, LINE)
+        return z, x * 8 + z * 2 + level
+
+    def pair_copy(c):
+        return pltpu.make_async_remote_copy(
+            src_ref=kv_ref.at[c],
+            dst_ref=pools[c].at[pl.ds(level * blocks, blocks)],
+            send_sem=pair_send.at[c],
+            recv_sem=pair_recv.at[c],
+            device_id={"ctx": twin},
+            device_id_type=MESH,
+        )
+
+    def halo_copy(k):
+        src, dst, to = (
+            (blocks - MAXR, 0, lax.rem(me + 1, count)),
+            (0, blocks + MAXR, lax.rem(me + count - 1, count)),
+        )[k]
+        return pltpu.make_async_remote_copy(
+            src_ref=kv_ref.at[:, pl.ds(src, MAXR)],
+            dst_ref=ext.at[:, pl.ds(dst, MAXR)],
+            send_sem=halo_send.at[k],
+            recv_sem=halo_recv.at[k],
+            device_id={"ctx": to},
+            device_id_type=MESH,
+        )
+
+    def weight_copy(k):
+        other = mates[k]
+        return pltpu.make_async_remote_copy(
+            src_ref=weight_ref.at[:, pl.ds(pl.multiple_of(other * wcols, wcols), wcols)],
+            dst_ref=(w1_ref, w2_ref, w3_ref)[k],
+            send_sem=weight_send.at[k],
+            recv_sem=weight_recv.at[k],
+            device_id={"tp": other},
+            device_id_type=MESH,
+        )
+
+    def small(kind, k, scattered, src, dst):
+        to = lax.rem(me + k, count)
+        return pltpu.make_async_remote_copy(
+            src_ref=src.at[to if scattered else me],
+            dst_ref=dst.at[me],
+            send_sem=small_send.at[kind, k],
+            recv_sem=small_recv.at[kind, k],
+            device_id={"ctx": to},
+            device_id_type=MESH,
+        )
+
+    def bulk(c, stage, d):
+        slots = (FIRST, SECOND)[stage]
+        mine = spot[(c + stage) % 2]
+        buffer = (stage1, stage2)[stage]
+        return pltpu.make_async_remote_copy(
+            src_ref=buffer.at[c, pl.ds((d - 1) * slots, slots)],
+            dst_ref=(holds, lasts)[stage][c].at[pl.ds(mine * slots, slots)],
+            send_sem=bulk_send.at[stage, c, d - 1],
+            recv_sem=bulk_recv.at[stage, c, d - 1],
+            device_id={"ctx": along(c, stage, d)[1]},
+            device_id_type=MESH,
+        )
+
+    def each(action):
+        def body(k, carry):
+            action(k)
+            return carry
+
+        lax.fori_loop(1, count, body, 0)
+
+    for g in range(G):
+        local = list_ref[G + g]
+        row = jnp.concatenate([kv_ref[c, local] for c in range(heads)] + [q_ref[local]], axis=1)
+        cut = row.shape[1] // 4
+        for r in range(4):
+            for s in range(4):
+                cand[(g * 4 + r) * 4 + s] = row[r * 16 : r * 16 + 16, s * cut : (s + 1) * cut]
+    for c in range(heads):
+        pools[c][pl.ds(level * blocks, blocks)] = kv_ref[c]
+        ext[c, pl.ds(MAXR, blocks)] = kv_ref[c]
+    pl.semaphore_wait(barrier, count - 1 + 3)
+
+    each(lambda k: small(0, k, True, cand, got).start())
+    for c in range(heads):
+        pair_copy(c).start()
+    for k in range(2):
+        halo_copy(k).start()
+    got[me] = cand[me]
+    each(lambda k: small(0, k, True, cand, got).wait())
+    full[me] = got[list_ref[me // (count // G)]]
+    each(lambda k: small(1, k, False, full, full).start())
+
+    for c in range(heads):
+        pair_copy(c).wait()
+        for d in range(1, LINE):
+            target, _ = along(c, 0, d)
+
+            def fill(j, carry):
+                source = list_ref[base(c) + target * FIRST + j]
+                stage1[c, (d - 1) * FIRST + j] = pools[c][source]
+                return carry
+
+            lax.fori_loop(0, FIRST, fill, 0)
+        for d in (1, 3, 2):
+            bulk(c, 0, d).start()
+
+    each(lambda k: small(1, k, False, full, full).wait())
+    for g in range(G):
+        for r in range(4):
+            row = jnp.concatenate([full[(g * 4 + r) * 4 + s] for s in range(4)], axis=1)
+            gkv[g, r * 16 : r * 16 + 16, :] = row[:, : heads * pair]
+            gq[g, r * 16 : r * 16 + 16, :] = row[:, heads * pair :]
+
+    for h in range(heads):
+        gq_h = gq[:, :, h * size : (h + 1) * size].reshape(G * rows, size)
+        k_h = kv_ref[h, :, :, 0:size].reshape(blocks * rows, size)
+        v_h = kv_ref[h, :, :, size:pair].reshape(blocks * rows, size)
+        s = (
+            lax.dot_general(gq_h, k_h, (((1,), (1,)), ((), ())), preferred_element_type=jnp.float32)
+            * scale
+        )
+        peak = jnp.max(s, axis=1, keepdims=True)
+        p = jnp.exp(s - peak)
+        total = jnp.sum(p, axis=1, keepdims=True)
+        acc = jnp.dot(p.astype(jnp.bfloat16), v_h, preferred_element_type=jnp.float32)
+        peak = jnp.broadcast_to(peak, acc.shape)
+        total = jnp.broadcast_to(total, acc.shape)
+        for r in range(8):
+            cut = slice(r * 16, r * 16 + 16)
+            part[h * 8 + r, 0:16, :] = acc[cut]
+            part[h * 8 + r, 16:32, :] = peak[cut]
+            part[h * 8 + r, 32:48, :] = total[cut]
+    far_got[me] = part[me]
+    for k in range(3):
+        weight_copy(k).start()
+    each(lambda k: small(2, k, True, part, far_got).start())
+
+    held = 2 * blocks
+    ended = held + LINE * FIRST
+
+    for c in range(heads):
+        for d in range(1, LINE):
+            bulk(c, 0, d).wait()
+        for d in range(1, LINE):
+            target, _ = along(c, 1, d)
+
+            def fill(j, carry):
+                source = list_ref[base(c) + LINE * FIRST + target * SECOND + j]
+                stage2[c, (d - 1) * SECOND + j] = jnp.where(
+                    source < held,
+                    pools[c][jnp.minimum(source, held - 1)],
+                    holds[c][jnp.maximum(source - held, 0)],
+                )
+                return carry
+
+            lax.fori_loop(0, SECOND, fill, 0)
+        for d in (1, 3, 2):
+            bulk(c, 1, d).start()
+
+    each(lambda k: small(2, k, True, part, far_got).wait())
+
+    def top(i, so_far):
+        return jnp.maximum(so_far, far_got[i, 16:32, :])
+
+    far_peak = lax.fori_loop(1, count, top, far_got[0, 16:32, :])
+
+    def add(i, so_far):
+        acc, total = so_far
+        factor = jnp.exp(far_got[i, 16:32, :] - far_peak)
+        return acc + far_got[i, 0:16, :] * factor, total + far_got[i, 32:48, :] * factor
+
+    zero = jnp.zeros_like(far_peak)
+    far_acc, far_total = lax.fori_loop(0, count, add, (zero, zero))
+    far[me] = (far_acc / far_total).astype(far.dtype)
+    each(lambda k: small(3, k, False, far, far).start())
+
+    for k in range(2):
+        halo_copy(k).wait()
+
+    place = lax.broadcasted_iota(jnp.int32, (rows, near), 1) // rows - MAXR
+    for c in range(heads):
+        for d in range(1, LINE):
+            bulk(c, 1, d).wait()
+        lanes = slice(c * size, (c + 1) * size)
+        reach = list_ref[2 * G + c]
+        allowed = jnp.abs(place) <= reach
+        g_k = gkv[:, :, c * pair : c * pair + size].reshape(G * rows, size)
+        g_v = gkv[:, :, c * pair + size : (c + 1) * pair].reshape(G * rows, size)
+
+        def attend(b, carry):
+            block = me * blocks + b
+            inside = (place + block >= 0) & (place + block < count * blocks)
+            q = q_ref[b, :, lanes]
+            picked = []
+            for r in range(R):
+                at = list_ref[base(c) + LINE * (FIRST + SECOND) + b * R + r]
+                picked.append(
+                    jnp.where(
+                        at < held,
+                        pools[c][jnp.minimum(at, held - 1)],
+                        jnp.where(
+                            at < ended,
+                            holds[c][jnp.clip(at - held, 0, LINE * FIRST - 1)],
+                            lasts[c][jnp.maximum(at - ended, 0)],
+                        ),
+                    )
+                )
+
+            def score(keys):
+                return (
+                    lax.dot_general(
+                        q, keys, (((1,), (1,)), ((), ())), preferred_element_type=jnp.float32
+                    )
+                    * scale
+                )
+
+            window = ext[c, pl.ds(b, SPAN)].reshape(near, pair)
+            s1 = jnp.where(inside & allowed, score(window[:, :size]), -jnp.inf)
+            s2 = score(jnp.concatenate([g_k] + [x[:, :size] for x in picked], axis=0))
+            peak = jnp.maximum(
+                jnp.max(s1, axis=1, keepdims=True), jnp.max(s2, axis=1, keepdims=True)
+            )
+            p1 = jnp.exp(s1 - peak)
+            p2 = jnp.exp(s2 - peak)
+            total = jnp.sum(p1, axis=1, keepdims=True) + jnp.sum(p2, axis=1, keepdims=True)
+            acc = jnp.dot(
+                p1.astype(jnp.bfloat16), window[:, size:], preferred_element_type=jnp.float32
+            ) + jnp.dot(
+                p2.astype(jnp.bfloat16),
+                jnp.concatenate([g_v] + [x[:, size:] for x in picked], axis=0),
+                preferred_element_type=jnp.float32,
+            )
+            out_ref[b, :, lanes] = (acc / total).astype(out_ref.dtype)
+            return carry
+
+        lax.fori_loop(0, blocks, attend, 0)
+
+    each(lambda k: small(3, k, False, far, far).wait())
+    swap = []
+    for g in range(G):
+        swap.append(
+            jnp.concatenate(
+                [
+                    jnp.concatenate([far[h * 8 + g * 4 + r] for r in range(4)], axis=0)
+                    for h in range(heads)
+                ],
+                axis=1,
+            )
+        )
+
+    def replace(b, carry):
+        which = list_ref[2 * G + heads + b]
+        out_ref[b] = jnp.where(which == 0, swap[0], jnp.where(which == 1, swap[1], out_ref[b]))
+        return carry
+
+    lax.fori_loop(0, blocks, replace, 0)
+    for k in range(3):
+        weight_copy(k).wait()
+
+
+def front(lists, kv, q, weight, scale, count, tp_count):
+    heads, blocks, rows, pair = kv.shape
+    size = pair // 2
+    kept = kv.dtype
+    vmem = pl.BlockSpec(memory_space=VMEM)
+    hbm = pl.BlockSpec(memory_space=pl.ANY)
+    cols = weight.shape[1] // tp_count
+    moved = jax.ShapeDtypeStruct((weight.shape[0], cols), kept)
+    cut = (heads * pair + heads * size) // 4
+    dma = pltpu.SemaphoreType.DMA
+    return pl.pallas_call(
+        functools.partial(front_kernel, count, scale),
+        name="front",
+        out_shape=(jax.ShapeDtypeStruct(q.shape, kept), moved, moved, moved),
+        in_specs=[pl.BlockSpec(memory_space=SMEM), vmem, vmem, hbm],
+        out_specs=(vmem, hbm, hbm, hbm),
+        scratch_shapes=[
+            VMEM((heads, blocks + 2 * MAXR, rows, pair), kept),
+            VMEM((count, 16, cut), kept),
+            VMEM((count, 16, cut), kept),
+            VMEM((count, 16, cut), kept),
+            VMEM((G, rows, heads * pair), kept),
+            VMEM((G, rows, heads * size), kept),
+            VMEM((count, 48, size), jnp.float32),
+            VMEM((count, 48, size), jnp.float32),
+            VMEM((count, 16, size), kept),
+        ]
+        + [VMEM((2 * blocks, rows, pair), kept)] * heads
+        + [VMEM((LINE * FIRST, rows, pair), kept)] * heads
+        + [VMEM((LINE * SECOND, rows, pair), kept)] * heads
+        + [
+            VMEM((heads, (LINE - 1) * FIRST, rows, pair), kept),
+            VMEM((heads, (LINE - 1) * SECOND, rows, pair), kept),
+            dma((heads,)),
+            dma((heads,)),
+            dma((2,)),
+            dma((2,)),
+            dma((3,)),
+            dma((3,)),
+            dma((4, count)),
+            dma((4, count)),
+            dma((2, heads, LINE - 1)),
+            dma((2, heads, LINE - 1)),
+        ],
+        compiler_params=pltpu.CompilerParams(
+            collective_id=3, has_side_effects=True, vmem_limit_bytes=60 * 2**20
+        ),
+    )(lists, kv, q, weight)
+
+
+def exclusive(flags):
+    ones = flags.astype(jnp.int32)
+    return jnp.cumsum(ones, axis=-1) - ones
+
+
+def listing(flags, ranks, values, slots):
+    wanted = jnp.arange(slots, dtype=jnp.int32)[:, None]
+    hit = flags[..., None, :] & (ranks[..., None, :] == wanted)
+    return jnp.sum(jnp.where(hit, values, 0), axis=-1)
+
+
+def route(asked, first, second, entries):
+    many = asked.shape[-1]
+    ids = jnp.arange(many, dtype=jnp.int32)
+    line = jnp.arange(LINE, dtype=jnp.int32)
+    need = jnp.any(asked, axis=1)
+    rank = exclusive(need)
+    mine = need[:, first, second]
+    list1 = listing(mine, rank[:, first, second], ids, FIRST)
+    held = many + line[:, None, None] * FIRST + jnp.minimum(rank[first], FIRST - 1)
+    where = jnp.where(line[:, None, None] == first, ids, held)
+    here = asked[first]
+    wanted = here[:, :, second].reshape(LINE, LINE * many)
+    list2 = listing(wanted, exclusive(wanted), where[:, second].reshape(-1), SECOND)
+    own = jnp.swapaxes(here[second], 0, 1).reshape(LINE, LINE * many)
+    ended = (
+        many
+        + LINE * FIRST
+        + line[:, None] * SECOND
+        + jnp.minimum(exclusive(own), SECOND - 1)
+    )
+    ended = jnp.swapaxes(ended.reshape(LINE, LINE, many), 0, 1)
+    final = jnp.where(line[None, :, None] == second, where, ended)
+    return list1.reshape(-1), list2.reshape(-1), final
+
+
+def plan(random_blocks, block_count, ctx_count, me):
+    req_count = block_count * R
+    all_blocks = block_count * ctx_count
+    requests = random_blocks.reshape(ctx_count, req_count)
+    asked = jnp.any(
+        requests[:, :, None] == jnp.arange(all_blocks, dtype=jnp.int32)[None, None, :], axis=1
+    )
+    asked = asked.reshape(LINE, LINE, 2, LINE, LINE, 2 * block_count)
+    line = jnp.arange(LINE, dtype=jnp.int32)
+    apart = line[:, None] != line[None, :]
+    ones = asked.astype(jnp.int32)
+
+    def most(counts, mask):
+        return jnp.max(jnp.where(mask, counts, 0))
+
+    first_x = most(jnp.sum(jnp.max(ones, axis=1), axis=-1), apart[:, None, :, None])
+    first_z = most(jnp.sum(jnp.max(ones, axis=0), axis=-1), apart[:, None, None, :])
+    second_z = most(jnp.sum(ones, axis=(3, 5)), apart[None, :, None, :])
+    second_x = most(jnp.sum(ones, axis=(4, 5)), apart[:, None, None, :])
+    fits = (jnp.maximum(first_x, first_z) <= FIRST) & (jnp.maximum(second_x, second_z) <= SECOND)
+    x, z, level = me // 8, me // 2 % LINE, me % 2
+    flat = asked[:, :, level]
+    mine = requests[me]
+    picked = mine[:, None] == jnp.arange(all_blocks, dtype=jnp.int32)[None, :]
+    lists = []
+    for turned in (False, True):
+        if turned:
+            a, b, final = route(jnp.transpose(flat, (1, 0, 3, 2, 4)), z, x, mine)
+            final = jnp.swapaxes(final, 0, 1)
+        else:
+            a, b, final = route(flat, x, z, mine)
+        lists += [a, b, jnp.sum(jnp.where(picked, final.reshape(-1)[None, :], 0), axis=1)]
+    return fits, lists
+
+
+def direct(place, info, source_ids, my_index, kv_heads, q, out_weight, scale, count, slots):
+    heads, block_count, rows, pair = kv_heads.shape
+    kv = jnp.transpose(
+        kv_heads.reshape(heads, block_count, rows, 2, pair // 2), (1, 2, 3, 0, 4)
+    ).reshape(block_count, rows, heads * pair)
+    ext, gkv, gq = edges(place, kv, q, count)
+    partials = far_partials(gq, kv, scale, heads, count)
+    random, far = exchange(source_ids, kv, partials, count, slots)
+    attended = attention(
+        my_index, info, q, ext, gkv, far, random, scale, heads, count * block_count
+    )
+    tp = lax.axis_index("tp")
+    tp_count = lax.axis_size("tp")
+    cols = out_weight.shape[1] // tp_count
+    mates = (tp, tp + 1 - 2 * lax.rem(tp, 2), lax.rem(tp + 2, tp_count), tp_count - 1 - tp)
+    weights = []
+    for k in range(1, tp_count):
+        block = lax.dynamic_slice_in_dim(out_weight, mates[k] * cols, cols, axis=1)
+        weights.append(lax.ppermute(block, "tp", [(i, i ^ k) for i in range(tp_count)]))
+    return (attended, *weights)
 
 
 def shards(
@@ -699,54 +1187,56 @@
     head_count = window_reach.shape[0]
     head_size = head_cols // head_count
     ctx_count = lax.axis_size("ctx")
+    tp_count = lax.axis_size("tp")
     me = lax.axis_index("ctx")
     block_count = tok_rows // BLOCK
-    all_blocks = block_count * ctx_count
     scale = 1.0 / math.sqrt(head_size)
     q = queries.reshape(block_count, BLOCK, head_cols)
-    kv = keyvals.reshape(block_count, BLOCK, 2 * head_cols)
-
-    req_count = block_count * R
-    slots = 1 + (req_count + ctx_count - 2) // ctx_count
-    requests = random_blocks.reshape(ctx_count, req_count)
-    owners = requests // block_count
-    local_ids = requests % block_count
-    positions = jnp.arange(req_count, dtype=jnp.int32)
-    earlier = positions[None, :] < positions[:, None]
-    ranks = jnp.sum(
-        ((owners[:, :, None] == owners[:, None, :]) & earlier[None, :, :]).astype(jnp.int32), axis=2
-    )
-    slot_ids = jnp.arange(slots, dtype=jnp.int32)
-    matches = (owners[:, None, :] == me) & (ranks[:, None, :] == slot_ids[None, :, None])
-    source_ids = jnp.sum(jnp.where(matches, local_ids[:, None, :], 0), axis=2).reshape(-1)
-    my_index = lax.dynamic_index_in_dim(owners * slots + ranks, me, 0, keepdims=False)
+    kv_heads = jnp.transpose(
+        keyvals.reshape(block_count, BLOCK, 2, head_count, head_size), (3, 0, 1, 2, 4)
+    ).reshape(head_count, block_count, BLOCK, 2 * head_size)
+
     place = jnp.concatenate([global_blocks // block_count, global_blocks % block_count])
     own_ids = me * block_count + jnp.arange(block_count, dtype=jnp.int32)
     replaced = jnp.where(
         own_ids == global_blocks[0], 0, jnp.where(own_ids == global_blocks[1], 1, -1)
     )
     info = jnp.concatenate([window_reach, replaced])
-
-    ext, gkv, gq = edges(place, kv, q, ctx_count)
-    partials = far_partials(gq, kv, scale, head_count, ctx_count)
-    random, far = exchange(source_ids, kv, partials, ctx_count, slots)
-    attended = attention(my_index, info, q, ext, gkv, far, random, scale, head_count, all_blocks)
+    fits, lists = plan(random_blocks, block_count, ctx_count, me)
+    lists = jnp.concatenate([place, info] + lists)
+
+    def staged(kv_heads, q, out_weight):
+        return tuple(front(lists, kv_heads, q, out_weight, scale, ctx_count, tp_count))
+
+    def plain(kv_heads, q, out_weight):
+        req_count = block_count * R
+        slots = 1 + (req_count + ctx_count - 2) // ctx_count
+        requests = random_blocks.reshape(ctx_count, req_count)
+        owners = requests // block_count
+        local_ids = requests % block_count
+        positions = jnp.arange(req_count, dtype=jnp.int32)
+        earlier = positions[None, :] < positions[:, None]
+        ranks = jnp.sum(
+            ((owners[:, :, None] == owners[:, None, :]) & earlier[None, :, :]).astype(jnp.int32),
+            axis=2,
+        )
+        slot_ids = jnp.arange(slots, dtype=jnp.int32)
+        matches = (owners[:, None, :] == me) & (ranks[:, None, :] == slot_ids[None, :, None])
+        source_ids = jnp.sum(jnp.where(matches, local_ids[:, None, :], 0), axis=2).reshape(-1)
+        my_index = lax.dynamic_index_in_dim(owners * slots + ranks, me, 0, keepdims=False)
+        return direct(
+            place, info, source_ids, my_index, kv_heads, q, out_weight, scale, ctx_count, slots
+        )
+
+    attended, *weights = lax.cond(fits, staged, plain, kv_heads, q, out_weight)
     attended = attended.reshape(tok_rows, head_cols)
-    tp = lax.axis_index("tp")
-    tp_count = lax.axis_size("tp")
     cols = residual.shape[1]
-    mates = (tp, tp + 1 - 2 * lax.rem(tp, 2), lax.rem(tp + 2, tp_count), tp_count - 1 - tp)
-    weights = []
-    for k in range(tp_count):
-        block = lax.dynamic_slice_in_dim(out_weight, mates[k] * cols, cols, axis=1)
-        if k > 0:
-            block = lax.ppermute(block, "tp", [(i, i ^ k) for i in range(tp_count)])
-        weights.append(block)
     encoded, cross_kv = project(
         attended,
         residual,
         norm_gain.reshape(1, cols),
         norm_bias.reshape(1, cols),
+        out_weight,
         weights,
         cross_weight.reshape(D, 2 * head_cols),
         ctx_count,

time: 533 us -> 284 us (0.53)
  Pallas kernels: 497 us -> 232 us
  other arithmetic: 2.5 us -> 17 us
    pallas_call x4 -> x1, Pallas kernels: 395 us -> 157 us  [front(): pl.pallas_call(functools.partial(front_kernel, count, scale), name='front...]
    pallas_call x1, Pallas kernels: 102 us -> 75.4 us  [project(): pl.pallas_call(functools.partial(project_kernel, ctx_count, tp_count, CHU...]
    another operation x0 -> x6, other arithmetic: none -> 7.36 us  [exclusive(): return jnp.cumsum(ones, axis=-1) - ones]
    unnamed x28 -> x17, local copies, waits for them, and re-layouts: 14.6 us -> 11.3 us
  transfers between devices with their start and end apart: 3 -> 0, of which waited for: 0 -> 0; matrix products, arithmetic and copies ran while one was open for 3% -> 0% of each run, Pallas kernels for 74% -> 0%
where the time goes in v3:
time: 284 us
  Pallas kernels  232 us (82%)
  local copies, waits for them, and re-layouts  30.5 us (11%)
  other arithmetic  17 us (6%)
  between operations  3.65 us (1%)
    pallas_call x1, Pallas kernels, front(): pl.pallas_call(functools.partial(front_kernel, count, scale), name='front...  157 us
    pallas_call x1, Pallas kernels, project(): pl.pallas_call(functools.partial(project_kernel, ctx_count, tp_count, CHU...  75.4 us
    unnamed x17, local copies, waits for them, and re-layouts  11.3 us
    another operation x6, other arithmetic, exclusive(): return jnp.cumsum(ones, axis=-1) - ones  7.36 us

profile of v3, /device:TPU:1, one launch (start us, length us, event | category | flops | bytes accessed | tf_op | source)
XLA Modules:
  0.0 283.8 jit_solution(8884186011937279988)
XLA Ops:
  0.7 0.8 copy.123
  1.5 0.1 eq.178
  1.7 0.1 copy.124
  1.7 0.3 fusion.4
  2.0 0.2 reshape.289
  2.3 0.1 and.128
  2.4 0.3 reduce_window_sum.55
  2.7 0.1 reshape.301
  2.8 0.3 reduce_window_sum.56
  3.0 0.1 reduce_window_sum.57
  3.1 0.1 reshape.300
  3.2 0.3 reduce_window_sum.52
  3.5 0.1 reduce_window_sum.53
  3.6 0.1 dynamic-slice_reduce_fusion
  3.7 3.1 %reduce_window_sum.54 = s32[4,4,4,24]{3,2,1,0:T(4,128)S(1)} reduce-window(s32[4,4,4,24]{3,2,1,0:T(4,128)S(1)} %convert_bitcast_fusion, s32[]{:T(128)} %constant.307.clone.1), window={size=1x1x1x24 pad=0_0x0_0x0_0x23_0}, to_apply=%region_19.20 | reduce-window | flops 35328 | bytes 12292 | tf_op jit(solution)/shard_map/jit(cumsum)/reduce_window_sum | solution.py:1083
  6.8 0.1 fusion.10
  6.9 3.1 %reduce_window_sum.42 = s32[4,4,4,24]{3,2,1,0:T(4,128)S(1)} reduce-window(s32[4,4,4,24]{3,2,1,0:T(4,128)S(1)} %convert_element_type.80, s32[]{:T(128)} %constant.307.clone.1), window={size=1x1x1x24 pad=0_0x0_0x0_0x23_0}, to_apply=%region_12.13 | reduce-window | flops 35328 | bytes 12292 | tf_op jit(solution)/shard_map/jit(cumsum)/reduce_window_sum | solution.py:1083
  10.1 0.1 bitcast_select_fusion.1
  10.2 0.1 reshape_squeeze.9
  10.3 0.3 select_reduce_fusion.5
  10.5 0.1 copy.132
  10.6 0.1 reshape.295
  10.8 0.1 select_reduce_fusion.3
  10.9 0.1 reshape.294
  11.0 0.1 broadcast_in_dim.190
  11.1 0.1 broadcast_in_dim.198
  11.2 0.2 select_reduce_fusion.1
  11.5 0.1 and.122
  11.6 0.3 reduce_window_sum.43
  11.9 0.1 reshape_squeeze.8
  11.9 0.3 select_reduce_fusion.6
  12.2 0.1 copy.128
  12.3 0.1 reshape.293
  12.4 0.2 select_reduce_fusion.4
  12.6 0.1 reshape.292
  12.7 1.3 fusion.22
  14.0 1.3 compare_select_fusion.1
  15.3 0.7 and_select_fusion.1
  15.9 0.7 concatenate.12
  16.7 2.8 reshape.308
  19.5 0.0 copy-start.10
  19.5 0.0 copy-start.5
  19.5 0.0 copy-start.7
  19.5 2.0 copy.169
  21.5 3.0 %convert_reduce_fusion.1 = (s32[4,4,2,4]{3,2,1,0:T(2,128)S(1)}, s32[4,2,4,4,24]{4,3,2,1,0:T(4,128)S(1)}, s32[4,4,2,4]{3,2,1,0:T(2,128)S(1)}, s32[4,2,4,4,24]{4,3,2,1,0:T(4,128)S(1)}) fusion(pred[4,4,2,4,4,24]{5,4,3,2,1,0:T(4,128)(4,1)S(1)} %reshape.289), kind=kLoop, calls=%fused_computation.23 | loop fusion | flops 55040 | bytes 37888 | tf_op jit(solution)/shard_map/reduce_sum | solution.py:1134
  24.5 0.7 select_reduce_fusion.7
  26.6 0.6 reduce_sum.108
  27.2 0.6 reduce_sum.109
  27.8 0.8 select_reduce_fusion.9
  30.0 0.1 pad_add_fusion.1
  30.1 0.1 pad_add_fusion
  30.2 0.0 copy-done.7
  30.2 162.5 %conditional.1 = (bf16[512,1024]{1,0:T(8,128)(2,1)}, bf16[512,1024]{1,0:T(8,128)(2,1)}, bf16[512,1024]{1,0:T(8,128)(2,1)}, bf16[768,512]{1,0:T(8,128)(2,1)}) conditional(s32[]{:T(128)} %convert_element_type.79, (bf16[512,4096]{1,0:T(8,128)(2,1)}, s32[384,3]{0,1:T(4,128)S(1)}, s32[]{:T(128)}, bf16[768,2,512]{2,1,0:T(2,128)(2,1)}, s32[4]{0:T(128)S(1)}, ...), branch_computations={%region_25.28_spmd, %region_28.29_spmd} | conditional | flops 195994 | bytes 50979072 | solution.py:1231
  30.3 3.0 %copy.137 = bf16[4,12,64,2,128]{4,3,2,1,0:T(2,128)(2,1)S(1)} copy(bf16[4,12,64,2,128]{4,0,2,1,3:T(4,128)(2,1)} %get-tuple-element.142) | data formatting | bytes 3145728 | tf_op jit(solution)/shard_map
  33.4 2.3 reshape.276.kv_ref
  35.7 157.0 %front.1 = (bf16[12,64,512]{2,1,0:T(8,128)(2,1)}, bf16[512,1024]{1,0:T(8,128)(2,1)}, bf16[512,1024]{1,0:T(8,128)(2,1)}, bf16[512,1024]{1,0:T(8,128)(2,1)}) custom-call(s32[316]{0:T(512)S(1)} %get-tuple-element.40.list_ref, bf16[4,12,64,256]{3,2,1,0:T(8,128)(2,1)} %reshape.276.kv_ref, bf16[12,64,512]{2,1,0:T(8,128)(2,1)S(1)} %get-tuple-element.42.q_ref, ...), custom_call_target="tpu_custom_call" | custom-call | tf_op jit(solution)/shard_map/cond/branch_1_fun/front/pallas_call | solution.py:1041
  192.6 0.0 copy-start.8
  192.7 0.0 copy-start.9
  192.7 9.3 %copy.144 = bf16[512,8,2,512]{3,1,2,0:T(8,128)(2,1)} copy(bf16[512,8,2,512]{3,2,1,0:T(2,128)(2,1)} %bitcast.64) | data formatting | bytes 16777216
  202.0 0.6 reshape.296.gain_ref
  202.6 0.6 reshape.297.bias_ref
  203.2 75.4 %project.1 = (bf16[768,1024]{1,0:T(8,128)(2,1)}, bf16[768,1024]{1,0:T(8,128)(2,1)}) custom-call(bf16[768,512]{1,0:T(8,128)(2,1)} %get-tuple-element.56.att_ref, bf16[768,1024]{1,0:T(8,128)(2,1)} %residual_ref.1, bf16[1,1024]{1,0:T(2,128)(2,1)} %reshape.296.gain_ref, bf16[1,1024]{1,0:T(2,128)(2,1)} %reshape.297.bias_ref, bf16[512,4096]{1,0:T(8,128)(2,1)} %w0.1, ...), custom_call_target="tpu_custom_call" | custom-call | tf_op jit(solution)/shard_map/project/pallas_call | solution.py:655
  278.7 4.0 %reshape.299 = bf16[768,2,512]{2,1,0:T(2,128)(2,1)} reshape(bf16[768,1024]{1,0:T(8,128)(2,1)} %get-tuple-element.61) | data formatting | bytes 3145728 | tf_op jit(solution)/shard_map/reshape | solution.py:1245
  282.6 1.1 copy.181
  (31 shorter events, 0.3 us)
Async XLA Ops:
  19.5 10.5 %copy-start.10 = (s32[4]{0:T(128)S(1)}, s32[4]{0:T(128)}, u32[]{:S(2)}) copy-start(s32[4]{0:T(128)} %param.19) | copy-start | bytes 52
  19.5 10.7 %copy-start.5 = (bf16[768,512]{1,0:T(8,128)(2,1)S(1)}, bf16[768,512]{1,0:T(8,128)(2,1)}, u32[]{:S(2)}) copy-start(bf16[768,512]{1,0:T(8,128)(2,1)} %param.12) | copy-start | bytes 2359300
  19.5 10.7 %copy-start.7 = (s32[384,3]{0,1:T(4,128)S(1)}, s32[384,3]{0,1:T(4,128)}, u32[]{:S(2)}) copy-start(s32[384,3]{0,1:T(4,128)} %param.21) | copy-start | bytes 13828
  192.6 9.4 %copy-start.8 = (bf16[1024]{0:T(1024)(128)(2,1)S(1)}, bf16[1024]{0:T(1024)(128)(2,1)}, u32[]{:S(2)}) copy-start(bf16[1024]{0:T(1024)(128)(2,1)} %param.16) | copy-start | bytes 6148
  192.7 9.9 %copy-start.9 = (bf16[1024]{0:T(1024)(128)(2,1)S(1)}, bf16[1024]{0:T(1024)(128)(2,1)}, u32[]{:S(2)}) copy-start(bf16[1024]{0:T(1024)(128)(2,1)} %param.17) | copy-start | bytes 6148
  278.6 4.0 %copy-start.6 = (bf16[768,1024]{1,0:T(8,128)(2,1)S(1)}, bf16[768,1024]{1,0:T(8,128)(2,1)}, u32[]{:S(2)}) copy-start(bf16[768,1024]{1,0:T(8,128)(2,1)} %get-tuple-element.192) | copy-start | bytes 4718596

commit v4 on v3

--- a/solution.py
+++ b/solution.py
@@ -3,6 +3,7 @@
 
 import jax
 import jax.numpy as jnp
+import numpy as np
 from jax import lax
 from jax.experimental import pallas as pl
 from jax.experimental.pallas import tpu as pltpu
@@ -444,6 +445,9 @@
     chunks,
     width,
     att_ref,
+    a1,
+    a2,
+    a3,
     residual_ref,
     gain_ref,
     bias_ref,
@@ -456,9 +460,6 @@
     out_ref,
     w_all,
     cross,
-    a1,
-    a2,
-    a3,
     mixed,
     stats,
     g0,
@@ -506,15 +507,6 @@
             device_id_type=MESH,
         )
 
-    def att_mate(c):
-        return hop(0, c, att_ref.at[cut(c)], a1.at[cut(c)], {"tp": mate})
-
-    def att_over(c):
-        return hop(1, c, att_ref.at[cut(c)], a2.at[cut(c)], {"tp": over})
-
-    def att_on(c):
-        return hop(2, c, a2.at[cut(c)], a3.at[cut(c)], {"tp": mate})
-
     def stat(c, k):
         other = (mate, over, cater)[k - 1]
         return hop(2 + k, c, stats.at[c, 0], stats.at[c, k], {"tp": other})
@@ -531,12 +523,6 @@
     def enc_on(c):
         return hop(9, c, g2.at[cut(c)], g3.at[cut(c)], {"tp": mate})
 
-    def begin(c, carry):
-        att_over(c).start()
-        att_mate(c).start()
-        return carry
-
-    lax.fori_loop(0, chunks, begin, 0)
     for k, w in enumerate((own_cols, w1, w2, w3)):
         pltpu.make_async_copy(w, w_all.at[k], w_sem.at[k]).wait()
 
@@ -547,10 +533,6 @@
             @pl.when((c >= 0) & (c < chunks))
             def _():
                 body(c)
-
-        def relay_att(c):
-            att_over(c).wait_recv()
-            att_on(c).start()
 
         def relay_enc(c):
             roll(c).wait_recv()
@@ -575,8 +557,6 @@
             ).astype(encoded_ref.dtype)
 
         def mix(c):
-            att_mate(c).wait_recv()
-            att_on(c).wait_recv()
             part = residual_ref[cut(c), :].astype(jnp.float32)
             for k, a in enumerate((att_ref, a1, a2, a3)):
                 part = part + jnp.dot(
@@ -598,11 +578,10 @@
                 acc = acc + jnp.dot(g[cut(c), :], cross[k], preferred_element_type=jnp.float32)
             out_ref[cut(c), :] = acc.astype(out_ref.dtype)
 
-        at(0, relay_att)
         at(ROLL, relay_enc)
-        at(ROLL + 2, relay_on)
-        at(2, normalize)
-        at(1, mix)
+        at(ROLL + 1, relay_on)
+        at(1, normalize)
+        at(0, mix)
 
         def send_rows(c):
             roll(c).start()
@@ -611,25 +590,22 @@
             for k in (1, 2, 3):
                 stat(c, k).start()
 
-        at(2, send_rows)
-        at(1, send_stats)
-
-        @pl.when(t == ROLL + 3)
+        at(1, send_rows)
+        at(0, send_stats)
+
+        @pl.when(t == ROLL + 2)
         def _():
             for k in range(4):
                 pltpu.make_async_copy(
                     cross_ref.at[pl.ds(0, cols)], cross.at[k], cross_sem.at[k]
                 ).wait()
 
-        at(ROLL + 3, cast)
+        at(ROLL + 2, cast)
         return carry
 
-    lax.fori_loop(0, chunks + ROLL + 3, step, 0)
+    lax.fori_loop(0, chunks + ROLL + 2, step, 0)
 
     def finish(c, carry):
-        att_mate(c).wait_send()
-        att_over(c).wait_send()
-        att_on(c).wait_send()
         for k in (1, 2, 3):
             stat(c, k).wait_send()
         roll(c).wait_send()
@@ -641,12 +617,12 @@
     lax.fori_loop(0, chunks, finish, 0)
 
 
-ROLL = 5
+ROLL = 3
 CHUNKS = 6
 
 
 def project(att, residual, gain, bias, out_weight, weights, cross_weight, ctx_count, tp_count):
-    rows, depth = att.shape
+    rows, depth = att[0].shape
     cols = residual.shape[1]
     wide = cross_weight.shape[1]
     vmem = pl.BlockSpec(memory_space=VMEM)
@@ -659,14 +635,11 @@
             jax.ShapeDtypeStruct((rows, cols), kept),
             jax.ShapeDtypeStruct((rows, wide), kept),
         ),
-        in_specs=[vmem] * 4 + [hbm] * 5,
+        in_specs=[vmem] * 7 + [hbm] * 5,
         out_specs=(vmem, vmem),
         scratch_shapes=[
             VMEM((4, depth, cols), kept),
             VMEM((4, cols, wide), kept),
-            VMEM((rows, depth), kept),
-            VMEM((rows, depth), kept),
-            VMEM((rows, depth), kept),
             VMEM((rows, cols), jnp.float32),
             VMEM((CHUNKS, 4, 16, rows // CHUNKS), jnp.float32),
             VMEM((rows, cols), kept),
@@ -681,10 +654,10 @@
         compiler_params=pltpu.CompilerParams(
             collective_id=2, has_side_effects=True, vmem_limit_bytes=60 * 2**20
         ),
-    )(att, residual, gain, bias, out_weight, *weights, cross_weight)
-
-
-FIRST = 16
+    )(*att, residual, gain, bias, out_weight, *weights, cross_weight)
+
+
+FIRST = 14
 SECOND = 12
 LINE = 4
 HEAD_COLS = 128
@@ -701,6 +674,9 @@
     w1_ref,
     w2_ref,
     w3_ref,
+    a1_ref,
+    a2_ref,
+    a3_ref,
     ext,
     cand,
     got,
@@ -724,6 +700,10 @@
     last3,
     stage1,
     stage2,
+    sums,
+    stats,
+    att_send,
+    att_recv,
     pair_send,
     pair_recv,
     halo_send,
@@ -737,7 +717,8 @@
 ):
     me = lax.axis_index("ctx")
     tp = lax.axis_index("tp")
-    heads, blocks, rows, pair = kv_ref.shape
+    heads, blocks = ext.shape[0], kv_ref.shape[0]
+    rows, pair = ext.shape[2:]
     size = pair // 2
     spot = (me // 8, lax.rem(me // 2, LINE))
     level = lax.rem(me, 2)
@@ -758,11 +739,14 @@
         return carry
 
     lax.fori_loop(1, count, greeting, 0)
-    for other in mates:
+    for other in mates[:2]:
         pl.semaphore_signal(barrier, inc=1, device_id={"tp": other}, device_id_type=MESH)
+    pl.semaphore_signal(
+        barrier, inc=1, device_id={"ctx": twin, "tp": mates[2]}, device_id_type=MESH
+    )
 
     def base(c):
-        return 20 + (c % 2) * (LINE * FIRST + LINE * SECOND + blocks * R)
+        return HEADER + (c % 2) * ROUTE
 
     def along(c, stage, d):
         x, z = spot
@@ -774,7 +758,7 @@
 
     def pair_copy(c):
         return pltpu.make_async_remote_copy(
-            src_ref=kv_ref.at[c],
+            src_ref=ext.at[c, pl.ds(MAXR, blocks)],
             dst_ref=pools[c].at[pl.ds(level * blocks, blocks)],
             send_sem=pair_send.at[c],
             recv_sem=pair_recv.at[c],
@@ -782,17 +766,13 @@
             device_id_type=MESH,
         )
 
-    def halo_copy(k):
-        src, dst, to = (
-            (blocks - MAXR, 0, lax.rem(me + 1, count)),
-            (0, blocks + MAXR, lax.rem(me + count - 1, count)),
-        )[k]
+    def halo_copy(c):
         return pltpu.make_async_remote_copy(
-            src_ref=kv_ref.at[:, pl.ds(src, MAXR)],
-            dst_ref=ext.at[:, pl.ds(dst, MAXR)],
-            send_sem=halo_send.at[k],
-            recv_sem=halo_recv.at[k],
-            device_id={"ctx": to},
+            src_ref=pools[c].at[pl.ds((2 * blocks - MAXR) * (1 - level), MAXR)],
+            dst_ref=ext.at[c, pl.ds((blocks + MAXR) * level, MAXR)],
+            send_sem=halo_send.at[c],
+            recv_sem=halo_recv.at[c],
+            device_id={"ctx": lax.rem(me + 2 - 4 * level + count, count)},
             device_id_type=MESH,
         )
 
@@ -803,7 +783,7 @@
             dst_ref=(w1_ref, w2_ref, w3_ref)[k],
             send_sem=weight_send.at[k],
             recv_sem=weight_recv.at[k],
-            device_id={"tp": other},
+            device_id={"tp": other} if k < 2 else {"ctx": twin, "tp": other},
             device_id_type=MESH,
         )
 
@@ -840,82 +820,46 @@
 
     for g in range(G):
         local = list_ref[G + g]
-        row = jnp.concatenate([kv_ref[c, local] for c in range(heads)] + [q_ref[local]], axis=1)
+        row = jnp.concatenate([kv_ref[local], q_ref[local]], axis=1)
         cut = row.shape[1] // 4
         for r in range(4):
             for s in range(4):
                 cand[(g * 4 + r) * 4 + s] = row[r * 16 : r * 16 + 16, s * cut : (s + 1) * cut]
     for c in range(heads):
-        pools[c][pl.ds(level * blocks, blocks)] = kv_ref[c]
-        ext[c, pl.ds(MAXR, blocks)] = kv_ref[c]
+        for half in range(2):
+            lanes = slice(half * size, (half + 1) * size)
+            begin = half * heads * size + c * size
+            own = kv_ref[:, :, begin : begin + size]
+            pools[c][pl.ds(level * blocks, blocks), :, lanes] = own
+            ext[c, pl.ds(MAXR, blocks), :, lanes] = own
     pl.semaphore_wait(barrier, count - 1 + 3)
 
-    each(lambda k: small(0, k, True, cand, got).start())
-    for c in range(heads):
-        pair_copy(c).start()
-    for k in range(2):
-        halo_copy(k).start()
-    got[me] = cand[me]
-    each(lambda k: small(0, k, True, cand, got).wait())
-    full[me] = got[list_ref[me // (count // G)]]
-    each(lambda k: small(1, k, False, full, full).start())
-
-    for c in range(heads):
+    def scatter(c):
         pair_copy(c).wait()
+        halo_copy(c).start()
+        ext[c, pl.ds((blocks + MAXR) * (1 - level), MAXR)] = pools[c][
+            pl.ds(blocks - MAXR * level, MAXR)
+        ]
         for d in range(1, LINE):
             target, _ = along(c, 0, d)
 
             def fill(j, carry):
-                source = list_ref[base(c) + target * FIRST + j]
+                source = list_ref[base(c) + target * STRIDE + j]
                 stage1[c, (d - 1) * FIRST + j] = pools[c][source]
                 return carry
 
-            lax.fori_loop(0, FIRST, fill, 0)
+            lax.fori_loop(0, FIRST, fill, 0, unroll=2)
         for d in (1, 3, 2):
             bulk(c, 0, d).start()
 
-    each(lambda k: small(1, k, False, full, full).wait())
-    for g in range(G):
-        for r in range(4):
-            row = jnp.concatenate([full[(g * 4 + r) * 4 + s] for s in range(4)], axis=1)
-            gkv[g, r * 16 : r * 16 + 16, :] = row[:, : heads * pair]
-            gq[g, r * 16 : r * 16 + 16, :] = row[:, heads * pair :]
-
-    for h in range(heads):
-        gq_h = gq[:, :, h * size : (h + 1) * size].reshape(G * rows, size)
-        k_h = kv_ref[h, :, :, 0:size].reshape(blocks * rows, size)
-        v_h = kv_ref[h, :, :, size:pair].reshape(blocks * rows, size)
-        s = (
-            lax.dot_general(gq_h, k_h, (((1,), (1,)), ((), ())), preferred_element_type=jnp.float32)
-            * scale
-        )
-        peak = jnp.max(s, axis=1, keepdims=True)
-        p = jnp.exp(s - peak)
-        total = jnp.sum(p, axis=1, keepdims=True)
-        acc = jnp.dot(p.astype(jnp.bfloat16), v_h, preferred_element_type=jnp.float32)
-        peak = jnp.broadcast_to(peak, acc.shape)
-        total = jnp.broadcast_to(total, acc.shape)
-        for r in range(8):
-            cut = slice(r * 16, r * 16 + 16)
-            part[h * 8 + r, 0:16, :] = acc[cut]
-            part[h * 8 + r, 16:32, :] = peak[cut]
-            part[h * 8 + r, 32:48, :] = total[cut]
-    far_got[me] = part[me]
-    for k in range(3):
-        weight_copy(k).start()
-    each(lambda k: small(2, k, True, part, far_got).start())
-
-    held = 2 * blocks
-    ended = held + LINE * FIRST
-
-    for c in range(heads):
+    def forward(c):
         for d in range(1, LINE):
             bulk(c, 0, d).wait()
         for d in range(1, LINE):
             target, _ = along(c, 1, d)
 
             def fill(j, carry):
-                source = list_ref[base(c) + LINE * FIRST + target * SECOND + j]
+                source = list_ref[base(c) + (LINE + target) * STRIDE + j]
                 stage2[c, (d - 1) * SECOND + j] = jnp.where(
                     source < held,
                     pools[c][jnp.minimum(source, held - 1)],
@@ -923,47 +867,63 @@
                 )
                 return carry
 
-            lax.fori_loop(0, SECOND, fill, 0)
+            lax.fori_loop(0, SECOND, fill, 0, unroll=2)
         for d in (1, 3, 2):
             bulk(c, 1, d).start()
 
-    each(lambda k: small(2, k, True, part, far_got).wait())
-
-    def top(i, so_far):
-        return jnp.maximum(so_far, far_got[i, 16:32, :])
-
-    far_peak = lax.fori_loop(1, count, top, far_got[0, 16:32, :])
-
-    def add(i, so_far):
-        acc, total = so_far
-        factor = jnp.exp(far_got[i, 16:32, :] - far_peak)
-        return acc + far_got[i, 0:16, :] * factor, total + far_got[i, 32:48, :] * factor
-
-    zero = jnp.zeros_like(far_peak)
-    far_acc, far_total = lax.fori_loop(0, count, add, (zero, zero))
-    far[me] = (far_acc / far_total).astype(far.dtype)
-    each(lambda k: small(3, k, False, far, far).start())
-
-    for k in range(2):
-        halo_copy(k).wait()
+    held = 2 * blocks
+    ended = held + LINE * FIRST
 
     place = lax.broadcasted_iota(jnp.int32, (rows, near), 1) // rows - MAXR
-    for c in range(heads):
-        for d in range(1, LINE):
-            bulk(c, 1, d).wait()
+    left = lax.broadcasted_iota(jnp.int32, (rows, size), 1) < size // 2
+
+    def score(q, keys):
+        return (
+            lax.dot_general(q, keys, (((1,), (1,)), ((), ())), preferred_element_type=jnp.float32)
+            * scale
+        )
+
+    def nearby(c):
+        halo_copy(c).wait()
         lanes = slice(c * size, (c + 1) * size)
-        reach = list_ref[2 * G + c]
-        allowed = jnp.abs(place) <= reach
-        g_k = gkv[:, :, c * pair : c * pair + size].reshape(G * rows, size)
-        g_v = gkv[:, :, c * pair + size : (c + 1) * pair].reshape(G * rows, size)
+        allowed = jnp.abs(place) <= list_ref[2 * G + c]
+        g_k = gkv[:, :, c * size : (c + 1) * size].reshape(G * rows, size)
+        g_v = gkv[:, :, (heads + c) * size : (heads + c + 1) * size].reshape(G * rows, size)
 
         def attend(b, carry):
             block = me * blocks + b
             inside = (place + block >= 0) & (place + block < count * blocks)
             q = q_ref[b, :, lanes]
+            window = ext[c, pl.ds(b, SPAN)].reshape(near, pair)
+            s1 = jnp.where(inside & allowed, score(q, window[:, :size]), -jnp.inf)
+            s2 = score(q, g_k)
+            peak = jnp.maximum(
+                jnp.max(s1, axis=1, keepdims=True), jnp.max(s2, axis=1, keepdims=True)
+            )
+            p1 = jnp.exp(s1 - peak)
+            p2 = jnp.exp(s2 - peak)
+            total = jnp.sum(p1, axis=1, keepdims=True) + jnp.sum(p2, axis=1, keepdims=True)
+            sums[c, b] = jnp.dot(
+                p1.astype(jnp.bfloat16), window[:, size:], preferred_element_type=jnp.float32
+            ) + jnp.dot(p2.astype(jnp.bfloat16), g_v, preferred_element_type=jnp.float32)
+            stats[c, b] = jnp.where(left, peak, total)
+            return carry
+
+        lax.fori_loop(0, blocks, attend, 0)
+
+    def distant(c):
+        for d in range(1, LINE):
+            bulk(c, 1, d).wait()
+        lanes = slice(c * size, (c + 1) * size)
+        swap = [
+            jnp.concatenate([far[c * 8 + g * 4 + r] for r in range(4)], axis=0) for g in range(G)
+        ]
+
+        def attend(b, carry):
+            q = q_ref[b, :, lanes]
             picked = []
             for r in range(R):
-                at = list_ref[base(c) + LINE * (FIRST + SECOND) + b * R + r]
+                at = list_ref[base(c) + 2 * LINE * STRIDE + b * R + r]
                 picked.append(
                     jnp.where(
                         at < held,
@@ -975,75 +935,157 @@
                         ),
                     )
                 )
-
-            def score(keys):
-                return (
-                    lax.dot_general(
-                        q, keys, (((1,), (1,)), ((), ())), preferred_element_type=jnp.float32
-                    )
-                    * scale
-                )
-
-            window = ext[c, pl.ds(b, SPAN)].reshape(near, pair)
-            s1 = jnp.where(inside & allowed, score(window[:, :size]), -jnp.inf)
-            s2 = score(jnp.concatenate([g_k] + [x[:, :size] for x in picked], axis=0))
-            peak = jnp.maximum(
-                jnp.max(s1, axis=1, keepdims=True), jnp.max(s2, axis=1, keepdims=True)
+            extra = jnp.concatenate(picked, axis=0)
+            s2 = score(q, extra[:, :size])
+            first_peak = stats[c, b, :, 0:1]
+            peak = jnp.maximum(first_peak, jnp.max(s2, axis=1, keepdims=True))
+            factor = jnp.exp(first_peak - peak)
+            p2 = jnp.exp(s2 - peak)
+            total = stats[c, b, :, size // 2 : size // 2 + 1] * factor + jnp.sum(
+                p2, axis=1, keepdims=True
             )
-            p1 = jnp.exp(s1 - peak)
-            p2 = jnp.exp(s2 - peak)
-            total = jnp.sum(p1, axis=1, keepdims=True) + jnp.sum(p2, axis=1, keepdims=True)
-            acc = jnp.dot(
-                p1.astype(jnp.bfloat16), window[:, size:], preferred_element_type=jnp.float32
-            ) + jnp.dot(
-                p2.astype(jnp.bfloat16),
-                jnp.concatenate([g_v] + [x[:, size:] for x in picked], axis=0),
-                preferred_element_type=jnp.float32,
+            acc = sums[c, b] * factor + jnp.dot(
+                p2.astype(jnp.bfloat16), extra[:, size:], preferred_element_type=jnp.float32
             )
-            out_ref[b, :, lanes] = (acc / total).astype(out_ref.dtype)
+            which = list_ref[2 * G + heads + b]
+            result = (acc / total).astype(out_ref.dtype)
+            out_ref[b, :, lanes] = jnp.where(
+                which == 0, swap[0], jnp.where(which == 1, swap[1], result)
+            )
             return carry
 
         lax.fori_loop(0, blocks, attend, 0)
 
+    def att_copy(kind, c, src, dst, other):
+        lanes = pl.ds(c * size, size)
+        return pltpu.make_async_remote_copy(
+            src_ref=src.at[:, :, lanes],
+            dst_ref=dst.at[:, :, lanes],
+            send_sem=att_send.at[kind, c],
+            recv_sem=att_recv.at[kind, c],
+            device_id={"tp": other},
+            device_id_type=MESH,
+        )
+
+    def att_mate(c):
+        return att_copy(0, c, out_ref, a1_ref, mates[0])
+
+    def att_over(c):
+        return att_copy(1, c, out_ref, a2_ref, mates[1])
+
+    def att_on(c):
+        return att_copy(2, c, a2_ref, a3_ref, mates[0])
+
+    each(lambda k: small(0, k, True, cand, got).start())
+    for c in range(heads):
+        pair_copy(c).start()
+    got[me] = cand[me]
+    each(lambda k: small(0, k, True, cand, got).wait())
+    full[me] = got[list_ref[me // (count // G)]]
+    each(lambda k: small(1, k, False, full, full).start())
+    scatter(0)
+    scatter(1)
+
+    each(lambda k: small(1, k, False, full, full).wait())
+    for g in range(G):
+        for r in range(4):
+            row = jnp.concatenate([full[(g * 4 + r) * 4 + s] for s in range(4)], axis=1)
+            gkv[g, r * 16 : r * 16 + 16, :] = row[:, : heads * pair]
+            gq[g, r * 16 : r * 16 + 16, :] = row[:, heads * pair :]
+
+    half_lane = lax.broadcasted_iota(jnp.int32, (G * rows, size), 1) < size // 2
+    for h in range(heads):
+        gq_h = gq[:, :, h * size : (h + 1) * size].reshape(G * rows, size)
+        k_h = kv_ref[:, :, h * size : (h + 1) * size].reshape(blocks * rows, size)
+        v_h = kv_ref[:, :, (heads + h) * size : (heads + h + 1) * size].reshape(
+            blocks * rows, size
+        )
+        s = (
+            lax.dot_general(gq_h, k_h, (((1,), (1,)), ((), ())), preferred_element_type=jnp.float32)
+            * scale
+        )
+        peak = jnp.max(s, axis=1, keepdims=True)
+        p = jnp.exp(s - peak)
+        total = jnp.sum(p, axis=1, keepdims=True)
+        acc = jnp.dot(p.astype(jnp.bfloat16), v_h, preferred_element_type=jnp.float32)
+        both = jnp.where(half_lane, peak, total)
+        for r in range(8):
+            cut = slice(r * 16, r * 16 + 16)
+            part[h * 8 + r, 0:16, :] = acc[cut]
+            part[h * 8 + r, 16:32, :] = both[cut]
+    far_got[me] = part[me]
+    each(lambda k: small(2, k, True, part, far_got).start())
+    scatter(2)
+    scatter(3)
+    for k in range(3):
+        weight_copy(k).start()
+    forward(0)
+    nearby(0)
+    forward(1)
+    nearby(1)
+
+    each(lambda k: small(2, k, True, part, far_got).wait())
+
+    def top(i, so_far):
+        return jnp.maximum(so_far, far_got[i, 16:32, 0:1])
+
+    far_peak = lax.fori_loop(1, count, top, far_got[0, 16:32, 0:1], unroll=4)
+
+    def add(i, so_far):
+        acc, total = so_far
+        factor = jnp.exp(far_got[i, 16:32, 0:1] - far_peak)
+        return (
+            acc + far_got[i, 0:16, :] * factor,
+            total + far_got[i, 16:32, size // 2 : size // 2 + 1] * factor,
+        )
+
+    far_acc, far_total = lax.fori_loop(
+        0, count, add, (jnp.zeros((16, size), jnp.float32), jnp.zeros((16, 1), jnp.float32)), unroll=4
+    )
+    far[me] = (far_acc / far_total).astype(far.dtype)
+    each(lambda k: small(3, k, False, far, far).start())
+    forward(2)
+    forward(3)
+
+    nearby(2)
+    nearby(3)
+
     each(lambda k: small(3, k, False, far, far).wait())
-    swap = []
-    for g in range(G):
-        swap.append(
-            jnp.concatenate(
-                [
-                    jnp.concatenate([far[h * 8 + g * 4 + r] for r in range(4)], axis=0)
-                    for h in range(heads)
-                ],
-                axis=1,
-            )
-        )
-
-    def replace(b, carry):
-        which = list_ref[2 * G + heads + b]
-        out_ref[b] = jnp.where(which == 0, swap[0], jnp.where(which == 1, swap[1], out_ref[b]))
-        return carry
-
-    lax.fori_loop(0, blocks, replace, 0)
+    for c in range(heads):
+        distant(c)
+        if c > 0:
+            att_over(c - 1).wait_recv()
+            att_on(c - 1).start()
+        att_over(c).start()
+        att_mate(c).start()
+    att_over(heads - 1).wait_recv()
+    att_on(heads - 1).start()
+    for c in range(heads):
+        att_over(c).wait_send()
+        att_mate(c).wait()
+        att_on(c).wait()
     for k in range(3):
         weight_copy(k).wait()
 
 
-def front(lists, kv, q, weight, scale, count, tp_count):
-    heads, blocks, rows, pair = kv.shape
+def front(lists, kv, q, heads, weight, scale, count, tp_count):
+    blocks, rows, wide = kv.shape
+    pair = wide // heads
     size = pair // 2
     kept = kv.dtype
     vmem = pl.BlockSpec(memory_space=VMEM)
     hbm = pl.BlockSpec(memory_space=pl.ANY)
     cols = weight.shape[1] // tp_count
     moved = jax.ShapeDtypeStruct((weight.shape[0], cols), kept)
+    same = jax.ShapeDtypeStruct(q.shape, kept)
     cut = (heads * pair + heads * size) // 4
     dma = pltpu.SemaphoreType.DMA
     return pl.pallas_call(
         functools.partial(front_kernel, count, scale),
         name="front",
-        out_shape=(jax.ShapeDtypeStruct(q.shape, kept), moved, moved, moved),
+        out_shape=(jax.ShapeDtypeStruct(q.shape, kept),) + (moved,) * 3 + (same,) * 3,
         in_specs=[pl.BlockSpec(memory_space=SMEM), vmem, vmem, hbm],
-        out_specs=(vmem, hbm, hbm, hbm),
+        out_specs=(vmem,) + (hbm,) * 6,
         scratch_shapes=[
             VMEM((heads, blocks + 2 * MAXR, rows, pair), kept),
             VMEM((count, 16, cut), kept),
@@ -1051,8 +1093,8 @@
             VMEM((count, 16, cut), kept),
             VMEM((G, rows, heads * pair), kept),
             VMEM((G, rows, heads * size), kept),
-            VMEM((count, 48, size), jnp.float32),
-            VMEM((count, 48, size), jnp.float32),
+            VMEM((count, 32, size), jnp.float32),
+            VMEM((count, 32, size), jnp.float32),
             VMEM((count, 16, size), kept),
         ]
         + [VMEM((2 * blocks, rows, pair), kept)] * heads
@@ -1061,10 +1103,14 @@
         + [
             VMEM((heads, (LINE - 1) * FIRST, rows, pair), kept),
             VMEM((heads, (LINE - 1) * SECOND, rows, pair), kept),
+            VMEM((heads, blocks, rows, size), jnp.float32),
+            VMEM((heads, blocks, rows, size), jnp.float32),
+            dma((3, heads)),
+            dma((3, heads)),
             dma((heads,)),
             dma((heads,)),
-            dma((2,)),
-            dma((2,)),
+            dma((heads,)),
+            dma((heads,)),
             dma((3,)),
             dma((3,)),
             dma((4, count)),
@@ -1078,82 +1124,157 @@
     )(lists, kv, q, weight)
 
 
-def exclusive(flags):
-    ones = flags.astype(jnp.int32)
-    return jnp.cumsum(ones, axis=-1) - ones
-
-
-def listing(flags, ranks, values, slots):
-    wanted = jnp.arange(slots, dtype=jnp.int32)[:, None]
-    hit = flags[..., None, :] & (ranks[..., None, :] == wanted)
-    return jnp.sum(jnp.where(hit, values, 0), axis=-1)
-
-
-def route(asked, first, second, entries):
-    many = asked.shape[-1]
-    ids = jnp.arange(many, dtype=jnp.int32)
-    line = jnp.arange(LINE, dtype=jnp.int32)
-    need = jnp.any(asked, axis=1)
-    rank = exclusive(need)
-    mine = need[:, first, second]
-    list1 = listing(mine, rank[:, first, second], ids, FIRST)
-    held = many + line[:, None, None] * FIRST + jnp.minimum(rank[first], FIRST - 1)
-    where = jnp.where(line[:, None, None] == first, ids, held)
-    here = asked[first]
-    wanted = here[:, :, second].reshape(LINE, LINE * many)
-    list2 = listing(wanted, exclusive(wanted), where[:, second].reshape(-1), SECOND)
-    own = jnp.swapaxes(here[second], 0, 1).reshape(LINE, LINE * many)
-    ended = (
-        many
-        + LINE * FIRST
-        + line[:, None] * SECOND
-        + jnp.minimum(exclusive(own), SECOND - 1)
+STRIDE = 16
+HEADER = 24
+ROUTE = 2 * LINE * STRIDE + 40
+
+
+def plan_kernel(count, blocks, row_ref, col_ref, req_ref, reqt_ref, reach_ref, gb_ref, out_ref):
+    me = lax.axis_index("ctx")
+    x, z, level = me // 8, lax.rem(me // 2, LINE), lax.rem(me, 2)
+    many = 2 * blocks
+    total = count * blocks
+    low = jnp.bfloat16
+
+    def iota(shape, dim):
+        return lax.broadcasted_iota(jnp.int32, shape, dim)
+
+    def product(a, b):
+        return jnp.dot(a.astype(low), b.astype(low), preferred_element_type=jnp.float32)
+
+    def flag(condition):
+        return jnp.where(condition, 1.0, 0.0)
+
+    ids = iota((count, total), 1)
+    asked = jnp.zeros((count, total), jnp.float32)
+    for e in range(blocks * R):
+        asked = jnp.where(req_ref[:, e : e + 1] == ids, 1.0, asked)
+
+    place = {"x": row_ref[0:1, :], "z": row_ref[1:2, :]}
+    inner = row_ref[2:3, :].astype(jnp.float32)
+    group = row_ref[3:4, :]
+    place_col = {"x": col_ref[:, 0:1], "z": col_ref[:, 1:2]}
+    group_col = col_ref[:, 3:4]
+    before = iota((total, total), 0) < iota((total, total), 1)
+
+    r8, s8 = iota((8, count), 0), iota((8, count), 1)
+    where_of = {"x": s8 >> 3, "z": (s8 >> 1) & 3}
+    lane = iota((8, 128), 1)
+    line8 = iota((8, 128), 0) >> 1
+    lane32 = iota((count, 128), 1)
+    row32 = iota((count, 128), 0)
+    own32 = {"x": row32 >> 3, "z": (row32 >> 1) & 3}
+    pair_of = {"x": lane >> 2, "z": lane & 3}
+    seats = flag(group_col == iota((total, 128), 1))
+    longest = []
+    for first, second in (("x", "z"), ("z", "x")):
+        same = (where_of[first] == r8 >> 1) & ((s8 & 1) == (r8 & 1))
+        need = flag(product(flag(same), asked) > 0)
+        counts = product(need, seats)
+        apart = (lane < LINE * LINE) & (pair_of[first] != line8)
+        longest.append(jnp.max(jnp.where(apart, counts - FIRST, -1.0)))
+        counts = product(asked, flag(place_col[second] == iota((total, 128), 1)))
+        apart = (lane32 < LINE) & (lane32 != own32[second])
+        longest.append(jnp.max(jnp.where(apart, counts - SECOND, -1.0)))
+    over = jnp.maximum(
+        jnp.maximum(longest[0], longest[1]), jnp.maximum(longest[2], longest[3])
     )
-    ended = jnp.swapaxes(ended.reshape(LINE, LINE, many), 0, 1)
-    final = jnp.where(line[None, :, None] == second, where, ended)
-    return list1.reshape(-1), list2.reshape(-1), final
-
-
-def plan(random_blocks, block_count, ctx_count, me):
-    req_count = block_count * R
-    all_blocks = block_count * ctx_count
-    requests = random_blocks.reshape(ctx_count, req_count)
-    asked = jnp.any(
-        requests[:, :, None] == jnp.arange(all_blocks, dtype=jnp.int32)[None, None, :], axis=1
+
+    head = iota((HEADER, 128), 0)
+    top = jnp.where(head == 20, jnp.where(over > 0, 0, 1), 0)
+    entries = []
+    for g in range(G):
+        entries.append((g, gb_ref[g] // blocks))
+        entries.append((G + g, lax.rem(gb_ref[g], blocks)))
+    for h in range(4):
+        entries.append((2 * G + h, reach_ref[h]))
+    for b in range(blocks):
+        block = me * blocks + b
+        which = jnp.where(block == gb_ref[0], 0, jnp.where(block == gb_ref[1], 1, -1))
+        entries.append((2 * G + 4 + b, which))
+    for k, value in entries:
+        top = jnp.where(head == k, value, top)
+    out_ref[0:HEADER, :] = top
+
+    spots = {"x": x, "z": z}
+    mine = (place["x"] == x) & (place["z"] == z)
+    turn = iota((8, total), 0)
+    asked_col = jnp.sum(
+        jnp.where(iota(reqt_ref.shape, 1) == me, reqt_ref[...], 0), axis=1, keepdims=True
     )
-    asked = asked.reshape(LINE, LINE, 2, LINE, LINE, 2 * block_count)
-    line = jnp.arange(LINE, dtype=jnp.int32)
-    apart = line[:, None] != line[None, :]
-    ones = asked.astype(jnp.int32)
-
-    def most(counts, mask):
-        return jnp.max(jnp.where(mask, counts, 0))
-
-    first_x = most(jnp.sum(jnp.max(ones, axis=1), axis=-1), apart[:, None, :, None])
-    first_z = most(jnp.sum(jnp.max(ones, axis=0), axis=-1), apart[:, None, None, :])
-    second_z = most(jnp.sum(ones, axis=(3, 5)), apart[None, :, None, :])
-    second_x = most(jnp.sum(ones, axis=(4, 5)), apart[:, None, None, :])
-    fits = (jnp.maximum(first_x, first_z) <= FIRST) & (jnp.maximum(second_x, second_z) <= SECOND)
-    x, z, level = me // 8, me // 2 % LINE, me % 2
-    flat = asked[:, :, level]
-    mine = requests[me]
-    picked = mine[:, None] == jnp.arange(all_blocks, dtype=jnp.int32)[None, :]
-    lists = []
-    for turned in (False, True):
-        if turned:
-            a, b, final = route(jnp.transpose(flat, (1, 0, 3, 2, 4)), z, x, mine)
-            final = jnp.swapaxes(final, 0, 1)
-        else:
-            a, b, final = route(flat, x, z, mine)
-        lists += [a, b, jnp.sum(jnp.where(picked, final.reshape(-1)[None, :], 0), axis=1)]
-    return fits, lists
-
-
-def direct(place, info, source_ids, my_index, kv_heads, q, out_weight, scale, count, slots):
-    heads, block_count, rows, pair = kv_heads.shape
-    kv = jnp.transpose(
-        kv_heads.reshape(heads, block_count, rows, 2, pair // 2), (1, 2, 3, 0, 4)
-    ).reshape(block_count, rows, heads * pair)
+
+    def store(offset, column):
+        out_ref[offset : offset + column.shape[0], :] = jnp.broadcast_to(
+            column.astype(jnp.int32), (column.shape[0], 128)
+        )
+
+    for o, (first, second) in enumerate((("x", "z"), ("z", "x"))):
+        start = HEADER + o * ROUTE
+        line_first = place[first].astype(jnp.float32)
+        line_second = place[second].astype(jnp.float32)
+        same = (where_of[first] == r8) & ((s8 & 1) == level)
+        need = flag(product(flag(same), asked) > 0)
+        rank = product(need, flag(before & (group_col == group)))
+        slot = iota((STRIDE, total), 0).astype(jnp.float32)
+        for t in range(LINE):
+            hit = (need[t : t + 1] > 0) & mine & (rank[t : t + 1] == slot)
+            column = jnp.sum(jnp.where(hit, inner, 0.0), axis=1, keepdims=True)
+            store(start + t * STRIDE, column)
+        my_rank = jnp.sum(jnp.where(turn == spots[first], rank, 0.0), axis=0, keepdims=True)
+        found = jnp.where(
+            place[first] == spots[first],
+            inner,
+            many + line_first * FIRST + jnp.minimum(my_rank, FIRST - 1),
+        )
+        line = (where_of[first] == spots[first]) & (where_of[second] == r8)
+        here = product(flag(line & ((s8 & 1) == level)), asked)
+        wanted = flag((here > 0) & (place[second] == spots[second]))
+        rank = product(wanted, flag(before))
+        for t in range(LINE):
+            hit = (wanted[t : t + 1] > 0) & (rank[t : t + 1] == slot)
+            column = jnp.sum(jnp.where(hit, found, 0.0), axis=1, keepdims=True)
+            store(start + (LINE + t) * STRIDE, column)
+        own = jnp.sum(jnp.where(turn == spots[second], here, 0.0), axis=0, keepdims=True)
+        rank = product(
+            jnp.broadcast_to(own, (8, total)),
+            flag(before & (place_col[second] == place[second])),
+        )[0:1]
+        final = jnp.where(
+            place[second] == spots[second],
+            found,
+            many + LINE * FIRST + line_second * SECOND + jnp.minimum(rank, SECOND - 1),
+        )
+        hit = asked_col == iota((reqt_ref.shape[0], total), 1)
+        column = jnp.sum(jnp.where(hit, final, 0.0), axis=1, keepdims=True)
+        store(start + 2 * LINE * STRIDE, column)
+
+
+def plan(random_blocks, global_blocks, window_reach, blocks, count):
+    requests = random_blocks.reshape(count, blocks * R)
+    total = count * blocks
+    ids = np.arange(total)
+    table = np.zeros((8, total), np.int32)
+    table[0] = ids // (LINE * 2 * blocks)
+    table[1] = ids // (2 * blocks) % LINE
+    table[2] = ids % (2 * blocks)
+    table[3] = ids // (2 * blocks)
+    turned = jnp.pad(requests.T, ((0, 40 - blocks * R), (0, 0)), constant_values=-1)
+    vmem = pl.BlockSpec(memory_space=VMEM)
+    smem = pl.BlockSpec(memory_space=SMEM)
+    out = pl.pallas_call(
+        functools.partial(plan_kernel, count, blocks),
+        name="plan",
+        out_shape=jax.ShapeDtypeStruct((HEADER + 2 * ROUTE, 128), jnp.int32),
+        in_specs=[vmem] * 4 + [smem] * 2,
+        out_specs=vmem,
+        compiler_params=pltpu.CompilerParams(vmem_limit_bytes=48 * 2**20),
+    )(table, np.ascontiguousarray(table.T), requests, turned, window_reach, global_blocks)
+    return out[:, 0]
+
+
+def direct(place, info, source_ids, my_index, kv, q, out_weight, scale, count, slots):
+    block_count = q.shape[0]
+    heads = info.shape[0] - block_count
     ext, gkv, gq = edges(place, kv, q, count)
     partials = far_partials(gq, kv, scale, heads, count)
     random, far = exchange(source_ids, kv, partials, count, slots)
@@ -1168,6 +1289,8 @@
     for k in range(1, tp_count):
         block = lax.dynamic_slice_in_dim(out_weight, mates[k] * cols, cols, axis=1)
         weights.append(lax.ppermute(block, "tp", [(i, i ^ k) for i in range(tp_count)]))
+    for k in range(1, tp_count):
+        weights.append(lax.ppermute(attended, "tp", [(i, i ^ k) for i in range(tp_count)]))
     return (attended, *weights)
 
 
@@ -1192,23 +1315,14 @@
     block_count = tok_rows // BLOCK
     scale = 1.0 / math.sqrt(head_size)
     q = queries.reshape(block_count, BLOCK, head_cols)
-    kv_heads = jnp.transpose(
-        keyvals.reshape(block_count, BLOCK, 2, head_count, head_size), (3, 0, 1, 2, 4)
-    ).reshape(head_count, block_count, BLOCK, 2 * head_size)
-
-    place = jnp.concatenate([global_blocks // block_count, global_blocks % block_count])
-    own_ids = me * block_count + jnp.arange(block_count, dtype=jnp.int32)
-    replaced = jnp.where(
-        own_ids == global_blocks[0], 0, jnp.where(own_ids == global_blocks[1], 1, -1)
-    )
-    info = jnp.concatenate([window_reach, replaced])
-    fits, lists = plan(random_blocks, block_count, ctx_count, me)
-    lists = jnp.concatenate([place, info] + lists)
-
-    def staged(kv_heads, q, out_weight):
-        return tuple(front(lists, kv_heads, q, out_weight, scale, ctx_count, tp_count))
-
-    def plain(kv_heads, q, out_weight):
+    kv = keyvals.reshape(block_count, BLOCK, 2 * head_cols)
+    lists = plan(random_blocks, global_blocks, window_reach, block_count, ctx_count)
+    fits = lists[20] > 0
+
+    def staged(kv, q, out_weight):
+        return tuple(front(lists, kv, q, head_count, out_weight, scale, ctx_count, tp_count))
+
+    def plain(kv, q, out_weight):
         req_count = block_count * R
         slots = 1 + (req_count + ctx_count - 2) // ctx_count
         requests = random_blocks.reshape(ctx_count, req_count)
@@ -1224,15 +1338,18 @@
         matches = (owners[:, None, :] == me) & (ranks[:, None, :] == slot_ids[None, :, None])
         source_ids = jnp.sum(jnp.where(matches, local_ids[:, None, :], 0), axis=2).reshape(-1)
         my_index = lax.dynamic_index_in_dim(owners * slots + ranks, me, 0, keepdims=False)
+        place = lists[: 2 * G]
+        info = lists[2 * G : 2 * G + head_count + block_count]
         return direct(
-            place, info, source_ids, my_index, kv_heads, q, out_weight, scale, ctx_count, slots
-        )
-
-    attended, *weights = lax.cond(fits, staged, plain, kv_heads, q, out_weight)
-    attended = attended.reshape(tok_rows, head_cols)
+            place, info, source_ids, my_index, kv, q, out_weight, scale, ctx_count, slots
+        )
+
+    attended, *rest = lax.cond(fits, staged, plain, kv, q, out_weight)
+    weights = rest[: tp_count - 1]
+    gathered = [x.reshape(tok_rows, head_cols) for x in [attended] + rest[tp_count - 1 :]]
     cols = residual.shape[1]
     encoded, cross_kv = project(
-        attended,
+        gathered,
         residual,
         norm_gain.reshape(1, cols),
         norm_bias.reshape(1, cols),

time: 284 us -> 240 us (0.85)
  Pallas kernels: 232 us -> 212 us
  other arithmetic: 17 us -> 0 us
  local copies, waits for them, and re-layouts: 30.5 us -> 24.2 us
    pallas_call x1, Pallas kernels: 75.4 us -> 60 us  [project(): pl.pallas_call(functools.partial(project_kernel, ctx_count, tp_count, CHU...]
    another operation x6 -> x0, other arithmetic: 7.36 us -> none  [exclusive(): return jnp.cumsum(ones, axis=-1) - ones]
    pallas_call x1, Pallas kernels: 157 us -> 150 us  [front(): pl.pallas_call(functools.partial(front_kernel, count, scale), name='front...]
    reduce_sum x8 -> x0, other arithmetic: 5.32 us -> none  [the longest x1 3 us: plan(): second_z = most(jnp.sum(ones, axis=(3, 5)), apart[None, :, None, :])]
    reshape x8 -> x3, local copies, waits for them, and re-layouts: 7.54 us -> 4.06 us  [the longest x1 3.86 us: shards(): kv = keyvals.reshape(block_count, BLOCK, 2 * head_cols)]
    another operation x7 -> x0, local copies, waits for them, and re-layouts: 3.41 us -> none
    unnamed x17 -> x21, local copies, waits for them, and re-layouts: 11.3 us -> 14.3 us
where the time goes in v4:
time: 240 us; the launch traced here: 238 us
  Pallas kernels  212 us (88%)
  local copies, waits for them, and re-layouts  24.2 us (10%)
    pallas_call x1, Pallas kernels, front(): pl.pallas_call(functools.partial(front_kernel, count, scale), name='front...  150 us
    pallas_call x1, Pallas kernels, project(): pl.pallas_call(functools.partial(project_kernel, ctx_count, tp_count, CHU...  60 us
    unnamed x21, local copies, waits for them, and re-layouts  14.3 us

profile of v4, /device:TPU:1, one launch (start us, length us, event | category | flops | bytes accessed | tf_op | source)
XLA Modules:
  0.0 238.2 jit_solution(5181891134214151328)
XLA Ops:
  0.6 0.8 copy.53
  1.5 0.1 reshape.127.req_ref
  1.6 0.1 copy.54
  1.7 0.0 copy-start.1
  1.7 0.9 copy-done.1
  2.6 0.0 copy-start.3
  2.6 0.7 copy-done.3
  3.3 0.0 copy-start.4
  3.3 0.7 copy-done.4
  4.0 0.0 copy-start.5
  4.0 0.7 copy-done.5
  4.6 2.0 plan.1
  6.6 0.2 slice_reduce_fusion
  6.8 0.0 copy-start.6
  6.8 0.0 copy-start.8
  6.8 3.9 %reshape.128 = bf16[12,64,1024]{2,1,0:T(8,128)(2,1)} reshape(bf16[768,2,512]{2,1,0:T(2,128)(2,1)} %param.15) | data formatting | bytes 3145728 | tf_op jit(solution)/shard_map/reshape | solution.py:1318
  10.7 0.5 slice.16
  11.8 0.0 copy-done.6
  11.8 0.0 copy-done.8
  11.8 150.6 %conditional.1 = (bf16[512,1024]{1,0:T(8,128)(2,1)S(1)}, bf16[512,1024]{1,0:T(8,128)(2,1)S(1)}, bf16[512,1024]{1,0:T(8,128)(2,1)}, bf16[768,512]{1,0:T(8,128)(2,...) conditional(s32[]{:T(128)} %bitcast.10, (bf16[512,4096]{1,0:T(8,128)(2,1)}, ...), branch_computations={%region_0.3_spmd, %region_3.4_spmd} | conditional | flops 195994 | bytes 32104924 | solution.py:1347
  12.0 150.4 %front.1 = (bf16[12,64,512]{2,1,0:T(8,128)(2,1)}, bf16[512,1024]{1,0:T(8,128)(2,1)S(1)}, bf16[512,1024]{1,0:T(8,128)(2,1)S(1)}, bf16[512,1024]{1,0:T(8,128)(2,1)...) custom-call(s32[360]{0:T(512)S(1)} %get-tuple-element.42.list_ref, ...), custom_call_target="tpu_custom_call" | custom-call | tf_op jit(solution)/shard_map/cond/branch_1_fun/front/pallas_call | solution.py:1083
  162.5 0.0 copy-start.9
  162.5 0.0 copy-start.10
  162.5 9.3 %copy.56 = bf16[512,8,2,512]{3,1,2,0:T(8,128)(2,1)} copy(bf16[512,8,2,512]{3,2,1,0:T(2,128)(2,1)} %bitcast.16) | data formatting | bytes 16777216
  171.9 0.0 copy-done.9
  171.9 0.6 reshape.130.gain_ref
  172.5 0.0 copy-done.10
  172.5 0.6 reshape.131.bias_ref
  173.1 60.0 %project.1 = (bf16[768,1024]{1,0:T(8,128)(2,1)}, bf16[768,1024]{1,0:T(8,128)(2,1)}) custom-call(bf16[768,512]{1,0:T(8,128)(2,1)} %get-tuple-element.64.att_ref, bf16[768,512]{1,0:T(8,128)(2,1)} %get-tuple-element.65.a1, bf16[768,512]{1,0:T(8,128)(2,1)} %get-tuple-element.66.a2, bf16[768,512]{1,0:T(8,128)(2,1)} %get-tuple-element.67.a3, ...), custom_call_target="tpu_custom_call" | custom-call | tf_op jit(solution)/shard_map/project/pallas_call | solution.py:631
  233.1 0.0 copy-start.7
  233.1 4.0 %reshape.133 = bf16[768,2,512]{2,1,0:T(2,128)(2,1)} reshape(bf16[768,1024]{1,0:T(8,128)(2,1)} %get-tuple-element.72) | data formatting | bytes 3145728 | tf_op jit(solution)/shard_map/reshape | solution.py:1362
  237.1 0.0 copy-done.7
  237.1 1.1 copy.72
  (1 shorter events, 0.0 us)
Async XLA Ops:
  1.7 0.9 copy-start.1
  2.6 0.7 copy-start.3
  3.3 0.7 copy-start.4
  4.0 0.7 copy-start.5
  6.8 5.1 %copy-start.6 = (bf16[768,512]{1,0:T(8,128)(2,1)S(1)}, bf16[768,512]{1,0:T(8,128)(2,1)}, u32[]{:S(2)}) copy-start(bf16[768,512]{1,0:T(8,128)(2,1)} %param.14) | copy-start | bytes 2359300
  6.8 5.1 %copy-start.8 = (s32[384,3]{0,1:T(4,128)S(1)}, s32[384,3]{0,1:T(4,128)}, u32[]{:S(2)}) copy-start(s32[384,3]{0,1:T(4,128)} %param.23) | copy-start | bytes 13828
  162.5 9.4 %copy-start.9 = (bf16[1024]{0:T(1024)(128)(2,1)S(1)}, bf16[1024]{0:T(1024)(128)(2,1)}, u32[]{:S(2)}) copy-start(bf16[1024]{0:T(1024)(128)(2,1)} %param.18) | copy-start | bytes 6148
  162.5 10.0 %copy-start.10 = (bf16[1024]{0:T(1024)(128)(2,1)S(1)}, bf16[1024]{0:T(1024)(128)(2,1)}, u32[]{:S(2)}) copy-start(bf16[1024]{0:T(1024)(128)(2,1)} %param.19) | copy-start | bytes 6148
  233.1 4.0 %copy-start.7 = (bf16[768,1024]{1,0:T(8,128)(2,1)S(1)}, bf16[768,1024]{1,0:T(8,128)(2,1)}, u32[]{:S(2)}) copy-start(bf16[768,1024]{1,0:T(8,128)(2,1)} %get-tuple-element.126) | copy-start | bytes 4718596

commit v5 on v4

--- a/solution.py
+++ b/solution.py
@@ -690,14 +690,26 @@
     pool1,
     pool2,
     pool3,
+    pool4,
+    pool5,
+    pool6,
+    pool7,
     hold0,
     hold1,
     hold2,
     hold3,
+    hold4,
+    hold5,
+    hold6,
+    hold7,
     last0,
     last1,
     last2,
     last3,
+    last4,
+    last5,
+    last6,
+    last7,
     stage1,
     stage2,
     sums,
@@ -717,16 +729,16 @@
 ):
     me = lax.axis_index("ctx")
     tp = lax.axis_index("tp")
-    heads, blocks = ext.shape[0], kv_ref.shape[0]
-    rows, pair = ext.shape[2:]
-    size = pair // 2
+    units, blocks = ext.shape[0], kv_ref.shape[0]
+    rows, size = ext.shape[2:]
+    heads, pair = units // 2, 2 * size
     spot = (me // 8, lax.rem(me // 2, LINE))
     level = lax.rem(me, 2)
     twin = me + 1 - 2 * level
     mates = (tp + 1 - 2 * lax.rem(tp, 2), lax.rem(tp + 2, 4), 3 - tp)
-    pools = (pool0, pool1, pool2, pool3)
-    holds = (hold0, hold1, hold2, hold3)
-    lasts = (last0, last1, last2, last3)
+    pools = (pool0, pool1, pool2, pool3, pool4, pool5, pool6, pool7)
+    holds = (hold0, hold1, hold2, hold3, hold4, hold5, hold6, hold7)
+    lasts = (last0, last1, last2, last3, last4, last5, last6, last7)
     wcols = w1_ref.shape[1]
     near = SPAN * rows
 
@@ -825,16 +837,16 @@
         for r in range(4):
             for s in range(4):
                 cand[(g * 4 + r) * 4 + s] = row[r * 16 : r * 16 + 16, s * cut : (s + 1) * cut]
-    for c in range(heads):
-        for half in range(2):
-            lanes = slice(half * size, (half + 1) * size)
-            begin = half * heads * size + c * size
-            own = kv_ref[:, :, begin : begin + size]
-            pools[c][pl.ds(level * blocks, blocks), :, lanes] = own
-            ext[c, pl.ds(MAXR, blocks), :, lanes] = own
+    for c in range(units):
+        begin = (c % 2 * heads + c // 2) * size
+        own = kv_ref[:, :, begin : begin + size]
+        pools[c][pl.ds(level * blocks, blocks)] = own
+        ext[c, pl.ds(MAXR, blocks)] = own
     pl.semaphore_wait(barrier, count - 1 + 3)
 
     def scatter(c):
+        if c + 3 < units:
+            pair_copy(c + 3).start()
         pair_copy(c).wait()
         halo_copy(c).start()
         ext[c, pl.ds((blocks + MAXR) * (1 - level), MAXR)] = pools[c][
@@ -884,7 +896,8 @@
         )
 
     def nearby(c):
-        halo_copy(c).wait()
+        halo_copy(2 * c).wait()
+        halo_copy(2 * c + 1).wait()
         lanes = slice(c * size, (c + 1) * size)
         allowed = jnp.abs(place) <= list_ref[2 * G + c]
         g_k = gkv[:, :, c * size : (c + 1) * size].reshape(G * rows, size)
@@ -894,8 +907,9 @@
             block = me * blocks + b
             inside = (place + block >= 0) & (place + block < count * blocks)
             q = q_ref[b, :, lanes]
-            window = ext[c, pl.ds(b, SPAN)].reshape(near, pair)
-            s1 = jnp.where(inside & allowed, score(q, window[:, :size]), -jnp.inf)
+            window_k = ext[2 * c, pl.ds(b, SPAN)].reshape(near, size)
+            window_v = ext[2 * c + 1, pl.ds(b, SPAN)].reshape(near, size)
+            s1 = jnp.where(inside & allowed, score(q, window_k), -jnp.inf)
             s2 = score(q, g_k)
             peak = jnp.maximum(
                 jnp.max(s1, axis=1, keepdims=True), jnp.max(s2, axis=1, keepdims=True)
@@ -904,7 +918,7 @@
             p2 = jnp.exp(s2 - peak)
             total = jnp.sum(p1, axis=1, keepdims=True) + jnp.sum(p2, axis=1, keepdims=True)
             sums[c, b] = jnp.dot(
-                p1.astype(jnp.bfloat16), window[:, size:], preferred_element_type=jnp.float32
+                p1.astype(jnp.bfloat16), window_v, preferred_element_type=jnp.float32
             ) + jnp.dot(p2.astype(jnp.bfloat16), g_v, preferred_element_type=jnp.float32)
             stats[c, b] = jnp.where(left, peak, total)
             return carry
@@ -913,30 +927,34 @@
 
     def distant(c):
         for d in range(1, LINE):
-            bulk(c, 1, d).wait()
+            bulk(2 * c, 1, d).wait()
+            bulk(2 * c + 1, 1, d).wait()
         lanes = slice(c * size, (c + 1) * size)
         swap = [
             jnp.concatenate([far[c * 8 + g * 4 + r] for r in range(4)], axis=0) for g in range(G)
         ]
 
-        def attend(b, carry):
-            q = q_ref[b, :, lanes]
+        def collect(u, b):
             picked = []
             for r in range(R):
-                at = list_ref[base(c) + 2 * LINE * STRIDE + b * R + r]
+                at = list_ref[base(u) + 2 * LINE * STRIDE + b * R + r]
                 picked.append(
                     jnp.where(
                         at < held,
-                        pools[c][jnp.minimum(at, held - 1)],
+                        pools[u][jnp.minimum(at, held - 1)],
                         jnp.where(
                             at < ended,
-                            holds[c][jnp.clip(at - held, 0, LINE * FIRST - 1)],
-                            lasts[c][jnp.maximum(at - ended, 0)],
+                            holds[u][jnp.clip(at - held, 0, LINE * FIRST - 1)],
+                            lasts[u][jnp.maximum(at - ended, 0)],
                         ),
                     )
                 )
-            extra = jnp.concatenate(picked, axis=0)
-            s2 = score(q, extra[:, :size])
+            return jnp.concatenate(picked, axis=0)
+
+        def attend(b, carry):
+            q = q_ref[b, :, lanes]
+            extra_v = collect(2 * c + 1, b)
+            s2 = score(q, collect(2 * c, b))
             first_peak = stats[c, b, :, 0:1]
             peak = jnp.maximum(first_peak, jnp.max(s2, axis=1, keepdims=True))
             factor = jnp.exp(first_peak - peak)
@@ -945,7 +963,7 @@
                 p2, axis=1, keepdims=True
             )
             acc = sums[c, b] * factor + jnp.dot(
-                p2.astype(jnp.bfloat16), extra[:, size:], preferred_element_type=jnp.float32
+                p2.astype(jnp.bfloat16), extra_v, preferred_element_type=jnp.float32
             )
             which = list_ref[2 * G + heads + b]
             result = (acc / total).astype(out_ref.dtype)
@@ -977,14 +995,14 @@
         return att_copy(2, c, a2_ref, a3_ref, mates[0])
 
     each(lambda k: small(0, k, True, cand, got).start())
-    for c in range(heads):
+    for c in range(3):
         pair_copy(c).start()
     got[me] = cand[me]
     each(lambda k: small(0, k, True, cand, got).wait())
     full[me] = got[list_ref[me // (count // G)]]
     each(lambda k: small(1, k, False, full, full).start())
-    scatter(0)
-    scatter(1)
+    for c in range(3):
+        scatter(c)
 
     each(lambda k: small(1, k, False, full, full).wait())
     for g in range(G):
@@ -1015,13 +1033,15 @@
             part[h * 8 + r, 16:32, :] = both[cut]
     far_got[me] = part[me]
     each(lambda k: small(2, k, True, part, far_got).start())
-    scatter(2)
-    scatter(3)
+    for c in range(3, units):
+        scatter(c)
     for k in range(3):
         weight_copy(k).start()
     forward(0)
+    forward(1)
     nearby(0)
-    forward(1)
+    forward(2)
+    forward(3)
     nearby(1)
 
     each(lambda k: small(2, k, True, part, far_got).wait())
@@ -1044,8 +1064,8 @@
     )
     far[me] = (far_acc / far_total).astype(far.dtype)
     each(lambda k: small(3, k, False, far, far).start())
-    forward(2)
-    forward(3)
+    for c in range(heads, units):
+        forward(c)
 
     nearby(2)
     nearby(3)
@@ -1087,7 +1107,7 @@
         in_specs=[pl.BlockSpec(memory_space=SMEM), vmem, vmem, hbm],
         out_specs=(vmem,) + (hbm,) * 6,
         scratch_shapes=[
-            VMEM((heads, blocks + 2 * MAXR, rows, pair), kept),
+            VMEM((2 * heads, blocks + 2 * MAXR, rows, size), kept),
             VMEM((count, 16, cut), kept),
             VMEM((count, 16, cut), kept),
             VMEM((count, 16, cut), kept),
@@ -1097,26 +1117,26 @@
             VMEM((count, 32, size), jnp.float32),
             VMEM((count, 16, size), kept),
         ]
-        + [VMEM((2 * blocks, rows, pair), kept)] * heads
-        + [VMEM((LINE * FIRST, rows, pair), kept)] * heads
-        + [VMEM((LINE * SECOND, rows, pair), kept)] * heads
+        + [VMEM((2 * blocks, rows, size), kept)] * (2 * heads)
+        + [VMEM((LINE * FIRST, rows, size), kept)] * (2 * heads)
+        + [VMEM((LINE * SECOND, rows, size), kept)] * (2 * heads)
         + [
-            VMEM((heads, (LINE - 1) * FIRST, rows, pair), kept),
-            VMEM((heads, (LINE - 1) * SECOND, rows, pair), kept),
+            VMEM((2 * heads, (LINE - 1) * FIRST, rows, size), kept),
+            VMEM((2 * heads, (LINE - 1) * SECOND, rows, size), kept),
             VMEM((heads, blocks, rows, size), jnp.float32),
             VMEM((heads, blocks, rows, size), jnp.float32),
             dma((3, heads)),
             dma((3, heads)),
-            dma((heads,)),
-            dma((heads,)),
-            dma((heads,)),
-            dma((heads,)),
+            dma((2 * heads,)),
+            dma((2 * heads,)),
+            dma((2 * heads,)),
+            dma((2 * heads,)),
             dma((3,)),
             dma((3,)),
             dma((4, count)),
             dma((4, count)),
-            dma((2, heads, LINE - 1)),
-            dma((2, heads, LINE - 1)),
+            dma((2, 2 * heads, LINE - 1)),
+            dma((2, 2 * heads, LINE - 1)),
         ],
         compiler_params=pltpu.CompilerParams(
             collective_id=3, has_side_effects=True, vmem_limit_bytes=60 * 2**20

time: 240 us -> 229 us (0.954)
  Pallas kernels: 212 us -> 202 us
    pallas_call x1, Pallas kernels: 150 us -> 140 us  [front(): pl.pallas_call(functools.partial(front_kernel, count, scale), name='front...]
where the time goes in v5:
time: 229 us; the launch traced here: 228 us
  Pallas kernels  202 us (88%)
  local copies, waits for them, and re-layouts  24.2 us (11%)
    pallas_call x1, Pallas kernels, front(): pl.pallas_call(functools.partial(front_kernel, count, scale), name='front...  140 us
    pallas_call x1, Pallas kernels, project(): pl.pallas_call(functools.partial(project_kernel, ctx_count, tp_count, CHU...  60.5 us
    unnamed x21, local copies, waits for them, and re-layouts  14.3 us

profile of v5, /device:TPU:1, one launch (start us, length us, event | category | flops | bytes accessed | tf_op | source)
XLA Modules:
  0.0 228.1 jit_solution(12390275335759321902)
XLA Ops:
  0.6 0.8 copy.53
  1.5 0.1 reshape.127.req_ref
  1.6 0.1 copy.54
  1.7 0.0 copy-start.1
  1.7 0.9 copy-done.1
  2.6 0.0 copy-start.3
  2.6 0.7 copy-done.3
  3.3 0.0 copy-start.4
  3.3 0.7 copy-done.4
  4.0 0.0 copy-start.5
  4.0 0.7 copy-done.5
  4.6 2.0 plan.1
  6.6 0.2 slice_reduce_fusion
  6.8 0.0 copy-start.6
  6.8 0.0 copy-start.8
  6.8 3.9 %reshape.128 = bf16[12,64,1024]{2,1,0:T(8,128)(2,1)} reshape(bf16[768,2,512]{2,1,0:T(2,128)(2,1)} %param.15) | data formatting | bytes 3145728 | tf_op jit(solution)/shard_map/reshape | solution.py:1338
  10.7 0.5 slice.16
  11.8 0.0 copy-done.6
  11.8 0.0 copy-done.8
  11.8 140.1 %conditional.1 = (bf16[512,1024]{1,0:T(8,128)(2,1)S(1)}, bf16[512,1024]{1,0:T(8,128)(2,1)S(1)}, bf16[512,1024]{1,0:T(8,128)(2,1)}, bf16[768,512]{1,0:T(8,128)(2,...) conditional(s32[]{:T(128)} %bitcast.10, (bf16[512,4096]{1,0:T(8,128)(2,1)}, ...), branch_computations={%region_0.3_spmd, %region_3.4_spmd} | conditional | flops 195994 | bytes 32104924 | solution.py:1367
  12.0 139.9 %front.1 = (bf16[12,64,512]{2,1,0:T(8,128)(2,1)}, bf16[512,1024]{1,0:T(8,128)(2,1)S(1)}, bf16[512,1024]{1,0:T(8,128)(2,1)S(1)}, bf16[512,1024]{1,0:T(8,128)(2,1)...) custom-call(s32[360]{0:T(512)S(1)} %get-tuple-element.42.list_ref, ...), custom_call_target="tpu_custom_call" | custom-call | tf_op jit(solution)/shard_map/cond/branch_1_fun/front/pallas_call | solution.py:1103
  151.9 0.0 copy-start.9
  151.9 0.0 copy-start.10
  151.9 9.3 %copy.56 = bf16[512,8,2,512]{3,1,2,0:T(8,128)(2,1)} copy(bf16[512,8,2,512]{3,2,1,0:T(2,128)(2,1)} %bitcast.16) | data formatting | bytes 16777216
  161.3 0.0 copy-done.9
  161.3 0.6 reshape.130.gain_ref
  161.9 0.0 copy-done.10
  161.9 0.6 reshape.131.bias_ref
  162.5 60.5 %project.1 = (bf16[768,1024]{1,0:T(8,128)(2,1)}, bf16[768,1024]{1,0:T(8,128)(2,1)}) custom-call(bf16[768,512]{1,0:T(8,128)(2,1)} %get-tuple-element.64.att_ref, bf16[768,512]{1,0:T(8,128)(2,1)} %get-tuple-element.65.a1, bf16[768,512]{1,0:T(8,128)(2,1)} %get-tuple-element.66.a2, bf16[768,512]{1,0:T(8,128)(2,1)} %get-tuple-element.67.a3, ...), custom_call_target="tpu_custom_call" | custom-call | tf_op jit(solution)/shard_map/project/pallas_call | solution.py:631
  223.0 0.0 copy-start.7
  223.0 4.0 %reshape.133 = bf16[768,2,512]{2,1,0:T(2,128)(2,1)} reshape(bf16[768,1024]{1,0:T(8,128)(2,1)} %get-tuple-element.72) | data formatting | bytes 3145728 | tf_op jit(solution)/shard_map/reshape | solution.py:1382
  227.0 0.0 copy-done.7
  227.0 1.1 copy.72
  (1 shorter events, 0.0 us)
Async XLA Ops:
  1.7 0.9 copy-start.1
  2.6 0.7 copy-start.3
  3.3 0.7 copy-start.4
  4.0 0.7 copy-start.5
  6.8 5.1 %copy-start.6 = (bf16[768,512]{1,0:T(8,128)(2,1)S(1)}, bf16[768,512]{1,0:T(8,128)(2,1)}, u32[]{:S(2)}) copy-start(bf16[768,512]{1,0:T(8,128)(2,1)} %param.14) | copy-start | bytes 2359300
  6.8 5.1 %copy-start.8 = (s32[384,3]{0,1:T(4,128)S(1)}, s32[384,3]{0,1:T(4,128)}, u32[]{:S(2)}) copy-start(s32[384,3]{0,1:T(4,128)} %param.23) | copy-start | bytes 13828
  151.9 9.4 %copy-start.9 = (bf16[1024]{0:T(1024)(128)(2,1)S(1)}, bf16[1024]{0:T(1024)(128)(2,1)}, u32[]{:S(2)}) copy-start(bf16[1024]{0:T(1024)(128)(2,1)} %param.18) | copy-start | bytes 6148
  151.9 10.0 %copy-start.10 = (bf16[1024]{0:T(1024)(128)(2,1)S(1)}, bf16[1024]{0:T(1024)(128)(2,1)}, u32[]{:S(2)}) copy-start(bf16[1024]{0:T(1024)(128)(2,1)} %param.19) | copy-start | bytes 6148
  223.0 4.0 %copy-start.7 = (bf16[768,1024]{1,0:T(8,128)(2,1)S(1)}, bf16[768,1024]{1,0:T(8,128)(2,1)}, u32[]{:S(2)}) copy-start(bf16[768,1024]{1,0:T(8,128)(2,1)} %get-tuple-element.126) | copy-start | bytes 4718596

commit v6 on v5

--- a/solution.py
+++ b/solution.py
@@ -459,6 +459,7 @@
     encoded_ref,
     out_ref,
     w_all,
+    raw,
     cross,
     mixed,
     stats,
@@ -485,7 +486,7 @@
         pltpu.make_async_copy(w, w_all.at[k], w_sem.at[k]).start()
     for k, block in enumerate((tp, mate, over, cater)):
         pltpu.make_async_copy(
-            cross_ref.at[pl.ds(block * cols, cols)], cross.at[k], cross_sem.at[k]
+            cross_ref.at[pl.ds(block * cols, cols)], raw.at[k], cross_sem.at[k]
         ).start()
 
     barrier = pltpu.get_barrier_semaphore()
@@ -573,10 +574,10 @@
         def cast(c):
             enc_mate(c).wait_recv()
             enc_on(c).wait_recv()
-            acc = jnp.zeros((rows, out_ref.shape[1]), jnp.float32)
+            acc = jnp.zeros((rows, cross.shape[2]), jnp.float32)
             for k, g in enumerate((g0, g1, g2, g3)):
                 acc = acc + jnp.dot(g[cut(c), :], cross[k], preferred_element_type=jnp.float32)
-            out_ref[cut(c), :] = acc.astype(out_ref.dtype)
+            out_ref[cut(c)] = acc.astype(out_ref.dtype).reshape(rows, 2, acc.shape[1] // 2)
 
         at(ROLL, relay_enc)
         at(ROLL + 1, relay_on)
@@ -593,12 +594,22 @@
         at(1, send_rows)
         at(0, send_stats)
 
-        @pl.when(t == ROLL + 2)
-        def _():
-            for k in range(4):
-                pltpu.make_async_copy(
-                    cross_ref.at[pl.ds(0, cols)], cross.at[k], cross_sem.at[k]
-                ).wait()
+        for i in range(3):
+            piece = t * 3 + i
+
+            @pl.when(piece < 4 * PIECES)
+            def _():
+                k = piece // PIECES
+
+                @pl.when(lax.rem(piece, PIECES) == 0)
+                def _():
+                    pltpu.make_async_copy(
+                        cross_ref.at[pl.ds(0, cols)], raw.at[k], cross_sem.at[k]
+                    ).wait()
+
+                span = cols // PIECES
+                some = pl.ds(pl.multiple_of(lax.rem(piece, PIECES) * span, span), span)
+                cross[k, some] = raw[k, some].reshape(span, cross.shape[2])
 
         at(ROLL + 2, cast)
         return carry
@@ -618,13 +629,15 @@
 
 
 ROLL = 3
+PIECES = 4
 CHUNKS = 6
 
 
 def project(att, residual, gain, bias, out_weight, weights, cross_weight, ctx_count, tp_count):
     rows, depth = att[0].shape
     cols = residual.shape[1]
-    wide = cross_weight.shape[1]
+    half = cross_weight.shape[2]
+    wide = 2 * half
     vmem = pl.BlockSpec(memory_space=VMEM)
     hbm = pl.BlockSpec(memory_space=pl.ANY)
     kept = jnp.bfloat16
@@ -633,12 +646,13 @@
         name="project",
         out_shape=(
             jax.ShapeDtypeStruct((rows, cols), kept),
-            jax.ShapeDtypeStruct((rows, wide), kept),
+            jax.ShapeDtypeStruct((rows, 2, half), kept),
         ),
         in_specs=[vmem] * 7 + [hbm] * 5,
         out_specs=(vmem, vmem),
         scratch_shapes=[
             VMEM((4, depth, cols), kept),
+            VMEM((4, cols, 2, half), kept),
             VMEM((4, cols, wide), kept),
             VMEM((rows, cols), jnp.float32),
             VMEM((CHUNKS, 4, 16, rows // CHUNKS), jnp.float32),
@@ -667,7 +681,7 @@
     count,
     scale,
     list_ref,
-    kv_ref,
+    raw_ref,
     q_ref,
     weight_ref,
     out_ref,
@@ -677,6 +691,7 @@
     a1_ref,
     a2_ref,
     a3_ref,
+    kv_ref,
     ext,
     cand,
     got,
@@ -830,6 +845,8 @@
 
         lax.fori_loop(1, count, body, 0)
 
+    for b in range(blocks):
+        kv_ref[b] = raw_ref[b * rows : (b + 1) * rows].reshape(rows, heads * pair)
     for g in range(G):
         local = list_ref[G + g]
         row = jnp.concatenate([kv_ref[local], q_ref[local]], axis=1)
@@ -1012,6 +1029,7 @@
             gq[g, r * 16 : r * 16 + 16, :] = row[:, heads * pair :]
 
     half_lane = lax.broadcasted_iota(jnp.int32, (G * rows, size), 1) < size // 2
+    last_lane = lax.broadcasted_iota(jnp.int32, (G * rows, size), 1) >= 3 * size // 4
     for h in range(heads):
         gq_h = gq[:, :, h * size : (h + 1) * size].reshape(G * rows, size)
         k_h = kv_ref[:, :, h * size : (h + 1) * size].reshape(blocks * rows, size)
@@ -1022,11 +1040,14 @@
             lax.dot_general(gq_h, k_h, (((1,), (1,)), ((), ())), preferred_element_type=jnp.float32)
             * scale
         )
-        peak = jnp.max(s, axis=1, keepdims=True)
+        peak = jnp.max(s, axis=1, keepdims=True).astype(jnp.bfloat16).astype(jnp.float32)
         p = jnp.exp(s - peak)
         total = jnp.sum(p, axis=1, keepdims=True)
         acc = jnp.dot(p.astype(jnp.bfloat16), v_h, preferred_element_type=jnp.float32)
-        both = jnp.where(half_lane, peak, total)
+        acc = acc.astype(part.dtype)
+        high = total.astype(part.dtype).astype(jnp.float32)
+        both = jnp.where(half_lane, peak, jnp.where(last_lane, total - high, high))
+        both = both.astype(part.dtype)
         for r in range(8):
             cut = slice(r * 16, r * 16 + 16)
             part[h * 8 + r, 0:16, :] = acc[cut]
@@ -1046,21 +1067,26 @@
 
     each(lambda k: small(2, k, True, part, far_got).wait())
 
-    def top(i, so_far):
-        return jnp.maximum(so_far, far_got[i, 16:32, 0:1])
-
-    far_peak = lax.fori_loop(1, count, top, far_got[0, 16:32, 0:1], unroll=4)
+    def terms(i):
+        both = far_got[i, 16:32, :].astype(jnp.float32)
+        total = both[:, size // 2 : size // 2 + 1] + both[:, size - 1 : size]
+        return far_got[i, 0:16, :].astype(jnp.float32), both[:, 0:1], total
+
+    far_peak = lax.fori_loop(
+        1, count, lambda i, m: jnp.maximum(m, terms(i)[1]), terms(0)[1], unroll=4
+    )
 
     def add(i, so_far):
-        acc, total = so_far
-        factor = jnp.exp(far_got[i, 16:32, 0:1] - far_peak)
-        return (
-            acc + far_got[i, 0:16, :] * factor,
-            total + far_got[i, 16:32, size // 2 : size // 2 + 1] * factor,
-        )
+        acc, peak, total = terms(i)
+        factor = jnp.exp(peak - far_peak)
+        return so_far[0] + acc * factor, so_far[1] + total * factor
 
     far_acc, far_total = lax.fori_loop(
-        0, count, add, (jnp.zeros((16, size), jnp.float32), jnp.zeros((16, 1), jnp.float32)), unroll=4
+        0,
+        count,
+        add,
+        (jnp.zeros((16, size), jnp.float32), jnp.zeros((16, 1), jnp.float32)),
+        unroll=4,
     )
     far[me] = (far_acc / far_total).astype(far.dtype)
     each(lambda k: small(3, k, False, far, far).start())
@@ -1089,9 +1115,9 @@
 
 
 def front(lists, kv, q, heads, weight, scale, count, tp_count):
-    blocks, rows, wide = kv.shape
-    pair = wide // heads
-    size = pair // 2
+    blocks, rows, half = q.shape
+    size = half // heads
+    pair = 2 * size
     kept = kv.dtype
     vmem = pl.BlockSpec(memory_space=VMEM)
     hbm = pl.BlockSpec(memory_space=pl.ANY)
@@ -1107,14 +1133,15 @@
         in_specs=[pl.BlockSpec(memory_space=SMEM), vmem, vmem, hbm],
         out_specs=(vmem,) + (hbm,) * 6,
         scratch_shapes=[
+            VMEM((blocks, rows, 2 * half), kept),
             VMEM((2 * heads, blocks + 2 * MAXR, rows, size), kept),
             VMEM((count, 16, cut), kept),
             VMEM((count, 16, cut), kept),
             VMEM((count, 16, cut), kept),
             VMEM((G, rows, heads * pair), kept),
             VMEM((G, rows, heads * size), kept),
-            VMEM((count, 32, size), jnp.float32),
-            VMEM((count, 32, size), jnp.float32),
+            VMEM((count, 32, size), kept),
+            VMEM((count, 32, size), kept),
             VMEM((count, 16, size), kept),
         ]
         + [VMEM((2 * blocks, rows, size), kept)] * (2 * heads)
@@ -1335,14 +1362,13 @@
     block_count = tok_rows // BLOCK
     scale = 1.0 / math.sqrt(head_size)
     q = queries.reshape(block_count, BLOCK, head_cols)
-    kv = keyvals.reshape(block_count, BLOCK, 2 * head_cols)
     lists = plan(random_blocks, global_blocks, window_reach, block_count, ctx_count)
     fits = lists[20] > 0
 
-    def staged(kv, q, out_weight):
-        return tuple(front(lists, kv, q, head_count, out_weight, scale, ctx_count, tp_count))
-
-    def plain(kv, q, out_weight):
+    def staged(keyvals, q, out_weight):
+        return tuple(front(lists, keyvals, q, head_count, out_weight, scale, ctx_count, tp_count))
+
+    def plain(keyvals, q, out_weight):
         req_count = block_count * R
         slots = 1 + (req_count + ctx_count - 2) // ctx_count
         requests = random_blocks.reshape(ctx_count, req_count)
@@ -1361,10 +1387,15 @@
         place = lists[: 2 * G]
         info = lists[2 * G : 2 * G + head_count + block_count]
         return direct(
-            place, info, source_ids, my_index, kv, q, out_weight, scale, ctx_count, slots
-        )
-
-    attended, *rest = lax.cond(fits, staged, plain, kv, q, out_weight)
+            place,
+            info,
+            source_ids,
+            my_index,
+            keyvals.reshape(block_count, BLOCK, 2 * head_cols),
+            q, out_weight, scale, ctx_count, slots
+        )
+
+    attended, *rest = lax.cond(fits, staged, plain, keyvals, q, out_weight)
     weights = rest[: tp_count - 1]
     gathered = [x.reshape(tok_rows, head_cols) for x in [attended] + rest[tp_count - 1 :]]
     cols = residual.shape[1]
@@ -1375,11 +1406,11 @@
         norm_bias.reshape(1, cols),
         out_weight,
         weights,
-        cross_weight.reshape(D, 2 * head_cols),
+        cross_weight,
         ctx_count,
         tp_count,
     )
-    return (encoded, cross_kv.reshape(tok_rows, 2, head_cols))
+    return (encoded, cross_kv)
 
 
 def solution(mesh):

time: 229 us -> 211 us (0.921)
  local copies, waits for them, and re-layouts: 24.2 us -> 9.78 us
  Pallas kernels: 202 us -> 199 us
    reshape x2 -> x0, local copies, waits for them, and re-layouts: 7.83 us -> none  [the longest x1 3.96 us: shards(): return (encoded, cross_kv.reshape(tok_rows, 2, head_cols))]
    unnamed x21 -> x17, local copies, waits for them, and re-layouts: 14.3 us -> 7.71 us
    pallas_call x1, Pallas kernels: 140 us -> 137 us  [front(): pl.pallas_call(functools.partial(front_kernel, count, scale), name='front...]
where the time goes in v6:
time: 211 us; the launch traced here: 210 us
  Pallas kernels  199 us (94%)
  local copies, waits for them, and re-layouts  9.78 us (5%)
    pallas_call x1, Pallas kernels, front(): pl.pallas_call(functools.partial(front_kernel, count, scale), name='front...  137 us
    pallas_call x1, Pallas kernels, project(): pl.pallas_call(functools.partial(project_kernel, ctx_count, tp_count, CHU...  59.7 us
    unnamed x17, local copies, waits for them, and re-layouts  7.71 us

profile of v6, /device:TPU:1, one launch (start us, length us, event | category | flops | bytes accessed | tf_op | source)
XLA Modules:
  0.0 210.2 jit_solution(17857568835942422087)
XLA Ops:
  0.6 0.8 copy.53
  1.5 0.1 reshape.121.req_ref
  1.6 0.1 copy.54
  1.7 0.0 copy-start.4
  1.7 0.9 copy-done.4
  2.6 0.0 copy-start.6
  2.6 0.7 copy-done.6
  3.3 0.0 copy-start.7
  3.3 0.7 copy-done.7
  4.0 0.0 copy-start.8
  4.0 0.7 copy-done.8
  4.6 2.0 plan.1
  6.6 0.2 slice_reduce_fusion
  6.8 0.5 slice.16
  7.9 0.0 copy-start.11
  8.0 0.0 copy-start.12
  8.0 137.4 %conditional.1 = (bf16[512,1024]{1,0:T(8,128)(2,1)S(1)}, bf16[512,1024]{1,0:T(8,128)(2,1)S(1)}, bf16[512,1024]{1,0:T(8,128)(2,1)S(1)}, bf16[768,512]{1,0:T(8,128...) conditional(s32[]{:T(128)} %bitcast.10, ...), branch_computations={%region_0.3_spmd, %region_3.4_spmd} | conditional | flops 195994 | bytes 63562316 | solution.py:1398
  8.2 137.2 %front.1 = (bf16[12,64,512]{2,1,0:T(8,128)(2,1)}, bf16[512,1024]{1,0:T(8,128)(2,1)S(1)}, bf16[512,1024]{1,0:T(8,128)(2,1)S(1)}, bf16[512,1024]{1,0:T(8,128)(2,1)...) custom-call(s32[360]{0:T(512)S(1)} %get-tuple-element.42.list_ref, ...), custom_call_target="tpu_custom_call" | custom-call | tf_op jit(solution)/shard_map/cond/branch_1_fun/front/pallas_call | solution.py:1129
  145.4 0.0 copy-done.11
  145.4 0.6 reshape.123.gain_ref
  146.0 0.0 copy-done.12
  146.0 0.6 reshape.124.bias_ref
  146.6 59.7 %project.1 = (bf16[768,1024]{1,0:T(8,128)(2,1)}, bf16[768,2,512]{2,1,0:T(2,128)(2,1)}) custom-call(bf16[768,512]{1,0:T(8,128)(2,1)} %get-tuple-element.62.att_ref, bf16[768,512]{1,0:T(8,128)(2,1)} %get-tuple-element.63.a1, bf16[768,512]{1,0:T(8,128)(2,1)} %get-tuple-element.64.a2, bf16[768,512]{1,0:T(8,128)(2,1)} %get-tuple-element.65.a3, ...), custom_call_target="tpu_custom_call" | custom-call | tf_op jit(solution)/shard_map/project/pallas_call | solution.py:644
  206.3 0.0 copy-start.10
  206.3 2.8 %copy.72 = bf16[768,1024]{1,0:T(8,128)(2,1)} copy(bf16[768,1024]{1,0:T(8,128)(2,1)} %get-tuple-element.122) | data formatting | bytes 3145728
  209.1 0.0 copy-done.10
  209.1 1.1 copy.73
  (1 shorter events, 0.0 us)
Async XLA Ops:
  1.7 0.9 copy-start.4
  2.6 0.7 copy-start.6
  3.3 0.7 copy-start.7
  4.0 0.7 copy-start.8
  7.9 137.5 %copy-start.11 = (bf16[1024]{0:T(1024)(128)(2,1)S(1)}, bf16[1024]{0:T(1024)(128)(2,1)}, u32[]{:S(2)}) copy-start(bf16[1024]{0:T(1024)(128)(2,1)} %param.18) | copy-start | bytes 6148
  8.0 138.1 %copy-start.12 = (bf16[1024]{0:T(1024)(128)(2,1)S(1)}, bf16[1024]{0:T(1024)(128)(2,1)}, u32[]{:S(2)}) copy-start(bf16[1024]{0:T(1024)(128)(2,1)} %param.19) | copy-start | bytes 6148
  206.3 2.8 %copy-start.10 = (bf16[768,2,512]{2,1,0:T(2,128)(2,1)S(1)}, bf16[768,2,512]{2,1,0:T(2,128)(2,1)}, u32[]{:S(2)}) copy-start(bf16[768,2,512]{2,1,0:T(2,128)(2,1)} %get-tuple-element.123) | copy-start | bytes 4718596

commit v7 on v6

--- a/solution.py
+++ b/solution.py
@@ -3,7 +3,6 @@
 
 import jax
 import jax.numpy as jnp
-import numpy as np
 from jax import lax
 from jax.experimental import pallas as pl
 from jax.experimental.pallas import tpu as pltpu
@@ -449,8 +448,7 @@
     a2,
     a3,
     residual_ref,
-    gain_ref,
-    bias_ref,
+    scale_ref,
     w0,
     w1,
     w2,
@@ -554,7 +552,7 @@
             variance = square / width - mean * mean
             scaled = (mixed[cut(c), :] - mean) * lax.rsqrt(variance + norm_eps)
             encoded_ref[cut(c), :] = (
-                scaled * gain_ref[...].astype(jnp.float32) + bias_ref[...].astype(jnp.float32)
+                scaled * scale_ref[0:1].astype(jnp.float32) + scale_ref[1:2].astype(jnp.float32)
             ).astype(encoded_ref.dtype)
 
         def mix(c):
@@ -633,7 +631,7 @@
 CHUNKS = 6
 
 
-def project(att, residual, gain, bias, out_weight, weights, cross_weight, ctx_count, tp_count):
+def project(att, residual, scales, out_weight, weights, cross_weight, ctx_count, tp_count):
     rows, depth = att[0].shape
     cols = residual.shape[1]
     half = cross_weight.shape[2]
@@ -648,7 +646,7 @@
             jax.ShapeDtypeStruct((rows, cols), kept),
             jax.ShapeDtypeStruct((rows, 2, half), kept),
         ),
-        in_specs=[vmem] * 7 + [hbm] * 5,
+        in_specs=[vmem] * 6 + [hbm] * 5,
         out_specs=(vmem, vmem),
         scratch_shapes=[
             VMEM((4, depth, cols), kept),
@@ -668,7 +666,7 @@
         compiler_params=pltpu.CompilerParams(
             collective_id=2, has_side_effects=True, vmem_limit_bytes=60 * 2**20
         ),
-    )(*att, residual, gain, bias, out_weight, *weights, cross_weight)
+    )(*att, residual, scales, out_weight, *weights, cross_weight)
 
 
 FIRST = 14
@@ -1061,10 +1059,6 @@
     forward(0)
     forward(1)
     nearby(0)
-    forward(2)
-    forward(3)
-    nearby(1)
-
     each(lambda k: small(2, k, True, part, far_got).wait())
 
     def terms(i):
@@ -1090,6 +1084,10 @@
     )
     far[me] = (far_acc / far_total).astype(far.dtype)
     each(lambda k: small(3, k, False, far, far).start())
+    forward(2)
+    forward(3)
+    nearby(1)
+
     for c in range(heads, units):
         forward(c)
 
@@ -1176,7 +1174,7 @@
 ROUTE = 2 * LINE * STRIDE + 40
 
 
-def plan_kernel(count, blocks, row_ref, col_ref, req_ref, reqt_ref, reach_ref, gb_ref, out_ref):
+def plan_kernel(count, blocks, req_ref, reach_ref, gb_ref, out_ref):
     me = lax.axis_index("ctx")
     x, z, level = me // 8, lax.rem(me // 2, LINE), lax.rem(me, 2)
     many = 2 * blocks
@@ -1197,11 +1195,16 @@
     for e in range(blocks * R):
         asked = jnp.where(req_ref[:, e : e + 1] == ids, 1.0, asked)
 
-    place = {"x": row_ref[0:1, :], "z": row_ref[1:2, :]}
-    inner = row_ref[2:3, :].astype(jnp.float32)
-    group = row_ref[3:4, :]
-    place_col = {"x": col_ref[:, 0:1], "z": col_ref[:, 1:2]}
-    group_col = col_ref[:, 3:4]
+    def groups(shape, dim):
+        index = iota(shape, dim)
+        group = jnp.floor((index.astype(jnp.float32) + 0.5) / many).astype(jnp.int32)
+        return index, group
+
+    index, group = groups((1, total), 1)
+    place = {"x": group >> 2, "z": group & 3}
+    inner = (index - group * many).astype(jnp.float32)
+    group_col = groups((total, 1), 0)[1]
+    place_col = {"x": group_col >> 2, "z": group_col & 3}
     before = iota((total, total), 0) < iota((total, total), 1)
 
     r8, s8 = iota((8, count), 0), iota((8, count), 1)
@@ -1246,8 +1249,12 @@
     spots = {"x": x, "z": z}
     mine = (place["x"] == x) & (place["z"] == z)
     turn = iota((8, total), 0)
+    listed = blocks * R
+    own_row = jnp.sum(
+        jnp.where(iota((count, listed), 0) == me, req_ref[...], 0), axis=0, keepdims=True
+    )
     asked_col = jnp.sum(
-        jnp.where(iota(reqt_ref.shape, 1) == me, reqt_ref[...], 0), axis=1, keepdims=True
+        jnp.where(iota((40, listed), 0) == iota((40, listed), 1), own_row, 0), axis=1, keepdims=True
     )
 
     def store(offset, column):
@@ -1291,31 +1298,23 @@
             found,
             many + LINE * FIRST + line_second * SECOND + jnp.minimum(rank, SECOND - 1),
         )
-        hit = asked_col == iota((reqt_ref.shape[0], total), 1)
+        hit = asked_col == iota((40, total), 1)
         column = jnp.sum(jnp.where(hit, final, 0.0), axis=1, keepdims=True)
         store(start + 2 * LINE * STRIDE, column)
 
 
 def plan(random_blocks, global_blocks, window_reach, blocks, count):
     requests = random_blocks.reshape(count, blocks * R)
-    total = count * blocks
-    ids = np.arange(total)
-    table = np.zeros((8, total), np.int32)
-    table[0] = ids // (LINE * 2 * blocks)
-    table[1] = ids // (2 * blocks) % LINE
-    table[2] = ids % (2 * blocks)
-    table[3] = ids // (2 * blocks)
-    turned = jnp.pad(requests.T, ((0, 40 - blocks * R), (0, 0)), constant_values=-1)
     vmem = pl.BlockSpec(memory_space=VMEM)
     smem = pl.BlockSpec(memory_space=SMEM)
     out = pl.pallas_call(
         functools.partial(plan_kernel, count, blocks),
         name="plan",
         out_shape=jax.ShapeDtypeStruct((HEADER + 2 * ROUTE, 128), jnp.int32),
-        in_specs=[vmem] * 4 + [smem] * 2,
+        in_specs=[vmem] + [smem] * 2,
         out_specs=vmem,
         compiler_params=pltpu.CompilerParams(vmem_limit_bytes=48 * 2**20),
-    )(table, np.ascontiguousarray(table.T), requests, turned, window_reach, global_blocks)
+    )(requests, window_reach, global_blocks)
     return out[:, 0]
 
 
@@ -1402,8 +1401,7 @@
     encoded, cross_kv = project(
         gathered,
         residual,
-        norm_gain.reshape(1, cols),
-        norm_bias.reshape(1, cols),
+        jnp.stack([norm_gain, norm_bias]),
         out_weight,
         weights,
         cross_weight,

time: 211 us -> 204 us (0.967)
  Pallas kernels: 199 us -> 194 us
  local copies, waits for them, and re-layouts: 9.78 us -> 6.87 us
    pallas_call x1, Pallas kernels: 137 us -> 133 us  [front(): pl.pallas_call(functools.partial(front_kernel, count, scale), name='front...]
    unnamed x17 -> x13, local copies, waits for them, and re-layouts: 7.71 us -> 6.08 us
where the time goes in v7:
time: 204 us; the launch traced here: 203 us
  Pallas kernels  194 us (95%)
  local copies, waits for them, and re-layouts  6.87 us (3%)
    pallas_call x1, Pallas kernels, front(): pl.pallas_call(functools.partial(front_kernel, count, scale), name='front...  133 us
    pallas_call x1, Pallas kernels, project(): pl.pallas_call(functools.partial(project_kernel, ctx_count, tp_count, CHU...  59 us
    unnamed x13, local copies, waits for them, and re-layouts  6.08 us

profile of v7, /device:TPU:1, one launch (start us, length us, event | category | flops | bytes accessed | tf_op | source)
XLA Modules:
  0.0 203.3 jit_solution(1735928222113888166)
XLA Ops:
  0.6 0.8 copy.48
  1.5 0.1 reshape.115.req_ref
  1.6 0.0 copy-start.5
  1.6 0.6 copy-done.5
  2.2 0.0 copy-start.6
  2.2 0.7 copy-done.6
  2.9 2.0 plan.1
  4.9 0.2 slice_reduce_fusion
  5.0 0.5 slice.16
  6.2 0.0 copy-start.9
  6.2 0.0 copy-start.10
  6.2 133.4 %conditional.1 = (bf16[512,1024]{1,0:T(8,128)(2,1)S(1)}, bf16[512,1024]{1,0:T(8,128)(2,1)S(1)}, bf16[512,1024]{1,0:T(8,128)(2,1)S(1)}, bf16[768,512]{1,0:T(8,128...) conditional(s32[]{:T(128)} %bitcast.9, (bf16[512,4096]{1,0:T(8,128)(2,1)}, ...), branch_computations={%region_0.3_spmd, %region_3.4_spmd} | conditional | flops 195994 | bytes 63562316 | solution.py:1397
  6.4 133.3 %front.1 = (bf16[12,64,512]{2,1,0:T(8,128)(2,1)}, bf16[512,1024]{1,0:T(8,128)(2,1)S(1)}, bf16[512,1024]{1,0:T(8,128)(2,1)S(1)}, bf16[512,1024]{1,0:T(8,128)(2,1)...) custom-call(s32[360]{0:T(512)S(1)} %get-tuple-element.42.list_ref, ...), custom_call_target="tpu_custom_call" | custom-call | tf_op jit(solution)/shard_map/cond/branch_1_fun/front/pallas_call | solution.py:1127
  139.7 0.0 copy-done.9
  139.7 0.0 copy-done.10
  139.7 0.6 pad_maximum_fusion.scale_ref
  140.3 59.0 %project.1 = (bf16[768,1024]{1,0:T(8,128)(2,1)}, bf16[768,2,512]{2,1,0:T(2,128)(2,1)}) custom-call(bf16[768,512]{1,0:T(8,128)(2,1)} %get-tuple-element.62.att_ref, bf16[768,512]{1,0:T(8,128)(2,1)} %get-tuple-element.63.a1, bf16[768,512]{1,0:T(8,128)(2,1)} %get-tuple-element.64.a2, bf16[768,512]{1,0:T(8,128)(2,1)} %get-tuple-element.65.a3, ...), custom_call_target="tpu_custom_call" | custom-call | tf_op jit(solution)/shard_map/project/pallas_call | solution.py:642
  199.3 0.0 copy-start.8
  199.4 2.8 %copy.66 = bf16[768,1024]{1,0:T(8,128)(2,1)} copy(bf16[768,1024]{1,0:T(8,128)(2,1)} %get-tuple-element.122) | data formatting | bytes 3145728
  202.1 0.0 copy-done.8
  202.2 1.1 copy.67
  (2 shorter events, 0.0 us)
Async XLA Ops:
  1.6 0.7 copy-start.5
  2.2 0.7 copy-start.6
  6.2 133.5 %copy-start.9 = (bf16[1024]{0:T(1024)(128)(2,1)S(1)}, bf16[1024]{0:T(1024)(128)(2,1)}, u32[]{:S(2)}) copy-start(bf16[1024]{0:T(1024)(128)(2,1)} %param.17) | copy-start | bytes 6148
  6.2 133.5 %copy-start.10 = (bf16[1024]{0:T(1024)(128)(2,1)S(1)}, bf16[1024]{0:T(1024)(128)(2,1)}, u32[]{:S(2)}) copy-start(bf16[1024]{0:T(1024)(128)(2,1)} %param.16) | copy-start | bytes 6148
  199.3 2.8 %copy-start.8 = (bf16[768,2,512]{2,1,0:T(2,128)(2,1)S(1)}, bf16[768,2,512]{2,1,0:T(2,128)(2,1)}, u32[]{:S(2)}) copy-start(bf16[768,2,512]{2,1,0:T(2,128)(2,1)} %get-tuple-element.123) | copy-start | bytes 4718596
